TPU v7x, 32 devices: a whole 2x2x4 slice. The times are simulated.
32 devices in a mesh: dp: 4 (over y, x), fsdp: 8 (over z, core).
Axes of the slice: x: 2, y: 2, z: 4, core: 2. Of those that a mesh axis runs over, the one named last changes fastest.
Arguments:
- tokens: bfloat16 [32768, 1024], P(('dp', 'fsdp')), may hold values from -6 to 6
- segment_ids: int32 [32, 1024], P(('dp', 'fsdp')), may hold values from 0 to 19, never falling along the last dimension, each value on 1 to 512 neighbouring positions
- expert_ids: int32 [32768, 1], P(('dp', 'fsdp')), may hold values from 0 to 1; in each aligned block of 1024 rows (0 to 1023, 1024 to 2047, ...) at most 640 rows name the same one
- ln1_gain: bfloat16 [1024], P(('dp', 'fsdp')), may hold values from 0.5 to 1.5
- ln1_bias: bfloat16 [1024], P(('dp', 'fsdp')), may hold values from -0.59765625 to 0.59765625
- qkv_weight: bfloat16 [1024, 3072], P(('dp', 'fsdp')), may hold values from -0.1875 to 0.1875
- query_bias: bfloat16 [1024], P(('dp', 'fsdp')), may hold values from -0.59765625 to 0.59765625
- value_bias: bfloat16 [1024], P(('dp', 'fsdp')), may hold values from -0.59765625 to 0.59765625
- out_weight: bfloat16 [1024, 1024], P(('dp', 'fsdp')), may hold values from -0.375 to 0.375
- out_bias: bfloat16 [1024], P(('dp', 'fsdp')), may hold values from -0.59765625 to 0.59765625
- ln2_gain: bfloat16 [1024], P(('dp', 'fsdp')), may hold values from 0.5 to 1.5
- ln2_bias: bfloat16 [1024], P(('dp', 'fsdp')), may hold values from -0.59765625 to 0.59765625
- up_weight: bfloat16 [1024, 2, 4096], P(('dp', 'fsdp')), may hold values from -0.1875 to 0.1875
- up_bias: bfloat16 [2, 4096], P(None, ('dp', 'fsdp')), may hold values from -0.59765625 to 0.59765625
- down_weight: bfloat16 [4096, 2, 1024], P(('dp', 'fsdp')), may hold values from -0.125 to 0.125
- down_bias: bfloat16 [2, 1024], P(None, ('dp', 'fsdp')), may hold values from -0.59765625 to 0.59765625
- cotangent: bfloat16 [32768, 1024], P(('dp', 'fsdp')), may hold values from -6 to 6
Outputs:
- block_out: bfloat16 [32768, 1024], P(('dp', 'fsdp'))
- input_grad: float32 [32768, 1024], P(('dp', 'fsdp'))
- ln1_gain_grad: float32 [1024], P(('dp', 'fsdp'))
- ln1_bias_grad: float32 [1024], P(('dp', 'fsdp'))
- qkv_weight_grad: float32 [1024, 3072], P(('dp', 'fsdp'))
- query_bias_grad: float32 [1024], P(('dp', 'fsdp'))
- value_bias_grad: float32 [1024], P(('dp', 'fsdp'))
- out_weight_grad: float32 [1024, 1024], P(('dp', 'fsdp'))
- out_bias_grad: float32 [1024], P(('dp', 'fsdp'))
- ln2_gain_grad: float32 [1024], P(('dp', 'fsdp'))
- ln2_bias_grad: float32 [1024], P(('dp', 'fsdp'))
- up_weight_grad: float32 [1024, 2, 4096], P(('dp', 'fsdp'))
- up_bias_grad: float32 [2, 4096], P(None, ('dp', 'fsdp'))
- down_weight_grad: float32 [4096, 2, 1024], P(('dp', 'fsdp'))
- down_bias_grad: float32 [2, 1024], P(None, ('dp', 'fsdp'))
Inputs may be any that keep to these rules, and one draw needn't show every extreme that they name: `segment_ids`: each device's 1024 tokens are one packed sequence; its segment numbers never fall. `expert_ids`: at most 640 of the tokens of one device name one expert, and some device's tokens name one expert exactly that often.
All inputs are finite; a program needn't handle non-finite values.
Results may differ from a plain program's by a relative error of at most 0.012.
Values may be sent and summed in bfloat16 or wider, within the bound.
No kernel may reach another device: no remote copies, remote signals or barrier semaphores. Data moves between devices by JAX's collectives and lax.ppermute only.
A program may use at most 512 MiB of HBM per device.

v0:
```python
import jax
import jax.numpy as jnp
from jax import lax
from jax.sharding import PartitionSpec as P

HEADS = 16
HEAD_DIM = 64
EXPERTS = 2
CAPACITY = 640


epsilon = 1e-05


def layer_norm(values, gain, shift):
    centre = values - jnp.mean(values, -1, keepdims=True)
    spread = jnp.mean(centre * centre, -1, keepdims=True)
    return centre * lax.rsqrt(spread + epsilon) * gain + shift


def shards(
    tokens,
    segment_ids,
    expert_ids,
    ln1_gain,
    ln1_bias,
    qkv_weight,
    query_bias,
    value_bias,
    out_weight,
    out_bias,
    ln2_gain,
    ln2_bias,
    up_weight,
    up_bias,
    down_weight,
    down_bias,
    cotangent,
):
    float_type = jnp.float32
    half_type = jnp.bfloat16
    attention_full = (
        lax.all_gather(qkv_weight, ("dp", "fsdp"), axis=0, tiled=True),
        lax.all_gather(out_weight, ("dp", "fsdp"), axis=0, tiled=True),
        lax.all_gather(ln1_gain, ("dp", "fsdp"), axis=0, tiled=True),
        lax.all_gather(ln1_bias, ("dp", "fsdp"), axis=0, tiled=True),
        lax.all_gather(query_bias, ("dp", "fsdp"), axis=0, tiled=True),
        lax.all_gather(value_bias, ("dp", "fsdp"), axis=0, tiled=True),
        lax.all_gather(out_bias, ("dp", "fsdp"), axis=0, tiled=True),
    )
    w_qkv, w_out, gain_one, shift_one, bias_query, bias_value, bias_out = attention_full
    row_count, width = tokens.shape
    scale = HEAD_DIM ** (-0.5)
    block_rows = min(512, row_count)
    block_starts = list(range(0, row_count, block_rows))
    inputs = tokens.astype(float_type)
    gain_first = gain_one.astype(float_type)
    shift_first = shift_one.astype(float_type)
    normed_one = layer_norm(inputs, gain_first, shift_first)
    normed_low = normed_one.astype(half_type)
    qkv_bias = jnp.concatenate([bias_query, jnp.zeros_like(bias_query), bias_value]).astype(
        float_type
    )
    qkv_low = (jnp.dot(normed_low, w_qkv, preferred_element_type=float_type) + qkv_bias).astype(
        half_type
    )
    queries = qkv_low[:, :width].reshape(row_count, HEADS, HEAD_DIM)
    keys_low = qkv_low[:, width : 2 * width].reshape(row_count, HEADS, HEAD_DIM)
    values_low = qkv_low[:, 2 * width :].reshape(row_count, HEADS, HEAD_DIM)
    positions = lax.iota(jnp.int32, row_count)
    segment_row = segment_ids[0]
    allowed = (positions[None, :] <= positions[:, None]) & (
        segment_row[None, :] == segment_row[:, None]
    )

    def masked_scores(start):
        query_block = queries[start : start + block_rows]
        raw = jnp.einsum("qhd,khd->hqk", query_block, keys_low, preferred_element_type=float_type)
        return jnp.where(allowed[start : start + block_rows][None], raw * scale, -1e30)

    total_pieces = []
    attended_pieces = []
    for start in block_starts:
        scores = masked_scores(start)
        top_score = jnp.max(scores, -1, keepdims=True)
        log_piece = top_score + jnp.log(jnp.sum(jnp.exp(scores - top_score), -1, keepdims=True))
        probs_low = jnp.exp(scores - log_piece).astype(half_type)
        total_pieces.append(log_piece)
        attended_pieces.append(
            jnp.einsum("hqk,khd->qhd", probs_low, values_low, preferred_element_type=float_type)
        )
    attended = jnp.concatenate(attended_pieces, 0)
    attended_low = attended.reshape(row_count, width).astype(half_type)
    projected = jnp.dot(attended_low, w_out, preferred_element_type=float_type) + bias_out.astype(
        float_type
    )
    middle = inputs + projected
    expert_full = (
        lax.all_gather(up_weight, ("dp", "fsdp"), axis=0, tiled=True),
        lax.all_gather(down_weight, ("dp", "fsdp"), axis=0, tiled=True),
        lax.all_gather(up_bias, ("dp", "fsdp"), axis=1, tiled=True),
        lax.all_gather(down_bias, ("dp", "fsdp"), axis=1, tiled=True),
        lax.all_gather(ln2_gain, ("dp", "fsdp"), axis=0, tiled=True),
        lax.all_gather(ln2_bias, ("dp", "fsdp"), axis=0, tiled=True),
    )
    w_up, w_down, bias_up, bias_down, gain_two, shift_two = expert_full
    gain_second = gain_two.astype(float_type)
    shift_second = shift_two.astype(float_type)
    normed_two = layer_norm(middle, gain_second, shift_second)
    normed_two_low = normed_two.astype(half_type)
    route_ids = expert_ids[:, 0]
    one_hot = (route_ids[:, None] == lax.iota(jnp.int32, EXPERTS)[None, :]).astype(jnp.int32)
    slot_index = jnp.sum((jnp.cumsum(one_hot, 0) - 1) * one_hot, 1)
    flat_slot = route_ids * CAPACITY + slot_index
    sender = jnp.full((EXPERTS * CAPACITY,), row_count, jnp.int32).at[flat_slot].set(positions)

    def dispatch(values):
        padded = jnp.concatenate([values, jnp.zeros((1, values.shape[1]), values.dtype)], 0)
        return padded[sender].reshape(EXPERTS, CAPACITY, values.shape[1])

    def combine(slotted):
        return slotted.reshape(EXPERTS * CAPACITY, slotted.shape[2])[flat_slot]

    expert_input = dispatch(normed_two_low)
    inner = (
        jnp.einsum("ecd,def->ecf", expert_input, w_up, preferred_element_type=float_type)
        + bias_up.astype(float_type)[:, None, :]
    )
    activated, pull_gelu = jax.vjp(jax.nn.gelu, inner)
    hidden_low = activated.astype(half_type)
    branch = (
        jnp.einsum("ecf,fed->ecd", hidden_low, w_down, preferred_element_type=float_type)
        + bias_down.astype(float_type)[:, None, :]
    )
    result = middle + combine(branch)
    block_out = result.astype(half_type)
    expert_back = (
        lax.all_gather(up_weight, ("dp", "fsdp"), axis=0, tiled=True),
        lax.all_gather(down_weight, ("dp", "fsdp"), axis=0, tiled=True),
        lax.all_gather(up_bias, ("dp", "fsdp"), axis=1, tiled=True),
        lax.all_gather(down_bias, ("dp", "fsdp"), axis=1, tiled=True),
        lax.all_gather(ln2_gain, ("dp", "fsdp"), axis=0, tiled=True),
        lax.all_gather(ln2_bias, ("dp", "fsdp"), axis=0, tiled=True),
    )
    w_up_back = expert_back[0]
    w_down_back = expert_back[1]
    grad_slots = dispatch(cotangent)
    down_grad = jnp.einsum(
        "ecf,ecd->fed", hidden_low, grad_slots, preferred_element_type=float_type
    )
    down_bias_grad = jnp.sum(grad_slots.astype(float_type), 1)
    hidden_grad = jnp.einsum(
        "ecd,fed->ecf", grad_slots, w_down_back, preferred_element_type=float_type
    )
    inner_grad = pull_gelu(hidden_grad)[0].astype(half_type)
    up_grad = jnp.einsum(
        "ecd,ecf->def", expert_input, inner_grad, preferred_element_type=float_type
    )
    up_bias_grad = jnp.sum(inner_grad.astype(float_type), 1)
    normed_two_grad = combine(
        jnp.einsum("ecf,def->ecd", inner_grad, w_up_back, preferred_element_type=float_type)
    )
    ignored_two, pull_two = jax.vjp(layer_norm, middle, gain_second, shift_second)
    middle_part, gain_two_grad, shift_two_grad = pull_two(normed_two_grad)
    middle_grad = cotangent.astype(float_type) + middle_part
    expert_sums = (
        lax.psum_scatter(up_grad, ("dp", "fsdp"), scatter_dimension=0, tiled=True),
        lax.psum_scatter(up_bias_grad, ("dp", "fsdp"), scatter_dimension=1, tiled=True),
        lax.psum_scatter(down_grad, ("dp", "fsdp"), scatter_dimension=0, tiled=True),
        lax.psum_scatter(down_bias_grad, ("dp", "fsdp"), scatter_dimension=1, tiled=True),
        lax.psum_scatter(gain_two_grad, ("dp", "fsdp"), scatter_dimension=0, tiled=True),
        lax.psum_scatter(shift_two_grad, ("dp", "fsdp"), scatter_dimension=0, tiled=True),
    )
    attention_back = (
        lax.all_gather(qkv_weight, ("dp", "fsdp"), axis=0, tiled=True),
        lax.all_gather(out_weight, ("dp", "fsdp"), axis=0, tiled=True),
        lax.all_gather(ln1_gain, ("dp", "fsdp"), axis=0, tiled=True),
        lax.all_gather(ln1_bias, ("dp", "fsdp"), axis=0, tiled=True),
        lax.all_gather(query_bias, ("dp", "fsdp"), axis=0, tiled=True),
        lax.all_gather(value_bias, ("dp", "fsdp"), axis=0, tiled=True),
        lax.all_gather(out_bias, ("dp", "fsdp"), axis=0, tiled=True),
    )
    w_qkv_back = attention_back[0]
    w_out_back = attention_back[1]
    projected_grad = middle_grad.astype(half_type)
    out_grad = jnp.einsum(
        "td,te->de", attended_low, projected_grad, preferred_element_type=float_type
    )
    out_bias_grad = jnp.sum(projected_grad.astype(float_type), 0)
    attended_grad = jnp.einsum(
        "te,de->td", projected_grad, w_out_back, preferred_element_type=float_type
    )
    attended_grad = attended_grad.astype(half_type).reshape(row_count, HEADS, HEAD_DIM)
    values_grad = jnp.zeros((row_count, HEADS, HEAD_DIM), float_type)
    keys_grad = jnp.zeros((row_count, HEADS, HEAD_DIM), float_type)
    query_pieces = []
    for number, start in enumerate(block_starts):
        probs = jnp.exp(masked_scores(start) - total_pieces[number])
        probs_again = probs.astype(half_type)
        grad_block = attended_grad[start : start + block_rows]
        query_block = queries[start : start + block_rows]
        probs_grad = jnp.einsum(
            "qhd,khd->hqk", grad_block, values_low, preferred_element_type=float_type
        )
        values_grad = values_grad + jnp.einsum(
            "hqk,qhd->khd", probs_again, grad_block, preferred_element_type=float_type
        )
        score_grad = probs * (probs_grad - jnp.sum(probs_grad * probs, -1, keepdims=True))
        score_low = (score_grad * scale).astype(half_type)
        query_pieces.append(
            jnp.einsum("hqk,khd->qhd", score_low, keys_low, preferred_element_type=float_type)
        )
        keys_grad = keys_grad + jnp.einsum(
            "hqk,qhd->khd", score_low, query_block, preferred_element_type=float_type
        )
    queries_grad = jnp.concatenate(query_pieces, 0)
    qkv_grad = jnp.concatenate(
        [
            queries_grad.reshape(row_count, width),
            keys_grad.reshape(row_count, width),
            values_grad.reshape(row_count, width),
        ],
        1,
    ).astype(half_type)
    qkv_weight_grad = jnp.einsum(
        "td,te->de", normed_low, qkv_grad, preferred_element_type=float_type
    )
    column_sums = jnp.sum(qkv_grad.astype(float_type), 0)
    query_bias_grad = column_sums[:width]
    value_bias_grad = column_sums[2 * width :]
    normed_one_grad = jnp.einsum(
        "te,de->td", qkv_grad, w_qkv_back, preferred_element_type=float_type
    )
    ignored_one, pull_one = jax.vjp(layer_norm, inputs, gain_first, shift_first)
    input_part, gain_one_grad, shift_one_grad = pull_one(normed_one_grad)
    input_grad = middle_grad + input_part
    attention_sums = (
        lax.psum_scatter(qkv_weight_grad, ("dp", "fsdp"), scatter_dimension=0, tiled=True),
        lax.psum_scatter(out_grad, ("dp", "fsdp"), scatter_dimension=0, tiled=True),
        lax.psum_scatter(gain_one_grad, ("dp", "fsdp"), scatter_dimension=0, tiled=True),
        lax.psum_scatter(shift_one_grad, ("dp", "fsdp"), scatter_dimension=0, tiled=True),
        lax.psum_scatter(query_bias_grad, ("dp", "fsdp"), scatter_dimension=0, tiled=True),
        lax.psum_scatter(value_bias_grad, ("dp", "fsdp"), scatter_dimension=0, tiled=True),
        lax.psum_scatter(out_bias_grad, ("dp", "fsdp"), scatter_dimension=0, tiled=True),
    )
    return (
        block_out,
        input_grad,
        attention_sums[2],
        attention_sums[3],
        attention_sums[0],
        attention_sums[4],
        attention_sums[5],
        attention_sums[1],
        attention_sums[6],
        expert_sums[4],
        expert_sums[5],
        expert_sums[0],
        expert_sums[1],
        expert_sums[2],
        expert_sums[3],
    )


def solution(mesh):
    in_specs = (
        P(("dp", "fsdp"), None),
        P(("dp", "fsdp"), None),
        P(("dp", "fsdp"), None),
        P(("dp", "fsdp")),
        P(("dp", "fsdp")),
        P(("dp", "fsdp"), None),
        P(("dp", "fsdp")),
        P(("dp", "fsdp")),
        P(("dp", "fsdp"), None),
        P(("dp", "fsdp")),
        P(("dp", "fsdp")),
        P(("dp", "fsdp")),
        P(("dp", "fsdp"), None, None),
        P(None, ("dp", "fsdp")),
        P(("dp", "fsdp"), None, None),
        P(None, ("dp", "fsdp")),
        P(("dp", "fsdp"), None),
    )
    out_specs = (
        P(("dp", "fsdp"), None),
        P(("dp", "fsdp"), None),
        P(("dp", "fsdp")),
        P(("dp", "fsdp")),
        P(("dp", "fsdp"), None),
        P(("dp", "fsdp")),
        P(("dp", "fsdp")),
        P(("dp", "fsdp"), None),
        P(("dp", "fsdp")),
        P(("dp", "fsdp")),
        P(("dp", "fsdp")),
        P(("dp", "fsdp"), None, None),
        P(None, ("dp", "fsdp")),
        P(("dp", "fsdp"), None, None),
        P(None, ("dp", "fsdp")),
    )
    return jax.shard_map(shards, mesh=mesh, in_specs=in_specs, out_specs=out_specs, check_vma=False)
```

profile of v0, /device:TPU:0, one launch (start us, length us, event | category | flops | bytes accessed | tf_op | source)
XLA Modules:
  0.0 1819.6 jit_solution(12890577069319250570)
XLA Ops:
  18.5 4.3 scatter_custom_fusion
  22.9 5.1 gather_fusion.2
  33.2 43.4 %all-reduce.18 = (bf16[1024]{0:T(1024)(128)(2,1)S(1)}, bf16[1024]{0:T(1024)(128)(2,1)S(1)}, bf16[1024]{0:T(1024)(128)(2,1)S(1)}, bf16[1024]{0:T(1024)(128)(2,1)S...) all-reduce(bf16[1024]{0:T(1024)(128)(2,1)S(1)} %dynamic-update-slic, ...), channel_id=1, replica_groups=mesh['dp'=4,'fsdp'=8] {'dp','fsdp'}, use_global_device_ids=true, to_apply=%add.6 | all-reduce | flops 7168 | bytes 28672
  81.6 39.9 %all_gather.53 = bf16[2,4096]{1,0:T(2,128)(2,1)S(1)} all-gather(bf16[2,128]{1,0:T(2,128)(2,1)S(1)} %copy-done.59), channel_id=1, replica_groups=mesh['dp'=4,'fsdp'=8] {'dp','fsdp'}, dimensions={1}, use_global_device_ids=true | all-gather | bytes 16896 | tf_op jit(solution)/shard_map/all_gather | solution.py:101
  123.2 10.3 add_convert_fusion
  137.5 2.9 copy.74
  142.6 2.7 copy.75
  145.2 3.9 copy.72
  149.2 15.5 fusion.5
  164.7 14.2 fusion.4
  178.9 25.7 %exponential_reduce_fusion = (f32[16,512]{1,0:T(8,128)S(1)}, f32[16,512]{1,0:T(8,128)S(1)}) fusion(f32[16,512,1024]{2,1,0:T(8,128)} %get-tuple-element.114, f32[16,512]{1,0:T(8,128)S(1)} %get-tuple-element.113, pred[512,1024]{1,0:T(8,128)(4,1)S(1)} %copy-done.16, f32[16,512]{1,0:T(8,128)S(1)} %get-tuple-element.115, f32[16,512,1024]{2,1,0:T(8,128)} %get-tuple-element.116, ...), kind=kLoop, calls=%fused_computation.14 | loop fusion | flops 67092480 | bytes 68288512 | tf_op jit(solution)/shard_map/reduce_sum | solution.py:86
  204.7 17.6 fusion.90
  222.3 15.7 fusion.91
  240.2 5.6 fusion.145
  248.8 5.1 gather_fusion
  253.8 4.9 all-gather.10.cloned.1.call-done
  258.7 19.5 %fusion.146 = f32[2,640,4096]{2,1,0:T(8,128)} fusion(bf16[2,640,1024]{2,1,0:T(8,128)(2,1)} %bitcast.116, bf16[1024,2,4096]{2,0,1:T(8,128)(2,1)} %all-gather.10.cloned.1.call-done), kind=kOutput, calls=%fused_computation.161 | convolution fusion | flops 10737418240 | bytes 40370176 | tf_op jit(solution)/shard_map/ecd,def->ecf/dot_general | solution.py:126
  278.1 96.4 %all-gather.12.cloned.1.call-done = bf16[4096,2,1024]{2,0,1:T(8,128)(2,1)} async-done(((bf16[128,2,1024]{2,0,1:T(8,128)(2,1)}), bf16[4096,2,1024]{2,0,1:T(8,128)(2,1)}) %all-gather.12.cloned.1.call-update) | async-done | bytes 16777232 | tf_op jit(solution)/shard_map/all_gather | solution.py:100
  374.6 29.6 %convert_reduce_fusion = (f32[2,4096]{1,0:T(2,128)S(1)}, bf16[2,640,4096]{2,1,0:T(8,128)(2,1)}) fusion(f32[2,640,4096]{2,1,0:T(8,128)} %fusion.146, f32[2,4096]{1,0:T(2,128)S(1)} %convert_element_type.108, bf16[2,640,1024]{2,1,0:T(8,128)(2,1)S(1)} %bitcast.102, bf16[4096,2,1024]{2,0,1:T(8,128)(2,1)} %all-gather.12.cloned.1.call-done), kind=kOutput, calls=%fused_computation.30 | convolution fusion | flops 10857996288 | bytes 50921472 | tf_op jit(solution)/shard_map/ecd,fed->ecf/dot_general | solution.py:152
  406.2 22.7 %convolution_bitcast_fusion = f32[1024,2,4096]{0,2,1:T(8,128)} fusion(bf16[2,640,4096]{2,1,0:T(8,128)(2,1)} %get-tuple-element.97, bf16[2,640,1024]{2,1,0:T(8,128)(2,1)} %bitcast.117), kind=kOutput, calls=%fused_computation.54 | convolution fusion | flops 10737418240 | bytes 46661632 | tf_op jit(solution)/shard_map/ecd,ecf->def/dot_general | solution.py:156
  429.0 49.3 %copy.80 = f32[1024,2,4096]{2,1,0:T(2,128)} copy(f32[1024,2,4096]{0,2,1:T(8,128)} %convolution_bitcast_fusion) | data formatting | bytes 67108864 | tf_op jit(solution)/shard_map/ecd,ecf->def/transpose | solution.py:156
  478.4 25.4 %convolution_bitcast_fusion.1 = f32[4096,2,1024]{0,2,1:T(8,128)} fusion(bf16[2,640,1024]{2,1,0:T(8,128)(2,1)S(1)} %bitcast.103, f32[2,640,4096]{2,1,0:T(8,128)} %fusion.146, f32[2,4096]{1,0:T(2,128)S(1)} %convert_element_type.108), kind=kOutput, calls=%fused_computation.55 | convolution fusion | flops 10789847040 | bytes 57180160 | tf_op jit(solution)/shard_map/ecf,ecd->fed/dot_general | solution.py:148
  504.4 38.4 %all-gather = bf16[32,32,2]{1,2,0:T(2,128)(2,1)S(1)} all-gather(bf16[1,32,2]{1,2,0:T(2,128)(2,1)S(1)} %bitcast.137), channel_id=1, replica_groups=mesh['dp'=4,'fsdp'=8] {'dp','fsdp'}, dimensions={0}, use_global_device_ids=true | all-gather | bytes 4224 | tf_op jit(solution)/shard_map/all_gather | solution.py:102
  543.0 19.3 %fusion.147 = f32[2,640,1024]{2,1,0:T(8,128)} fusion(bf16[2,640,4096]{2,1,0:T(8,128)(2,1)} %get-tuple-element.97, bf16[1024,2,4096]{2,0,1:T(8,128)(2,1)} %all-gather.10.cloned.1.call-done), kind=kOutput, calls=%fused_computation.162 | convolution fusion | flops 10737418240 | bytes 32505856 | tf_op jit(solution)/shard_map/ecf,def->ecd/dot_general | solution.py:161
  562.3 8.8 gather_fusion.3
  571.2 24.0 %broadcast_add_fusion = f32[2,640,1024]{2,1,0:T(8,128)} fusion(f32[2,1024]{1,0:T(2,128)S(1)} %bitcast.135, bf16[4096,2,1024]{2,0,1:T(8,128)(2,1)} %all-gather.12.cloned.1.call-done, f32[2,640,4096]{2,1,0:T(8,128)} %fusion.146, f32[2,4096]{1,0:T(2,128)S(1)} %convert_element_type.108), kind=kOutput, calls=%fused_computation.89 | convolution fusion | flops 10791157760 | bytes 43032576 | tf_op jit(solution)/shard_map/ecf,fed->ecd/dot_general | solution.py:132
  595.2 8.9 gather_fusion.1
  604.2 5.6 multiply_reduce_fusion.2
  610.1 4.8 fusion.139
  621.6 13.2 fusion.149
  634.8 59.4 %fusion.87 = bf16[512,16,64]{0,2,1:T(8,128)(2,1)} fusion(bf16[1024,16,64]{0,2,1:T(8,128)(2,1)S(1)} %bitcast.95, f32[16,512,1024]{2,1,0:T(8,128)} %fusion.149, f32[16,512,1024]{2,1,0:T(8,128)} %get-tuple-element.114, f32[16,512]{1,0:T(8,128)S(1)} %copy-done.48, pred[512,1024]{1,0:T(8,128)(4,1)} %get-tuple-element.110), kind=kOutput, calls=%fused_computation.98 | convolution fusion | flops 1166550016 | bytes 70811648 | tf_op jit(solution)/shard_map/hqk,khd->qhd/dot_general | solution.py:211
  694.1 6.9 fusion.150
  701.2 15.8 fusion.148
  717.0 62.9 %fusion.84 = bf16[512,16,64]{0,2,1:T(8,128)(2,1)} fusion(bf16[1024,16,64]{0,2,1:T(8,128)(2,1)S(1)} %bitcast.96, f32[16,512,1024]{2,1,0:T(8,128)} %fusion.148, f32[16,512,1024]{2,1,0:T(8,128)} %get-tuple-element.116, f32[16,512]{1,0:T(8,128)S(1)} %copy-done.50, pred[512,1024]{1,0:T(8,128)(4,1)} %get-tuple-element.109), kind=kOutput, calls=%fused_computation.97 | convolution fusion | flops 1166550016 | bytes 70811648 | tf_op jit(solution)/shard_map/hqk,khd->qhd/dot_general | solution.py:211
  779.8 3.2 pad_maximum_fusion.2
  783.0 61.5 %fusion.19 = f32[16,64,1024]{2,1,0:T(8,128)} fusion(bf16[512,16,64]{0,2,1:T(8,128)(2,1)S(1)} %bitcast.105, f32[16,512,1024]{2,1,0:T(8,128)} %fusion.148, f32[16,512,1024]{2,1,0:T(8,128)} %get-tuple-element.116, f32[16,512]{1,0:T(8,128)S(1)} %copy-done.50, pred[512,1024]{1,0:T(8,128)(4,1)} %get-tuple-element.109), kind=kOutput, calls=%fused_computation.33 | convolution fusion | flops 1166025728 | bytes 72908800 | tf_op jit(solution)/shard_map/hqk,qhd->khd/dot_general | solution.py:213
  844.6 60.4 %add_convert_fusion.2 = bf16[16,64,1024]{2,1,0:T(8,128)(2,1)} fusion(f32[16,64,1024]{2,1,0:T(8,128)} %fusion.19, bf16[512,16,64]{0,2,1:T(8,128)(2,1)S(1)} %bitcast.107, f32[16,512,1024]{2,1,0:T(8,128)} %fusion.149, f32[16,512,1024]{2,1,0:T(8,128)} %get-tuple-element.114, f32[16,512]{1,0:T(8,128)S(1)} %copy-done.48, pred[512,1024]{1,0:T(8,128)(4,1)} %get-tuple-element.110), kind=kOutput, calls=%fused_computation.80 | convolution fusion | flops 1168122880 | bytes 75005952 | tf_op jit(solution)/shard_map/hqk,qhd->khd/dot_general | solution.py:213
  905.0 17.6 fusion.94
  922.6 19.9 %add_convert_fusion.1 = bf16[16,64,1024]{2,1,0:T(8,128)(2,1)} fusion(f32[16,64,1024]{2,1,0:T(8,128)} %fusion.94, bf16[512,16,64]{0,2,1:T(8,128)(2,1)} %bitcast.113, f32[16,512,1024]{2,1,0:T(8,128)} %get-tuple-element.114, f32[16,512]{1,0:T(8,128)S(1)} %copy-done.48, pred[512,1024]{1,0:T(8,128)(4,1)S(1)} %copy-done.18), kind=kOutput, calls=%fused_computation.79 | convolution fusion | flops 1109393408 | bytes 41451520 | tf_op jit(solution)/shard_map/hqk,qhd->khd/dot_general | solution.py:205
  942.5 14.6 fusion.131
  958.6 11.7 fusion.136
  970.4 4.8 convert_reduce_fusion.1
  977.5 40.5 %all-reduce.17 = (f32[1024]{0:T(1024)S(1)}, f32[1024]{0:T(1024)S(1)}, f32[1024]{0:T(1024)S(1)}, f32[1024]{0:T(1024)S(1)}, f32[1024]{0:T(1024)S(1)}, /*index=5*/f32[1024]{0:T(1024)S(1)}, f32[1024]{0:T(1024)S(1)}) all-reduce(f32[1024]{0:T(1024)S(1)} %get-tuple-element.77, ...), channel_id=2, replica_groups=mesh['dp'=4,'fsdp'=8] {'dp','fsdp'}, use_global_device_ids=true, to_apply=%region_19.20.clone | all-reduce | flops 7168 | bytes 57344
  1022.1 6.8 add_add_fusion.2
  1030.4 117.0 %all-reduce.21.cloned.1.call-done = f32[1024,2,4096]{2,1,0:T(2,128)} async-done(((f32[1024,2,4096]{2,1,0:T(2,128)}), f32[1024,2,4096]{2,1,0:T(2,128)}) %all-reduce.21.cloned.1.call-update) | async-done | bytes 33554448
  1149.7 360.8 %reduce-scatter.14.cloned.1.call-done = f32[128,2,1024]{0,2,1:T(8,128)} async-done(((f32[4096,2,1024]{0,2,1:T(8,128)}), f32[128,2,1024]{0,2,1:T(8,128)}) %reduce-scatter.14.cloned.1.call-update) | async-done | bytes 1048592 | tf_op jit(solution)/shard_map/reduce_scatter | solution.py:169
  1512.8 139.9 %reduce-scatter.12.cloned.1.call-done = f32[32,1024]{1,0:T(8,128)} async-done(((f32[1024,1024]{1,0:T(8,128)}), f32[32,1024]{1,0:T(8,128)}) %reduce-scatter.12.cloned.1.call-update) | async-done | bytes 131088 | tf_op jit(solution)/shard_map/reduce_scatter | solution.py:239
  1652.7 159.6 %reduce-scatter.10.cloned.1.call-done = f32[32,3072]{1,0:T(8,128)} async-done(((f32[1024,3072]{1,0:T(8,128)}), f32[32,3072]{1,0:T(8,128)}) %reduce-scatter.10.cloned.1.call-update) | async-done | bytes 393232 | tf_op jit(solution)/shard_map/reduce_scatter | solution.py:238
  (240 shorter events, 57.9 us)
Async XLA Ops:
  7.2 116.0 %all-gather.6.cloned.1.call-start = ((), (), s32[]{:S(2)}) async-start(), calls=%async_computation.5 | async-start | bytes 6488064 | tf_op jit(solution)/shard_map/all_gather | solution.py:43
  7.9 232.3 %all-gather.8.cloned.1.call-start = ((), (), s32[]{:S(2)}) async-start(), calls=%async_computation.6 | async-start | bytes 2162688 | tf_op jit(solution)/shard_map/all_gather | solution.py:44
  8.7 250.0 %all-gather.10.cloned.1.call-start = ((), (), s32[]{:S(2)}) async-start(), calls=%async_computation.7 | async-start | bytes 17301504 | tf_op jit(solution)/shard_map/all_gather | solution.py:99
  10.9 363.7 %all-gather.12.cloned.1.call-start = ((), (), s32[]{:S(2)}) async-start(), calls=%async_computation.8 | async-start | bytes 17301504 | tf_op jit(solution)/shard_map/all_gather | solution.py:100
  12.9 944.3 %reduce-scatter.18.cloned.1.call-start = ((), (), s32[]{:S(2)}) async-start(), calls=%async_computation.13 | async-start | bytes 540672
  22.9 10.0 copy-start.68
  22.9 58.7 %copy-start.59 = (bf16[2,128]{1,0:T(2,128)(2,1)S(1)}, bf16[2,128]{1,0:T(2,128)(2,1)}, u32[]{:S(2)}) copy-start(bf16[2,128]{1,0:T(2,128)(2,1)} %param.30) | copy-start | bytes 1540
  22.9 98.6 %copy-start.54 = (s32[1,1024]{1,0:T(1,128)S(1)}, s32[1,1024]{1,0:T(1,128)}, u32[]{:S(2)}) copy-start(s32[1,1024]{1,0:T(1,128)} %param.18) | copy-start | bytes 12292
  28.0 95.1 %copy-start.8 = (bf16[1024,1024]{1,0:T(8,128)(2,1)S(1)}, bf16[1024,1024]{1,0:T(8,128)(2,1)}, u32[]{:S(2)}) copy-start(bf16[1024,1024]{1,0:T(8,128)(2,1)} %param.17) | copy-start | bytes 6291460
  31.4 997.5 %reduce-scatter.16.cloned.1.call-start = ((), (), s32[]{:S(2)}) async-start(), calls=%async_computation.12 | async-start | bytes 2162688
  76.6 56.9 %copy-start.39 = (f32[1024]{0:T(1024)}, f32[1024]{0:T(1024)S(1)}, u32[]{:S(2)}) copy-start(f32[1024]{0:T(1024)S(1)} %convert_element_type.95) | copy-start | bytes 12292
  76.6 170.8 %copy-start.31 = (f32[1024]{0:T(1024)}, f32[1024]{0:T(1024)S(1)}, u32[]{:S(2)}) copy-start(f32[1024]{0:T(1024)S(1)} %convert_element_type.104) | copy-start | bytes 12292
  76.6 56.9 %copy-start.57 = (f32[1024]{0:T(1024)}, f32[1024]{0:T(1024)S(1)}, u32[]{:S(2)}) copy-start(f32[1024]{0:T(1024)S(1)} %convert_element_type.96) | copy-start | bytes 12292
  78.6 54.9 %copy-start.35 = (f32[1024]{0:T(1024)}, f32[1024]{0:T(1024)S(1)}, u32[]{:S(2)}) copy-start(f32[1024]{0:T(1024)S(1)} %broadcast_multiply_fusion.1) | copy-start | bytes 12292
  81.6 51.9 %copy-start.41 = (f32[1024]{0:T(1024)}, f32[1024]{0:T(1024)S(1)}, u32[]{:S(2)}) copy-start(f32[1024]{0:T(1024)S(1)} %fusion.101) | copy-start | bytes 12292
  140.4 24.4 %copy-start.2 = (bf16[1024,1024]{0,1:T(8,128)(2,1)}, bf16[1024,1024]{0,1:T(8,128)(2,1)S(1)}, u32[]{:S(2)}) copy-start(bf16[1024,1024]{0,1:T(8,128)(2,1)S(1)} %copy.74) | copy-start | bytes 6291460
  142.6 22.1 %copy-start.13 = (bf16[512,1024]{0,1:T(8,128)(2,1)}, bf16[512,1024]{0,1:T(8,128)(2,1)S(1)}, u32[]{:S(2)}) copy-start(bf16[512,1024]{0,1:T(8,128)(2,1)S(1)} %copy.73) | copy-start | bytes 3145732
  149.2 15.5 copy-start.19
  164.7 14.2 copy-start.16
  178.9 25.7 %copy-start.4 = (bf16[1024,1024]{0,1:T(8,128)(2,1)S(1)}, bf16[1024,1024]{0,1:T(8,128)(2,1)}, u32[]{:S(2)}) copy-start(bf16[1024,1024]{0,1:T(8,128)(2,1)} %copy.72) | copy-start | bytes 6291460
  178.9 25.7 %copy-start.20 = (pred[512,1024]{1,0:T(8,128)(4,1)S(1)}, pred[512,1024]{1,0:T(8,128)(4,1)}, u32[]{:S(2)}) copy-start(pred[512,1024]{1,0:T(8,128)(4,1)} %get-tuple-element.109) | copy-start | bytes 1572868
  204.6 17.7 copy-start.47
  204.7 17.7 copy-start.49
  204.7 17.7 copy-start.17
  258.7 115.9 %copy-start.12 = (bf16[1280,1024]{1,0:T(8,128)(2,1)S(1)}, bf16[1280,1024]{1,0:T(8,128)(2,1)}, u32[]{:S(2)}) copy-start(bf16[1280,1024]{1,0:T(8,128)(2,1)} %gather_fusion.2) | copy-start | bytes 7864324
  406.2 741.2 %all-reduce.21.cloned.1.call-start = ((), (), s32[]{:S(2)}) async-start(), calls=%async_computation.14 | async-start | bytes 67108864
  478.3 1032.2 %reduce-scatter.14.cloned.1.call-start = ((), (), s32[]{:S(2)}) async-start(), calls=%async_computation.11 | async-start | bytes 34603008 | tf_op jit(solution)/shard_map/reduce_scatter | solution.py:169
  503.8 39.2 %copy-start.56 = (s32[1024,1]{0,1:T(1,128)S(1)}, s32[1024,1]{0,1:T(1,128)}, u32[]{:S(2)}) copy-start(s32[1024,1]{0,1:T(1,128)} %copy-done.55) | copy-start | bytes 12292
  503.8 1148.8 %reduce-scatter.12.cloned.1.call-start = ((), (), s32[]{:S(2)}) async-start(), calls=%async_computation.10 | async-start | bytes 4325376 | tf_op jit(solution)/shard_map/reduce_scatter | solution.py:239
  620.6 80.5 %copy-start.24 = (bf16[512,1024]{0,1:T(8,128)(2,1)}, bf16[512,1024]{0,1:T(8,128)(2,1)S(1)}, u32[]{:S(2)}) copy-start(bf16[512,1024]{0,1:T(8,128)(2,1)S(1)} %get-tuple-element.108) | copy-start | bytes 3145732
  621.6 13.2 copy-start.3
  621.6 13.2 copy-start.48
  701.1 1111.2 %reduce-scatter.10.cloned.1.call-start = ((), (), s32[]{:S(2)}) async-start(), calls=%async_computation.9 | async-start | bytes 12976128 | tf_op jit(solution)/shard_map/reduce_scatter | solution.py:238
  701.2 15.8 copy-start.50
  717.0 66.0 %copy-start.14 = (bf16[512,1024]{0,1:T(8,128)(2,1)S(1)}, bf16[512,1024]{0,1:T(8,128)(2,1)}, u32[]{:S(2)}) copy-start(bf16[512,1024]{0,1:T(8,128)(2,1)} %copy-done.13) | copy-start | bytes 3145732
  783.0 61.5 %copy-start.15 = (bf16[512,1024]{0,1:T(8,128)(2,1)S(1)}, bf16[512,1024]{0,1:T(8,128)(2,1)}, u32[]{:S(2)}) copy-start(bf16[512,1024]{0,1:T(8,128)(2,1)} %copy.75) | copy-start | bytes 3145732
  844.5 60.4 %copy-start.21 = (pred[512,1024]{1,0:T(8,128)(4,1)S(1)}, pred[512,1024]{1,0:T(8,128)(4,1)}, u32[]{:S(2)}) copy-start(pred[512,1024]{1,0:T(8,128)(4,1)} %get-tuple-element.109) | copy-start | bytes 1572868
  905.0 17.6 copy-start.18
  922.5 19.9 %copy-start.9 = (bf16[1024,1024]{1,0:T(8,128)(2,1)S(1)}, bf16[1024,1024]{1,0:T(8,128)(2,1)}, u32[]{:S(2)}) copy-start(bf16[1024,1024]{1,0:T(8,128)(2,1)} %param.17) | copy-start | bytes 6291460
  922.5 19.9 %copy-start.36 = (f32[1024]{0:T(1024)S(1)}, f32[1024]{0:T(1024)}, u32[]{:S(2)}) copy-start(f32[1024]{0:T(1024)} %copy-done.35) | copy-start | bytes 12292
  922.6 19.9 %copy-start.40 = (f32[1024]{0:T(1024)S(1)}, f32[1024]{0:T(1024)}, u32[]{:S(2)}) copy-start(f32[1024]{0:T(1024)} %copy-done.39) | copy-start | bytes 12292
  922.6 19.9 %copy-start.42 = (f32[1024]{0:T(1024)S(1)}, f32[1024]{0:T(1024)}, u32[]{:S(2)}) copy-start(f32[1024]{0:T(1024)} %copy-done.41) | copy-start | bytes 12292
  922.6 19.9 %copy-start.58 = (f32[1024]{0:T(1024)S(1)}, f32[1024]{0:T(1024)}, u32[]{:S(2)}) copy-start(f32[1024]{0:T(1024)} %copy-done.57) | copy-start | bytes 12292
  958.6 11.8 copy-start.44
  958.6 11.8 copy-start.22
  958.6 11.8 copy-start.27
  958.6 11.8 copy-start.28
  970.3 51.8 %copy-start.38 = (f32[1024]{0:T(1024)S(1)}, f32[1024]{0:T(1024)}, u32[]{:S(2)}) copy-start(f32[1024]{0:T(1024)} %copy-done.37) | copy-start | bytes 12292
  (31 other events, 168.1 us)
Sparse Core Ops, SparseCore 0:
  11.0 72.1 all-gather.5
  86.2 55.7 all-gather.7
  145.0 113.6 all-gather.9
  261.6 112.9 all-gather.11
  376.7 132.1 reduce-scatter.17
  511.1 133.0 reduce-scatter.15
  650.6 496.7 all-reduce.20
  1149.8 360.6 reduce-scatter.13
  1513.5 139.1 reduce-scatter.11
  1660.1 152.0 reduce-scatter.9
where the time goes:
time: 1830 us; the launch traced here: 1820 us
  waiting for transfers between devices  880 us (48%)
  matrix products  566 us (31%)
  blocking collectives  162 us (9%)
  local copies, waits for them, and re-layouts  127 us (7%)
  other arithmetic  68 us (4%)
    reduce_scatter x1, waiting for transfers between devices, shards(): lax.psum_scatter(down_grad, ('dp', 'fsdp'), scatter_dimension=0, tiled=True)  361 us
    reduce_scatter x1, waiting for transfers between devices, shards(): lax.psum_scatter(qkv_weight_grad, ('dp', 'fsdp'), scatter_dimension=0, ti...  160 us
    reduce_scatter x1, waiting for transfers between devices, shards(): lax.psum_scatter(out_grad, ('dp', 'fsdp'), scatter_dimension=0, tiled=True)  140 us
    dot_general x2, matrix products, shards(): jnp.einsum('hqk,khd->qhd', score_low, keys_low, preferred_element_type=fl...  122 us
    dot_general x2, matrix products, shards(): jnp.einsum('hqk,qhd->khd', score_low, query_block, preferred_element_type...  122 us
    unnamed x13, waiting for transfers between devices  119 us
    all_gather x1, waiting for transfers between devices, shards(): lax.all_gather(down_weight, ('dp', 'fsdp'), axis=0, tiled=True)  96.4 us
    unnamed x2, blocking collectives  84 us
  transfers between devices with their start and end apart: 10, of which 6 were waited for; matrix products, arithmetic and copies ran while one was open for 41% of the time, Pallas kernels for 0%

commit v1 on v0

v1 whole, which is shorter than its diff:
```python
import functools

import jax
import jax.numpy as jnp
from jax import lax
from jax.experimental import pallas as pl
from jax.experimental.pallas import tpu as pltpu
from jax.sharding import Mesh, PartitionSpec as P

HEAD_DIM = 64
CAPACITY = 640
LONGEST = 512
PAIR = 2 * HEAD_DIM
TILE_Q = 256
MASKED = -1e30
epsilon = 1e-05
bf16 = jnp.bfloat16
f32 = jnp.float32
ALL = ("dp", "z", "c")
NN = (((1,), (0,)), ((), ()))
NT = (((1,), (1,)), ((), ()))
TN = (((0,), (0,)), ((), ()))


def dot(a, b, dims=NN):
    return lax.dot_general(a, b, dims, preferred_element_type=f32)


def spans(rows):
    out = []
    for start in range(0, rows, TILE_Q):
        low = max(0, (start - LONGEST + 1) // TILE_Q * TILE_Q)
        out.append((start, low, start + TILE_Q))
    return out


def fill_bias(bias_refs, seg_col, seg_row, blocks):
    for bias, (start, low, high) in zip(bias_refs, blocks):
        shape = (high - low, TILE_Q)
        key = low + lax.broadcasted_iota(jnp.int32, shape, 0)
        query = start + lax.broadcasted_iota(jnp.int32, shape, 1)
        same = seg_col[low:high, :] == seg_row[:, start : start + TILE_Q]
        bias[...] = jnp.where((key <= query) & same, 0.0, MASKED)


def forward_kernel(blocks, seg_col, seg_row, q_ref, k_ref, v_ref, o_ref, lse_ref, *bias):
    @pl.when(pl.program_id(0) == 0)
    def _():
        fill_bias(bias, seg_col, seg_row, blocks)

    lane = lax.broadcasted_iota(jnp.int32, (TILE_Q, PAIR), 1)
    for masked, (start, low, high) in zip(bias, blocks):
        rows = slice(start, start + TILE_Q)
        q = q_ref[rows, :] * jnp.asarray(HEAD_DIM**-0.5, bf16)
        k = k_ref[low:high, :]
        v = v_ref[low:high, :]
        heads = []
        for head in range(2):
            mine = (lane < HEAD_DIM) == (head == 0)
            scores = dot(k, jnp.where(mine, q, jnp.zeros_like(q)), NT) + masked[...]
            top = jnp.max(scores, 0, keepdims=True)
            probs = jnp.exp(scores - top)
            total = jnp.sum(probs, 0, keepdims=True)
            out = dot(v, probs.astype(bf16), TN)
            heads.append(out[head * HEAD_DIM : (head + 1) * HEAD_DIM] * (1.0 / total))
            lse_ref[0, head : head + 1, rows] = top + jnp.log(total)
        o_ref[rows, :] = jnp.concatenate(heads, 0).T.astype(bf16)


def attention(qkv, seg_col, seg_row):
    rows, width = qkv.shape[0], qkv.shape[1] // 3
    pairs = width // PAIR
    blocks = spans(rows)
    return pl.pallas_call(
        functools.partial(forward_kernel, blocks),
        out_shape=(
            jax.ShapeDtypeStruct((rows, width), bf16),
            jax.ShapeDtypeStruct((pairs, 2, rows), f32),
        ),
        grid=(pairs,),
        in_specs=[
            pl.BlockSpec((rows, 1), lambda p: (0, 0)),
            pl.BlockSpec((1, rows), lambda p: (0, 0)),
            pl.BlockSpec((rows, PAIR), lambda p: (0, p)),
            pl.BlockSpec((rows, PAIR), lambda p: (0, pairs + p)),
            pl.BlockSpec((rows, PAIR), lambda p: (0, 2 * pairs + p)),
        ],
        out_specs=(
            pl.BlockSpec((rows, PAIR), lambda p: (0, p)),
            pl.BlockSpec((1, 2, rows), lambda p: (p, 0, 0)),
        ),
        scratch_shapes=[pltpu.VMEM((high - low, TILE_Q), f32) for _, low, high in blocks],
        compiler_params=pltpu.CompilerParams(vmem_limit_bytes=48 << 20),
        name="attention_forward",
    )(seg_col, seg_row, qkv, qkv, qkv)


def backward_kernel(
    blocks, first, seg_col, seg_row, q_ref, k_ref, v_ref, do_ref, lse_ref, d_ref, dk_sum, dv_sum, *bias
):
    @pl.when(pl.program_id(0) == 0)
    def _():
        fill_bias(bias, seg_col, seg_row, blocks)

    dk_sum[...] = jnp.zeros_like(dk_sum)
    dv_sum[...] = jnp.zeros_like(dv_sum)
    lane = lax.broadcasted_iota(jnp.int32, (TILE_Q, PAIR), 1)
    scale = HEAD_DIM**-0.5
    for masked, (start, low, high) in zip(bias, blocks):
        rows = slice(start, start + TILE_Q)
        q = q_ref[rows, :]
        do = do_ref[rows, :]
        k = k_ref[low:high, :]
        v = v_ref[low:high, :]
        scaled = q * jnp.asarray(scale, bf16)
        zero = jnp.zeros_like(q)
        dq, dk, dv = [], 0.0, 0.0
        for head in range(2):
            mine = (lane < HEAD_DIM) == (head == 0)
            do_head = jnp.where(mine, do, zero)
            scores = dot(k, jnp.where(mine, scaled, zero), NT) + masked[...]
            probs = jnp.exp(scores - lse_ref[0, head : head + 1, rows])
            weighted = probs * dot(v, do_head, NT)
            total = jnp.sum(weighted, 0, keepdims=True)
            ds = ((weighted - probs * total) * scale).astype(bf16)
            dv = dv + dot(probs.astype(bf16), do_head)
            dk = dk + dot(ds, jnp.where(mine, q, zero))
            dq.append(dot(k, ds, TN)[head * HEAD_DIM : (head + 1) * HEAD_DIM])
        d_ref[0, rows, :] = jnp.concatenate(dq, 0).T.astype(bf16)
        dk_sum[low:high, :] += dk
        dv_sum[low:high, :] += dv
    d_ref[1, ...] = dk_sum[...].astype(bf16)
    d_ref[2, ...] = dv_sum[...].astype(bf16)


def attention_grad(qkv, do, lse, seg_col, seg_row, half):
    rows, width = qkv.shape[0], qkv.shape[1] // 3
    pairs = width // PAIR
    count = pairs // 2
    blocks = spans(rows)
    first = jnp.reshape(half * count, (1,)).astype(jnp.int32)
    return pl.pallas_call(
        functools.partial(backward_kernel, blocks),
        out_shape=jax.ShapeDtypeStruct((3, rows, count * PAIR), bf16),
        grid_spec=pltpu.PrefetchScalarGridSpec(
            num_scalar_prefetch=1,
            grid=(count,),
            in_specs=[
                pl.BlockSpec((rows, 1), lambda p, b: (0, 0)),
                pl.BlockSpec((1, rows), lambda p, b: (0, 0)),
                pl.BlockSpec((rows, PAIR), lambda p, b: (0, b[0] + p)),
                pl.BlockSpec((rows, PAIR), lambda p, b: (0, pairs + b[0] + p)),
                pl.BlockSpec((rows, PAIR), lambda p, b: (0, 2 * pairs + b[0] + p)),
                pl.BlockSpec((rows, PAIR), lambda p, b: (0, b[0] + p)),
                pl.BlockSpec((1, 2, rows), lambda p, b: (b[0] + p, 0, 0)),
            ],
            out_specs=pl.BlockSpec((3, rows, PAIR), lambda p, b: (0, 0, p)),
            scratch_shapes=[pltpu.VMEM((rows, PAIR), f32)] * 2
            + [pltpu.VMEM((high - low, TILE_Q), f32) for _, low, high in blocks],
        ),
        compiler_params=pltpu.CompilerParams(vmem_limit_bytes=48 << 20),
        name="attention_backward",
    )(first, seg_col, seg_row, qkv, qkv, qkv, do, lse)


def layer_norm(values, gain, shift):
    centre = values - jnp.mean(values, -1, keepdims=True)
    spread = jnp.mean(centre * centre, -1, keepdims=True)
    return centre * lax.rsqrt(spread + epsilon) * gain + shift


def pick(array, index, axis=0):
    return lax.dynamic_index_in_dim(array, index, axis, keepdims=False)


def swap(value, axis, size, mask):
    return lax.ppermute(value, axis, [(i, i ^ mask) for i in range(size)])


def swap_core(value):
    return swap(value, "c", 2, 1)


def by_core(core, mine, other, axis=0):
    return jnp.where(core == 0, jnp.stack([mine, other], axis), jnp.stack([other, mine], axis))


def scatter_dp(partial, n_dp):
    me = lax.axis_index("dp")
    if n_dp != 4:
        total = pick(partial, me).astype(f32)
        for mask in range(1, n_dp):
            total = total + swap(pick(partial, me ^ mask), "dp", n_dp, mask).astype(f32)
        return total.astype(bf16)
    half = partial.shape[-1] // 2
    far = pick(partial, me ^ 3)
    by_x = swap(far[..., :half], "dp", 4, 1)
    by_y = swap(far[..., half:], "dp", 4, 2)
    next_x, next_y = pick(partial, me ^ 1), pick(partial, me ^ 2)
    add = lambda a, b: (a.astype(f32) + b.astype(f32)).astype(bf16)
    next_x = jnp.concatenate([next_x[..., :half], add(next_x[..., half:], by_y)], -1)
    next_y = jnp.concatenate([add(next_y[..., :half], by_x), next_y[..., half:]], -1)
    got_x = swap(next_x, "dp", 4, 1)
    got_y = swap(next_y, "dp", 4, 2)
    return (pick(partial, me).astype(f32) + got_x.astype(f32) + got_y.astype(f32)).astype(bf16)


def scatter(partial, n_dp, n_z):
    rows, columns = partial.shape
    mine = scatter_dp(partial.reshape(n_dp, rows // n_dp, columns), n_dp)
    blocks = mine.reshape(n_z, rows // n_dp // n_z, columns)
    at = lax.axis_index("z")
    total = pick(blocks, at).astype(f32)
    for mask in range(1, n_z):
        total = total + swap(pick(blocks, at ^ mask), "z", n_z, mask).astype(f32)
    core = lax.axis_index("c")
    halves = total.reshape(2, rows // n_dp // n_z // 2, columns)
    return pick(halves, core), swap_core(pick(halves, 1 - core))


def shards(
    n_dp,
    n_z,
    tokens,
    segment_ids,
    expert_ids,
    ln1_gain,
    ln1_bias,
    qkv_weight,
    query_bias,
    value_bias,
    out_weight,
    out_bias,
    ln2_gain,
    ln2_bias,
    up_weight,
    up_bias,
    down_weight,
    down_bias,
    cotangent,
):
    rows, width = tokens.shape
    devices = n_dp * n_z * 2
    share = qkv_weight.shape[0]
    up_share = up_bias.shape[1]
    hidden = up_share * devices
    core = lax.axis_index("c")

    small = jnp.concatenate(
        [ln1_gain, ln1_bias, query_bias, value_bias, out_bias, ln2_gain, ln2_bias, up_bias.reshape(-1), down_bias.reshape(-1)]
    )
    used = small.shape[0]
    small = jnp.pad(small, (0, share * 128 - used)).reshape(share, 128)
    packed = lax.all_gather(jnp.concatenate([qkv_weight, out_weight, small], 1), ALL, axis=0, tiled=True)
    w_qkv = packed[:, : 3 * width]
    w_out = packed[:, 3 * width : 4 * width]
    small = packed[:, 4 * width :].reshape(devices, share * 128)[:, :used].astype(f32)
    gain_one, shift_one, bias_query, bias_value, bias_out, gain_two, shift_two = (
        small[:, i * share : (i + 1) * share].reshape(-1) for i in range(7)
    )
    bias_up = small[:, 7 * share : 7 * share + 2 * up_share].reshape(devices, 2, up_share)
    bias_up = pick(bias_up, core, 1).reshape(-1)
    bias_down = small[:, 7 * share + 2 * up_share :].reshape(devices, 2, share)
    bias_down = jnp.swapaxes(bias_down, 0, 1).reshape(2, width)

    def expert_shard(weight):
        mine, other = pick(weight, core, 1), swap_core(pick(weight, 1 - core, 1))
        both = by_core(core, mine, other)
        return both.reshape(2 * weight.shape[0], weight.shape[2])

    w_up = lax.all_gather(expert_shard(up_weight), ("dp", "z"), axis=0, tiled=True)
    w_down = lax.all_gather(expert_shard(down_weight), ("dp", "z"), axis=0, tiled=True)

    route = expert_ids[:, 0]
    place = lax.iota(jnp.int32, rows)
    before = (route[:, None] == route[None, :]) & (place[None, :] < place[:, None])
    slot = jnp.sum(before.astype(jnp.int32), 1) + jnp.where(route == core, 0, CAPACITY)
    chosen = (lax.iota(jnp.int32, 2 * CAPACITY)[:, None] == slot[None, :]).astype(bf16)

    def dispatch(values):
        slots = dot(chosen, values).astype(bf16)
        return jnp.concatenate([slots[:CAPACITY], swap_core(slots[CAPACITY:])], 0)

    def combine(slots):
        both = jnp.concatenate([slots[:CAPACITY], swap_core(slots[CAPACITY:])], 0)
        return dot(chosen, both, TN)

    expert_grad = dispatch(cotangent)

    inputs = tokens.astype(f32)
    normed_one = layer_norm(inputs, gain_one, shift_one).astype(bf16)
    other_normed_one = swap_core(normed_one)
    qkv_bias = jnp.concatenate([bias_query, jnp.zeros_like(bias_query), bias_value])
    qkv = (dot(normed_one, w_qkv) + qkv_bias).astype(bf16)
    seg_row, seg_col = segment_ids, segment_ids.reshape(rows, 1)
    attended, lse = attention(qkv, seg_col, seg_row)
    other_attended = swap_core(attended)
    middle = inputs + dot(attended, w_out) + bias_out
    normed_two = layer_norm(middle, gain_two, shift_two).astype(bf16)

    expert_input = dispatch(normed_two)
    inner = dot(expert_input, w_up) + bias_up
    root = 0.7978845608028654
    inner_sq = inner * inner
    bent = jnp.tanh(root * inner * (1.0 + 0.044715 * inner_sq))
    act = (0.5 * inner * (1.0 + bent)).astype(bf16)
    slope = 0.5 * (1.0 + bent) + 0.5 * inner * (1.0 - bent * bent) * (root * (1.0 + 3 * 0.044715 * inner_sq))
    act, slope = lax.optimization_barrier((act, slope.astype(bf16)))
    down_partial = dot(act, expert_grad, TN).astype(bf16)
    branch = combine(dot(act, w_down).astype(bf16))
    token_bias = jnp.where(route[:, None] == 0, bias_down[:1], bias_down[1:])
    block_out = (middle + branch + token_bias).astype(bf16)

    inner_grad = (dot(expert_grad, w_down, NT) * slope.astype(f32)).astype(bf16)
    up_partial = dot(expert_input, inner_grad, TN).astype(bf16)
    up_bias_grad = jnp.sum(inner_grad.astype(f32), 0)
    down_bias_grad = jnp.sum(expert_grad.astype(f32), 0)
    normed_two_grad = combine(dot(inner_grad, w_up, NT).astype(bf16))
    down_mine, down_other = scatter(down_partial, n_dp, n_z)
    up_mine, up_other = scatter(up_partial, n_dp, n_z)
    down_weight_grad = by_core(core, down_mine, down_other, 1)
    up_weight_grad = by_core(core, up_mine, up_other, 1)

    _, pull_two = jax.vjp(layer_norm, middle, gain_two, shift_two)
    middle_part, gain_two_grad, shift_two_grad = pull_two(normed_two_grad)
    middle_grad = cotangent.astype(f32) + middle_part

    projected_grad = middle_grad.astype(bf16)
    halves = projected_grad.reshape(rows, 2, width // 2)
    mine_projected = pick(halves, core, 1)
    other_projected = swap_core(pick(halves, 1 - core, 1))
    out_partial = (dot(attended, mine_projected, TN) + dot(other_attended, other_projected, TN)).astype(bf16)
    out_bias_grad = jnp.sum(projected_grad.astype(f32), 0)
    attended_grad = dot(projected_grad, w_out, NT).astype(bf16)
    out_mine, out_other = scatter(out_partial, n_dp, n_z)
    out_weight_grad = by_core(core, out_mine, out_other, 1).reshape(share, width)

    grad_away = attention_grad(qkv, attended_grad, lse, seg_col, seg_row, 1 - core)
    grad_other = swap_core(grad_away)
    grad_mine = attention_grad(qkv, attended_grad, lse, seg_col, seg_row, core)
    qkv_partial = jnp.concatenate(
        [(dot(normed_one, grad_mine[j], TN) + dot(other_normed_one, grad_other[j], TN)).astype(bf16) for j in range(3)], 1
    )
    qkv_mine, qkv_other = scatter(qkv_partial, n_dp, n_z)
    qkv_weight_grad = by_core(
        core, qkv_mine.reshape(share, 3, width // 2), qkv_other.reshape(share, 3, width // 2), 2
    ).reshape(share, 3 * width)

    qkv_grad = by_core(core, grad_mine, grad_away, 2).reshape(3, rows, width)
    qkv_grad = jnp.concatenate([qkv_grad[0], qkv_grad[1], qkv_grad[2]], 1)
    query_bias_grad = jnp.sum(qkv_grad[:, :width].astype(f32), 0)
    value_bias_grad = jnp.sum(qkv_grad[:, 2 * width :].astype(f32), 0)
    normed_one_grad = dot(qkv_grad, w_qkv, NT)
    _, pull_one = jax.vjp(layer_norm, inputs, gain_one, shift_one)
    input_part, gain_one_grad, shift_one_grad = pull_one(normed_one_grad)
    input_grad = middle_grad + input_part

    vectors = [
        gain_one_grad,
        shift_one_grad,
        query_bias_grad,
        value_bias_grad,
        out_bias_grad,
        gain_two_grad,
        shift_two_grad,
        up_bias_grad,
        down_bias_grad,
    ]
    sent = jnp.concatenate([v.reshape(devices, -1) for v in vectors], 1)
    got = lax.all_to_all(sent, ALL, 0, 0, tiled=True).reshape(devices // 2, 2, -1)
    both = jnp.sum(got, 0)
    total = both[0] + both[1]
    sums = [total[i * share : (i + 1) * share] for i in range(7)]
    at = 7 * share
    up_bias_sum = both[:, at : at + up_share]
    down_bias_sum = both[:, at + up_share :]
    return (
        block_out,
        input_grad,
        sums[0],
        sums[1],
        qkv_weight_grad,
        sums[2],
        sums[3],
        out_weight_grad,
        sums[4],
        sums[5],
        sums[6],
        up_weight_grad,
        up_bias_sum,
        down_weight_grad,
        down_bias_sum,
    )


def solution(mesh):
    n_dp, n_z = mesh.shape["dp"], mesh.shape["fsdp"] // 2
    split = Mesh(mesh.devices.reshape(n_dp, n_z, 2), ALL)
    row, flat, wide, cube = P(ALL, None), P(ALL), P(None, ALL), P(ALL, None, None)
    in_specs = (row, row, row, flat, flat, row, flat, flat, row, flat, flat, flat, cube, wide, cube, wide, row)
    out_specs = (row, row, flat, flat, row, flat, flat, row, flat, flat, flat, cube, wide, cube, wide)
    return jax.shard_map(
        functools.partial(shards, n_dp, n_z), mesh=split, in_specs=in_specs, out_specs=out_specs, check_vma=False
    )
```

time: 1830 us -> 778 us (0.43)
  waiting for transfers between devices: 880 us -> 319 us
  matrix products: 566 us -> 187 us
  blocking collectives: 162 us -> 0 us
  Pallas kernels: 0 us -> 73.9 us
  starting transfers between devices: 0.41 us -> 39.5 us
  local copies, waits for them, and re-layouts: 127 us -> 89.5 us
  other arithmetic: 68 us -> 48.5 us
    reduce_scatter x3 -> x0, waiting for transfers between devices: 660 us -> none  [the longest x1 361 us: shards(): lax.psum_scatter(down_grad, ('dp', 'fsdp'), scatter_dimension=0, tiled=True)]
    dot_general x24 -> x22, matrix products: 566 us -> 187 us  [dot(): return lax.dot_general(a, b, dims, preferred_element_type=f32)]
    ppermute x0 -> x42, waiting for transfers between devices: none -> 127 us  [swap(): return lax.ppermute(value, axis, [(i, i ^ mask) for i in range(size)])]
    unnamed x13 -> x3, waiting for transfers between devices: 119 us -> 0.05 us
    all_gather x4 -> x3, waiting for transfers between devices: 101 us -> 192 us  [the longest x1 84.3 us: shards(): lax.all_gather(expert_shard(down_weight), ('dp', 'z'), axis=0, tiled=True)]
    unnamed x2 -> x0, blocking collectives: 84 us -> none
    all_gather x2 -> x0, blocking collectives: 78.3 us -> none  [the longest x1 39.9 us: shards(): lax.all_gather(up_bias, ('dp', 'fsdp'), axis=1, tiled=True)]
    pallas_call x0 -> x3, Pallas kernels: none -> 73.9 us  [the longest x2 41.3 us: attention_grad(): pl.pallas_call(functools.partial(backward_kernel, blocks), out_shape=jax....]
  transfers between devices with their start and end apart: 10 -> 46, of which waited for: 6 -> 23; matrix products, arithmetic and copies ran while one was open for 41% -> 39% of each run, Pallas kernels for 0% -> 10%
where the time goes in v1:
time: 778 us; the launch traced here: 773 us
  waiting for transfers between devices  319 us (41%)
  matrix products  187 us (24%)
  local copies, waits for them, and re-layouts  89.5 us (12%)
  Pallas kernels  73.9 us (9%)
  other arithmetic  48.5 us (6%)
  starting transfers between devices  39.5 us (5%)
  between operations  15.4 us (2%)
    dot_general x22, matrix products, dot(): return lax.dot_general(a, b, dims, preferred_element_type=f32)  187 us
    ppermute x42, waiting for transfers between devices, swap(): return lax.ppermute(value, axis, [(i, i ^ mask) for i in range(size)])  127 us
    all_gather x1, waiting for transfers between devices, shards(): lax.all_gather(expert_shard(down_weight), ('dp', 'z'), axis=0, tiled=True)  84.3 us
    all_gather x1, waiting for transfers between devices, shards(): lax.all_gather(jnp.concatenate([qkv_weight, out_weight, small], 1), ALL,...  62 us
    all_gather x1, waiting for transfers between devices, shards(): lax.all_gather(expert_shard(up_weight), ('dp', 'z'), axis=0, tiled=True)  45.5 us
    pallas_call x2, Pallas kernels, attention_grad(): pl.pallas_call(functools.partial(backward_kernel, blocks), out_shape=jax....  41.3 us
    ppermute x42, starting transfers between devices, swap(): return lax.ppermute(value, axis, [(i, i ^ mask) for i in range(size)])  36.3 us
    unnamed x124, local copies, waits for them, and re-layouts  32.7 us
  transfers between devices with their start and end apart: 46, of which 23 were waited for; matrix products, arithmetic and copies ran while one was open for 39% of the time, Pallas kernels for 10%

profile of v1, /device:TPU:0, one launch (start us, length us, event | category | flops | bytes accessed | tf_op | source)
XLA Modules:
  0.0 772.5 jit_solution(10867067316079077706)
XLA Ops:
  8.0 5.4 concatenate.54
  24.9 3.3 fusion.30
  30.6 3.1 copy.90
  34.7 62.0 %all-gather.4.cloned.1.call-done = bf16[1024,4224]{1,0:T(8,128)(2,1)} async-done(((bf16[32,4224]{1,0:T(8,128)(2,1)}), bf16[1024,4224]{1,0:T(8,128)(2,1)}) %all-gather.4.cloned.1.call-update) | async-done | bytes 8650768 | tf_op jit(solution)/shard_map/all_gather | solution.py:254
  100.5 11.6 %add_convert_fusion.1.q_ref.k_ref.v_ref = bf16[1024,3072]{1,0:T(8,128)(2,1)} fusion(f32[3072]{0:T(1024)S(1)} %pad_maximum_fusion.16, bf16[1024,1024]{0,1:T(8,128)(2,1)S(1)} %fusion.19, bf16[1024,4224]{1,0:T(8,128)(2,1)} %all-gather.4.cloned.1.call-done), kind=kOutput, calls=%fused_computation.5 | convolution fusion | flops 6448742400 | bytes 14692352 | tf_op jit(solution)/shard_map/dot_general | solution.py:26
  112.1 32.6 %attention_forward.1 = (bf16[1024,1024]{1,0:T(8,128)(2,1)}, f32[8,2,1024]{2,1,0:T(2,128)S(1)}) custom-call(s32[1024,1]{1,0:T(8,128)S(1)} %copy.91.seg_col, s32[1,1024]{1,0:T(1,128)S(1)} %copy-done.4, bf16[1024,3072]{1,0:T(8,128)(2,1)} %add_convert_fusion.1.q_ref.k_ref.v_ref, bf16[1024,3072]{1,0:T(8,128)(2,1)} %add_convert_fusion.1.q_ref.k_ref.v_ref, ...), custom_call_target="tpu_custom_call" | custom-call | tf_op jit(solution)/shard_map/attention_forward/pallas_call | solution.py:74
  144.7 5.1 fusion.92
  151.4 3.7 fusion.29
  166.0 45.5 %all-gather.6.cloned.1.call-done = bf16[1024,4096]{1,0:T(8,128)(2,1)} async-done(((bf16[64,4096]{1,0:T(8,128)(2,1)}), bf16[1024,4096]{1,0:T(8,128)(2,1)}) %all-gather.6.cloned.1.call-update) | async-done | bytes 8388624 | tf_op jit(solution)/shard_map/all_gather | solution.py:271
  211.5 30.1 %add_convert_fusion = (bf16[1280,4096]{1,0:T(8,128)(2,1)}, bf16[1280,4096]{1,0:T(8,128)(2,1)}) fusion(f32[4096]{0:T(1024)S(1)} %bitcast.238, bf16[1024,4096]{1,0:T(8,128)(2,1)} %all-gather.6.cloned.1.call-done, bf16[640,1024]{1,0:T(8,128)(2,1)} %collective-permute-done, bf16[640,1024]{1,0:T(8,128)(2,1)} %get-tuple-element.116), kind=kOutput, calls=%fused_computation.2 | convolution fusion | flops 10847518720 | bytes 31997952 | tf_op jit(solution)/shard_map/dot_general | solution.py:26
  241.7 84.3 %all-gather.8.cloned.1.call-done = bf16[4096,1024]{1,0:T(8,128)(2,1)} async-done(((bf16[256,1024]{1,0:T(8,128)(2,1)}), bf16[4096,1024]{1,0:T(8,128)(2,1)}) %all-gather.8.cloned.1.call-update) | async-done | bytes 8388624 | tf_op jit(solution)/shard_map/all_gather | solution.py:272
  326.0 15.9 %convolution_convert_fusion.3 = bf16[1280,1024]{1,0:T(8,128)(2,1)S(1)} fusion(bf16[1280,4096]{1,0:T(8,128)(2,1)} %get-tuple-element.20, bf16[4096,1024]{1,0:T(8,128)(2,1)} %all-gather.8.cloned.1.call-done), kind=kOutput, calls=%fused_computation.60 | convolution fusion | flops 10738728960 | bytes 21495808 | tf_op jit(solution)/shard_map/dot_general | solution.py:26
  343.7 19.1 %convert_reduce_fusion = (f32[4096]{0:T(1024)S(1)}, bf16[1280,4096]{1,0:T(8,128)(2,1)}) fusion(bf16[1280,4096]{1,0:T(8,128)(2,1)} %get-tuple-element.21, bf16[4096,1024]{1,0:T(8,128)(2,1)} %all-gather.8.cloned.1.call-done, bf16[640,1024]{1,0:T(8,128)(2,1)} %collective-permute-done.4, bf16[640,1024]{1,0:T(8,128)(2,1)S(1)} %copy-done.21), kind=kOutput, calls=%fused_computation | convolution fusion | flops 10768871424 | bytes 31997952 | tf_op jit(solution)/shard_map/dot_general | solution.py:26
  362.8 16.0 %convolution_convert_fusion.2 = bf16[1280,1024]{1,0:T(8,128)(2,1)S(1)} fusion(bf16[1280,4096]{1,0:T(8,128)(2,1)} %get-tuple-element.173, bf16[1024,4096]{1,0:T(8,128)(2,1)} %all-gather.6.cloned.1.call-done), kind=kOutput, calls=%fused_computation.59 | convolution fusion | flops 10738728960 | bytes 21495808 | tf_op jit(solution)/shard_map/dot_general | solution.py:26
  380.2 14.5 %convolution_convert_fusion.1 = bf16[1024,4096]{1,0:T(8,128)(2,1)S(1)} fusion(bf16[1280,4096]{1,0:T(8,128)(2,1)} %get-tuple-element.173, bf16[640,1024]{1,0:T(8,128)(2,1)} %collective-permute-done, bf16[640,1024]{1,0:T(8,128)(2,1)S(1)} %copy-done.29), kind=kOutput, calls=%fused_computation.7 | convolution fusion | flops 10746855424 | bytes 21495808 | tf_op jit(solution)/shard_map/dot_general | solution.py:26
  400.8 14.7 %convolution_convert_fusion = bf16[4096,1024]{1,0:T(8,128)(2,1)S(1)} fusion(bf16[1280,4096]{1,0:T(8,128)(2,1)} %get-tuple-element.20, bf16[640,1024]{1,0:T(8,128)(2,1)} %collective-permute-done.4, bf16[640,1024]{1,0:T(8,128)(2,1)S(1)} %copy-done.21), kind=kOutput, calls=%fused_computation.6 | convolution fusion | flops 10746855424 | bytes 21495808 | tf_op jit(solution)/shard_map/dot_general | solution.py:26
  419.2 6.2 collective-permute-done.28
  428.3 12.9 %collective-permute-done.26 = bf16[256,2048]{1,0:T(8,128)(2,1)S(1)} collective-permute-done((bf16[256,2048]{1,0:T(8,128)(2,1)}, bf16[256,2048]{1,0:T(8,128)(2,1)S(1)}, u32[]{:S(2)}, u32[]{:S(2)}) %collective-permute-start.26) | collective-permute-done | bytes 1048608 | tf_op jit(solution)/shard_map/ppermute | solution.py:177
  443.8 6.4 collective-permute-done.36
  455.2 12.1 %collective-permute-done.34 = bf16[1024,512]{1,0:T(8,128)(2,1)S(1)} collective-permute-done((bf16[1024,512]{1,0:T(8,128)(2,1)S(1)}, bf16[1024,512]{1,0:T(8,128)(2,1)S(1)}, u32[]{:S(2)}, u32[]{:S(2)}) %collective-permute-start.34) | collective-permute-done | bytes 1048608 | tf_op jit(solution)/shard_map/ppermute | solution.py:177
  470.0 5.7 multiply_reduce_fusion
  478.9 4.9 convolution_convert_fusion.4.do_ref
  483.9 20.6 %attention_backward.3 = bf16[3,1024,512]{2,1,0:T(8,128)(2,1)S(1)} custom-call(s32[1]{0:T(128)} %bitcast.16.first, s32[1024,1]{1,0:T(8,128)S(1)} %copy-done.3, s32[1,1024]{1,0:T(1,128)S(1)} %copy-done.5, bf16[1024,3072]{1,0:T(8,128)(2,1)} %add_convert_fusion.1.q_ref.k_ref.v_ref, bf16[1024,3072]{1,0:T(8,128)(2,1)} %add_convert_fusion.1.q_ref.k_ref.v_ref, ...), custom_call_target="tpu_custom_call" | custom-call | tf_op jit(solution)/shard_map/attention_backward/pallas_call | solution.py:142
  504.5 20.6 %attention_backward.2 = bf16[3,1024,512]{2,1,0:T(8,128)(2,1)S(1)} custom-call(s32[1]{0:T(128)} %bitcast.14.first, s32[1024,1]{1,0:T(8,128)S(1)} %copy-done.3, s32[1,1024]{1,0:T(1,128)S(1)} %copy-done.5, bf16[1024,3072]{1,0:T(8,128)(2,1)} %add_convert_fusion.1.q_ref.k_ref.v_ref, bf16[1024,3072]{1,0:T(8,128)(2,1)} %add_convert_fusion.1.q_ref.k_ref.v_ref, ...), custom_call_target="tpu_custom_call" | custom-call | tf_op jit(solution)/shard_map/attention_backward/pallas_call | solution.py:142
  531.5 4.0 copy.102
  535.5 4.0 copy.101
  539.4 4.0 copy.100
  543.4 12.2 %fusion.93 = (f32[1024]{0:T(1024)S(1)}, f32[1024,1024]{1,0:T(8,128)}) fusion(bf16[1024,4224]{1,0:T(8,128)(2,1)} %all-gather.4.cloned.1.call-done, bf16[1024,1024]{0,1:T(8,128)(2,1)} %bitcast.212, bf16[1024,1024]{0,1:T(8,128)(2,1)} %bitcast.213, bf16[1024,1024]{0,1:T(8,128)(2,1)} %bitcast.214), kind=kOutput, calls=%fused_computation.231 | convolution fusion | flops 6462372864 | bytes 16781312 | tf_op jit(solution)/shard_map/dot_general | solution.py:26
  555.6 5.4 copy.103
  561.0 3.7 fusion.22
  576.7 7.8 %add_convert_fusion.2 = bf16[1024,1024]{0,1:T(8,128)(2,1)} fusion(f32[1024,1024]{0,1:T(8,128)} %copy-done.16, f32[1024]{0:T(1024)S(1)} %copy-done.50, f32[1024]{0:T(1024)S(1)} %copy-done.51, pred[1024]{0:T(1024)(128)(4,1)S(1)} %copy-done.52, bf16[640,1024]{1,0:T(8,128)(2,1)} %collective-permute-done.3, bf16[640,1024]{1,0:T(8,128)(2,1)} %get-tuple-element.114, ...), kind=kOutput, calls=%fused_computation.53 | convolution fusion | flops 2695102464 | bytes 8926208 | tf_op jit(solution)/shard_map/dot_general | solution.py:26
  584.6 3.0 fusion.60
  588.0 4.2 add_add_fusion.2
  592.2 3.0 add_convert_fusion.9
  603.0 3.2 collective-permute-done.18
  614.6 3.3 collective-permute-start.24
  620.6 3.9 copy.110
  624.5 5.5 copy.111
  631.4 4.3 collective-permute-done.23
  642.9 3.9 fusion.27
  649.4 3.1 collective-permute-start.30
  660.8 3.1 copy.115
  665.7 22.2 %collective-permute-done.37 = bf16[1024,1024]{1,0:T(8,128)(2,1)} collective-permute-done((bf16[1024,1024]{1,0:T(8,128)(2,1)}, bf16[1024,1024]{1,0:T(8,128)(2,1)}, u32[]{:S(2)}, u32[]{:S(2)}) %collective-permute-start.37) | collective-permute-done | bytes 2097184 | tf_op jit(solution)/shard_map/ppermute | solution.py:177
  690.2 4.3 fusion.25
  699.9 8.1 %collective-permute-done.8 = bf16[256,768]{1,0:T(8,128)(2,1)S(1)} collective-permute-done((bf16[256,768]{1,0:T(8,128)(2,1)S(1)}, bf16[256,768]{1,0:T(8,128)(2,1)S(1)}, u32[]{:S(2)}, u32[]{:S(2)}) %collective-permute-start.8) | collective-permute-done | bytes 393248 | tf_op jit(solution)/shard_map/ppermute | solution.py:177
  713.9 13.2 %collective-permute-done.11 = bf16[256,1536]{1,0:T(8,128)(2,1)S(1)} collective-permute-done((bf16[256,1536]{1,0:T(8,128)(2,1)S(1)}, bf16[256,1536]{1,0:T(8,128)(2,1)S(1)}, u32[]{:S(2)}, u32[]{:S(2)}) %collective-permute-start.11) | collective-permute-done | bytes 786464 | tf_op jit(solution)/shard_map/ppermute | solution.py:177
  733.0 17.8 %collective-permute-done.39 = bf16[256,1024]{1,0:T(8,128)(2,1)S(1)} collective-permute-done((bf16[256,1024]{1,0:T(8,128)(2,1)S(1)}, bf16[256,1024]{1,0:T(8,128)(2,1)S(1)}, u32[]{:S(2)}, u32[]{:S(2)}) %collective-permute-start.39) | collective-permute-done | bytes 524320 | tf_op jit(solution)/shard_map/ppermute | solution.py:177
  751.3 6.7 collective-permute-done.13
  (334 shorter events, 146.9 us)
Async XLA Ops:
  7.2 89.5 %all-gather.4.cloned.1.call-start = ((), (), s32[]{:S(2)}) async-start(), calls=%async_computation.1 | async-start | bytes 8921088 | tf_op jit(solution)/shard_map/all_gather | solution.py:254
  15.2 196.4 %all-gather.6.cloned.1.call-start = ((), (), s32[]{:S(2)}) async-start(), calls=%async_computation.2 | async-start | bytes 8912896 | tf_op jit(solution)/shard_map/all_gather | solution.py:271
  18.0 1.7 collective-permute-start.1
  20.6 305.3 %all-gather.8.cloned.1.call-start = ((), (), s32[]{:S(2)}) async-start(), calls=%async_computation.3 | async-start | bytes 8912896 | tf_op jit(solution)/shard_map/all_gather | solution.py:272
  21.9 1.6 collective-permute-start.2
  24.9 125.5 %copy-start.48 = (s32[1024]{0:T(1024)}, s32[1024]{0:T(1024)S(1)}, u32[]{:S(2)}) copy-start(s32[1024]{0:T(1024)S(1)} %select_add_fusion) | copy-start | bytes 12292
  30.0 131.7 %collective-permute-start.4 = (bf16[640,1024]{1,0:T(8,128)(2,1)}, bf16[640,1024]{1,0:T(8,128)(2,1)}, u32[]{:S(2)}, u32[]{:S(2)}) collective-permute-start(bf16[640,1024]{1,0:T(8,128)(2,1)} %get-tuple-element.113), channel_id=1, source_target_pairs={{0,1},{1,0},{2,3},{3,2},{4,5},{5,4},{6,7},{7,6},{8,9},{9,8},{10,11... | collective-permute-start | bytes 3932168 | tf_op jit(solution)/shard_map/ppermute | solution.py:177
  33.6 111.1 %copy-start.6 = (bf16[1024,1024]{0,1:T(8,128)(2,1)}, bf16[1024,1024]{0,1:T(8,128)(2,1)S(1)}, u32[]{:S(2)}) copy-start(bf16[1024,1024]{0,1:T(8,128)(2,1)S(1)} %copy.90) | copy-start | bytes 6291460
  157.0 54.6 %collective-permute-start = (bf16[640,1024]{1,0:T(8,128)(2,1)}, bf16[640,1024]{1,0:T(8,128)(2,1)}, u32[]{:S(2)}, u32[]{:S(2)}) collective-permute-start(bf16[640,1024]{1,0:T(8,128)(2,1)} %get-tuple-element.117), channel_id=1, source_target_pairs={{0,1},{1,0},{2,3},{3,2},{4,5},{5,4},{6,7},{7,6},{8,9},{9,8},{10,11... | collective-permute-start | bytes 3932168 | tf_op jit(solution)/shard_map/ppermute | solution.py:177
  164.2 428.0 %collective-permute-start.16 = (bf16[1024,1024]{1,0:T(8,128)(2,1)}, bf16[1024,1024]{1,0:T(8,128)(2,1)}, u32[]{:S(2)}, u32[]{:S(2)}) collective-permute-start(bf16[1024,1024]{1,0:T(8,128)(2,1)} %get-tuple-element.19), channel_id=1, source_target_pairs={{0,1},{1,0},{2,3},{3,2},{4,5},{5,4},{6,7},{7,6},{8,9},{9,8},{10,11... | collective-permute-start | bytes 6291464 | tf_op jit(solution)/shard_map/ppermute | solution.py:177
  343.7 233.0 %collective-permute-start.3 = (bf16[640,1024]{1,0:T(8,128)(2,1)}, bf16[640,1024]{1,0:T(8,128)(2,1)}, u32[]{:S(2)}, u32[]{:S(2)}) collective-permute-start(bf16[640,1024]{1,0:T(8,128)(2,1)} %get-tuple-element.115), channel_id=1, source_target_pairs={{0,1},{1,0},{2,3},{3,2},{4,5},{5,4},{6,7},{7,6},{8,9},{9,8},{10,11... | collective-permute-start | bytes 3932168 | tf_op jit(solution)/shard_map/ppermute | solution.py:177
  379.2 90.8 %collective-permute-start.5 = (bf16[640,1024]{1,0:T(8,128)(2,1)S(1)}, bf16[640,1024]{1,0:T(8,128)(2,1)}, u32[]{:S(2)}, u32[]{:S(2)}) collective-permute-start(bf16[640,1024]{1,0:T(8,128)(2,1)S(1)} %get-tuple-element.111), channel_id=1, source_target_pairs={{0,1},{1,0},{2,3},{3,2},{4,5},{5,4},{6,7},{7,6},{8,9},{9,8},{10,11... | collective-permute-start | bytes 3932168 | tf_op jit(solution)/shard_map/ppermute | solution.py:177
  399.5 25.9 %collective-permute-start.28 = (bf16[256,2048]{1,0:T(8,128)(2,1)}, bf16[256,2048]{1,0:T(8,128)(2,1)}, u32[]{:S(2)}, u32[]{:S(2)}) collective-permute-start(bf16[256,2048]{1,0:T(8,128)(2,1)} %get-tuple-element.127), channel_id=1, source_target_pairs={{0,8},{8,0},{16,24},{24,16},{1,9},{9,1},{17,25},{25,17},{2,10},{10... | collective-permute-start | bytes 3145736 | tf_op jit(solution)/shard_map/ppermute | solution.py:177
  415.6 25.5 %collective-permute-start.26 = (bf16[256,2048]{1,0:T(8,128)(2,1)}, bf16[256,2048]{1,0:T(8,128)(2,1)S(1)}, u32[]{:S(2)}, u32[]{:S(2)}) collective-permute-start(bf16[256,2048]{1,0:T(8,128)(2,1)} %get-tuple-element.126), channel_id=1, source_target_pairs={{0,16},{8,24},{16,0},{24,8},{1,17},{9,25},{17,1},{25,9},{2,18},{10... | collective-permute-start | bytes 3145736 | tf_op jit(solution)/shard_map/ppermute | solution.py:177
  425.4 24.8 %collective-permute-start.36 = (bf16[1024,512]{1,0:T(8,128)(2,1)S(1)}, bf16[1024,512]{1,0:T(8,128)(2,1)S(1)}, u32[]{:S(2)}, u32[]{:S(2)}) collective-permute-start(bf16[1024,512]{1,0:T(8,128)(2,1)S(1)} %get-tuple-element.122), channel_id=1, source_target_pairs={{0,8},{8,0},{16,24},{24,16},{1,9},{9,1},{17,25},{25,17},{2,10},{10... | collective-permute-start | bytes 3145736 | tf_op jit(solution)/shard_map/ppermute | solution.py:177
  441.2 26.1 %collective-permute-start.34 = (bf16[1024,512]{1,0:T(8,128)(2,1)S(1)}, bf16[1024,512]{1,0:T(8,128)(2,1)S(1)}, u32[]{:S(2)}, u32[]{:S(2)}) collective-permute-start(bf16[1024,512]{1,0:T(8,128)(2,1)S(1)} %get-tuple-element.121), channel_id=1, source_target_pairs={{0,16},{8,24},{16,0},{24,8},{1,17},{9,25},{17,1},{25,9},{2,18},{10... | collective-permute-start | bytes 3145736 | tf_op jit(solution)/shard_map/ppermute | solution.py:177
  450.2 192.2 %collective-permute-start.29 = (bf16[256,4096]{1,0:T(8,128)(2,1)}, bf16[256,4096]{1,0:T(8,128)(2,1)}, u32[]{:S(2)}, u32[]{:S(2)}) collective-permute-start(bf16[256,4096]{1,0:T(8,128)(2,1)} %pad_maximum_fusion.4), channel_id=1, source_target_pairs={{0,16},{8,24},{16,0},{24,8},{1,17},{9,25},{17,1},{25,9},{2,18},{10... | collective-permute-start | bytes 6291464 | tf_op jit(solution)/shard_map/ppermute | solution.py:177
  467.3 175.7 %collective-permute-start.27 = (bf16[256,4096]{1,0:T(8,128)(2,1)}, bf16[256,4096]{1,0:T(8,128)(2,1)}, u32[]{:S(2)}, u32[]{:S(2)}) collective-permute-start(bf16[256,4096]{1,0:T(8,128)(2,1)} %pad_maximum_fusion.3), channel_id=1, source_target_pairs={{0,8},{8,0},{16,24},{24,16},{1,9},{9,1},{17,25},{25,17},{2,10},{10... | collective-permute-start | bytes 6291464 | tf_op jit(solution)/shard_map/ppermute | solution.py:177
  571.9 58.1 %all-to-all-start = ((f32[32,1,384]{2,1,0:T(1,128)}), f32[32,1,384]{2,1,0:T(1,128)S(1)}, u32[]{:S(2)}, u32[]{:S(2)}) async-start(f32[32,1,384]{2,1,0:T(1,128)} %all_to_all.6), calls=%async_computation | async-start | bytes 98304 | tf_op jit(solution)/shard_map/all_to_all | solution.py:370
  576.3 16.0 %collective-permute-start.17 = (bf16[1024,512]{0,1:T(8,128)(2,1)S(1)}, bf16[1024,512]{0,1:T(8,128)(2,1)S(1)}, u32[]{:S(2)}, u32[]{:S(2)}) collective-permute-start(bf16[1024,512]{0,1:T(8,128)(2,1)S(1)} %dynamic-slice_bitcast_fusion.6), channel_id=1, source_target_pairs={{0,1},{1,0},{2,3},{3,2},{4,5},{5,4},{6,7},{7,6},{8,9},{9,8},{10,11... | collective-permute-start | bytes 3145736 | tf_op jit(solution)/shard_map/ppermute | solution.py:177
  595.4 6.0 collective-permute-start.20
  599.8 49.6 %collective-permute-start.7 = (bf16[3,1024,512]{2,1,0:T(8,128)(2,1)S(1)}, bf16[3,1024,512]{2,1,0:T(8,128)(2,1)}, u32[]{:S(2)}, u32[]{:S(2)}) collective-permute-start(bf16[3,1024,512]{2,1,0:T(8,128)(2,1)S(1)} %attention_backward.3), channel_id=1, source_target_pairs={{0,1},{1,0},{2,3},{3,2},{4,5},{5,4},{6,7},{7,6},{8,9},{9,8},{10,11... | collective-permute-start | bytes 9437192 | tf_op jit(solution)/shard_map/ppermute | solution.py:177
  599.9 6.4 collective-permute-start.18
  601.5 9.9 %collective-permute-start.21 = (bf16[256,512]{1,0:T(8,128)(2,1)S(1)}, bf16[256,512]{1,0:T(8,128)(2,1)S(1)}, u32[]{:S(2)}, u32[]{:S(2)}) collective-permute-start(bf16[256,512]{1,0:T(8,128)(2,1)S(1)} %pad_maximum_fusion.15), channel_id=1, source_target_pairs={{0,16},{8,24},{16,0},{24,8},{1,17},{9,25},{17,1},{25,9},{2,18},{10... | collective-permute-start | bytes 786440 | tf_op jit(solution)/shard_map/ppermute | solution.py:177
  606.3 7.5 collective-permute-start.19
  614.6 15.7 %collective-permute-start.24 = (bf16[64,512]{1,0:T(8,128)(2,1)}, bf16[64,512]{1,0:T(8,128)(2,1)}, u32[]{:S(2)}, u32[]{:S(2)}) collective-permute-start(bf16[64,512]{1,0:T(8,128)(2,1)} %get-tuple-element.147), channel_id=1, source_target_pairs={{0,6},{2,4},{4,2},{6,0},{1,7},{3,5},{5,3},{7,1},{8,14},{10,12},{12... | collective-permute-start | bytes 196616 | tf_op jit(solution)/shard_map/ppermute | solution.py:177
  630.2 5.4 collective-permute-start.23
  630.3 5.4 collective-permute-start.22
  635.7 13.7 %collective-permute-start.6 = (bf16[1024,1024]{0,1:T(8,128)(2,1)}, bf16[1024,1024]{0,1:T(8,128)(2,1)S(1)}, u32[]{:S(2)}, u32[]{:S(2)}) collective-permute-start(bf16[1024,1024]{0,1:T(8,128)(2,1)} %copy-done.26), channel_id=1, source_target_pairs={{0,1},{1,0},{2,3},{3,2},{4,5},{5,4},{6,7},{7,6},{8,9},{9,8},{10,11... | collective-permute-start | bytes 6291464 | tf_op jit(solution)/shard_map/ppermute | solution.py:177
  636.6 3.3 collective-permute-start.25
  639.9 48.0 %collective-permute-start.37 = (bf16[1024,1024]{1,0:T(8,128)(2,1)}, bf16[1024,1024]{1,0:T(8,128)(2,1)}, u32[]{:S(2)}, u32[]{:S(2)}) collective-permute-start(bf16[1024,1024]{1,0:T(8,128)(2,1)} %pad_maximum_fusion.6), channel_id=1, source_target_pairs={{0,16},{8,24},{16,0},{24,8},{1,17},{9,25},{17,1},{25,9},{2,18},{10... | collective-permute-start | bytes 6291464 | tf_op jit(solution)/shard_map/ppermute | solution.py:177
  642.4 47.8 %collective-permute-start.35 = (bf16[1024,1024]{1,0:T(8,128)(2,1)}, bf16[1024,1024]{1,0:T(8,128)(2,1)}, u32[]{:S(2)}, u32[]{:S(2)}) collective-permute-start(bf16[1024,1024]{1,0:T(8,128)(2,1)} %pad_maximum_fusion.5), channel_id=1, source_target_pairs={{0,8},{8,0},{16,24},{24,16},{1,9},{9,1},{17,25},{25,17},{2,10},{10... | collective-permute-start | bytes 6291464 | tf_op jit(solution)/shard_map/ppermute | solution.py:177
  648.1 61.7 %collective-permute-start.32 = (bf16[64,4096]{1,0:T(8,128)(2,1)}, bf16[64,4096]{1,0:T(8,128)(2,1)}, u32[]{:S(2)}, u32[]{:S(2)}) collective-permute-start(bf16[64,4096]{1,0:T(8,128)(2,1)} %get-tuple-element.124), channel_id=1, source_target_pairs={{0,6},{2,4},{4,2},{6,0},{1,7},{3,5},{5,3},{7,1},{8,14},{10,12},{12... | collective-permute-start | bytes 1572872 | tf_op jit(solution)/shard_map/ppermute | solution.py:177
  649.3 60.6 %collective-permute-start.31 = (bf16[64,4096]{1,0:T(8,128)(2,1)}, bf16[64,4096]{1,0:T(8,128)(2,1)}, u32[]{:S(2)}, u32[]{:S(2)}) collective-permute-start(bf16[64,4096]{1,0:T(8,128)(2,1)} %get-tuple-element.125), channel_id=1, source_target_pairs={{0,4},{2,6},{4,0},{6,2},{1,5},{3,7},{5,1},{7,3},{8,12},{10,14},{12... | collective-permute-start | bytes 1572872 | tf_op jit(solution)/shard_map/ppermute | solution.py:177
  649.4 62.1 %collective-permute-start.30 = (bf16[64,4096]{1,0:T(8,128)(2,1)}, bf16[64,4096]{1,0:T(8,128)(2,1)}, u32[]{:S(2)}, u32[]{:S(2)}) collective-permute-start(bf16[64,4096]{1,0:T(8,128)(2,1)} %get-tuple-element.123), channel_id=1, source_target_pairs={{0,2},{2,0},{4,6},{6,4},{1,3},{3,1},{5,7},{7,5},{8,10},{10,8},{12,... | collective-permute-start | bytes 1572872 | tf_op jit(solution)/shard_map/ppermute | solution.py:177
  687.9 10.5 %collective-permute-start.10 = (bf16[256,768]{1,0:T(8,128)(2,1)S(1)}, bf16[256,768]{1,0:T(8,128)(2,1)S(1)}, u32[]{:S(2)}, u32[]{:S(2)}) collective-permute-start(bf16[256,768]{1,0:T(8,128)(2,1)S(1)} %get-tuple-element.139), channel_id=1, source_target_pairs={{0,8},{8,0},{16,24},{24,16},{1,9},{9,1},{17,25},{25,17},{2,10},{10... | collective-permute-start | bytes 1179656 | tf_op jit(solution)/shard_map/ppermute | solution.py:177
  694.7 36.8 %collective-permute-start.40 = (bf16[256,1024]{1,0:T(8,128)(2,1)S(1)}, bf16[256,1024]{1,0:T(8,128)(2,1)S(1)}, u32[]{:S(2)}, u32[]{:S(2)}) collective-permute-start(bf16[256,1024]{1,0:T(8,128)(2,1)S(1)} %get-tuple-element.119), channel_id=1, source_target_pairs={{0,6},{2,4},{4,2},{6,0},{1,7},{3,5},{5,3},{7,1},{8,14},{10,12},{12... | collective-permute-start | bytes 1572872 | tf_op jit(solution)/shard_map/ppermute | solution.py:177
  698.4 9.6 %collective-permute-start.8 = (bf16[256,768]{1,0:T(8,128)(2,1)S(1)}, bf16[256,768]{1,0:T(8,128)(2,1)S(1)}, u32[]{:S(2)}, u32[]{:S(2)}) collective-permute-start(bf16[256,768]{1,0:T(8,128)(2,1)S(1)} %get-tuple-element.138), channel_id=1, source_target_pairs={{0,16},{8,24},{16,0},{24,8},{1,17},{9,25},{17,1},{25,9},{2,18},{10... | collective-permute-start | bytes 1179656 | tf_op jit(solution)/shard_map/ppermute | solution.py:177
  708.0 42.7 %collective-permute-start.39 = (bf16[256,1024]{1,0:T(8,128)(2,1)S(1)}, bf16[256,1024]{1,0:T(8,128)(2,1)S(1)}, u32[]{:S(2)}, u32[]{:S(2)}) collective-permute-start(bf16[256,1024]{1,0:T(8,128)(2,1)S(1)} %get-tuple-element.120), channel_id=1, source_target_pairs={{0,4},{2,6},{4,0},{6,2},{1,5},{3,7},{5,1},{7,3},{8,12},{10,14},{12... | collective-permute-start | bytes 1572872 | tf_op jit(solution)/shard_map/ppermute | solution.py:177
  709.8 40.9 %collective-permute-start.38 = (bf16[256,1024]{1,0:T(8,128)(2,1)S(1)}, bf16[256,1024]{1,0:T(8,128)(2,1)S(1)}, u32[]{:S(2)}, u32[]{:S(2)}) collective-permute-start(bf16[256,1024]{1,0:T(8,128)(2,1)S(1)} %get-tuple-element.118), channel_id=1, source_target_pairs={{0,2},{2,0},{4,6},{6,4},{1,3},{3,1},{5,7},{7,5},{8,10},{10,8},{12,... | collective-permute-start | bytes 1572872 | tf_op jit(solution)/shard_map/ppermute | solution.py:177
  710.0 17.0 %collective-permute-start.11 = (bf16[256,1536]{1,0:T(8,128)(2,1)S(1)}, bf16[256,1536]{1,0:T(8,128)(2,1)S(1)}, u32[]{:S(2)}, u32[]{:S(2)}) collective-permute-start(bf16[256,1536]{1,0:T(8,128)(2,1)S(1)} %pad_maximum_fusion.10), channel_id=1, source_target_pairs={{0,16},{8,24},{16,0},{24,8},{1,17},{9,25},{17,1},{25,9},{2,18},{10... | collective-permute-start | bytes 2359304 | tf_op jit(solution)/shard_map/ppermute | solution.py:177
  711.5 16.8 %collective-permute-start.9 = (bf16[256,1536]{1,0:T(8,128)(2,1)S(1)}, bf16[256,1536]{1,0:T(8,128)(2,1)S(1)}, u32[]{:S(2)}, u32[]{:S(2)}) collective-permute-start(bf16[256,1536]{1,0:T(8,128)(2,1)S(1)} %pad_maximum_fusion.9), channel_id=1, source_target_pairs={{0,8},{8,0},{16,24},{24,16},{1,9},{9,1},{17,25},{25,17},{2,10},{10... | collective-permute-start | bytes 2359304 | tf_op jit(solution)/shard_map/ppermute | solution.py:177
  727.0 32.8 %collective-permute-start.33 = (f32[32,4096]{1,0:T(8,128)S(1)}, f32[32,4096]{1,0:T(8,128)S(1)}, u32[]{:S(2)}, u32[]{:S(2)}) collective-permute-start(f32[32,4096]{1,0:T(8,128)S(1)} %get-tuple-element.131), channel_id=1, source_target_pairs={{0,1},{1,0},{2,3},{3,2},{4,5},{5,4},{6,7},{7,6},{8,9},{9,8},{10,11... | collective-permute-start | bytes 1572872 | tf_op jit(solution)/shard_map/ppermute | solution.py:177
  729.8 21.5 %collective-permute-start.14 = (bf16[64,1536]{1,0:T(8,128)(2,1)S(1)}, bf16[64,1536]{1,0:T(8,128)(2,1)S(1)}, u32[]{:S(2)}, u32[]{:S(2)}) collective-permute-start(bf16[64,1536]{1,0:T(8,128)(2,1)S(1)} %get-tuple-element.136), channel_id=1, source_target_pairs={{0,6},{2,4},{4,2},{6,0},{1,7},{3,5},{5,3},{7,1},{8,14},{10,12},{12... | collective-permute-start | bytes 589832 | tf_op jit(solution)/shard_map/ppermute | solution.py:177
  731.4 26.5 %collective-permute-start.13 = (bf16[64,1536]{1,0:T(8,128)(2,1)S(1)}, bf16[64,1536]{1,0:T(8,128)(2,1)S(1)}, u32[]{:S(2)}, u32[]{:S(2)}) collective-permute-start(bf16[64,1536]{1,0:T(8,128)(2,1)S(1)} %get-tuple-element.137), channel_id=1, source_target_pairs={{0,4},{2,6},{4,0},{6,2},{1,5},{3,7},{5,1},{7,3},{8,12},{10,14},{12... | collective-permute-start | bytes 589832 | tf_op jit(solution)/shard_map/ppermute | solution.py:177
  750.7 8.9 %collective-permute-start.12 = (bf16[64,1536]{1,0:T(8,128)(2,1)S(1)}, bf16[64,1536]{1,0:T(8,128)(2,1)S(1)}, u32[]{:S(2)}, u32[]{:S(2)}) collective-permute-start(bf16[64,1536]{1,0:T(8,128)(2,1)S(1)} %get-tuple-element.135), channel_id=1, source_target_pairs={{0,2},{2,0},{4,6},{6,4},{1,3},{3,1},{5,7},{7,5},{8,10},{10,8},{12,... | collective-permute-start | bytes 589832 | tf_op jit(solution)/shard_map/ppermute | solution.py:177
  751.2 10.5 %collective-permute-start.41 = (f32[128,1024]{1,0:T(8,128)S(1)}, f32[128,1024]{1,0:T(8,128)S(1)}, u32[]{:S(2)}, u32[]{:S(2)}) collective-permute-start(f32[128,1024]{1,0:T(8,128)S(1)} %get-tuple-element.129), channel_id=1, source_target_pairs={{0,1},{1,0},{2,3},{3,2},{4,5},{5,4},{6,7},{7,6},{8,9},{9,8},{10,11... | collective-permute-start | bytes 1572872 | tf_op jit(solution)/shard_map/ppermute | solution.py:177
  759.8 4.1 collective-permute-start.15
  (54 other events, 615.6 us)
Sparse Core Ops, SparseCore 0:
  15.3 81.3 all-gather.3
  100.0 111.4 all-gather.5
  214.9 111.0 all-gather.7

commit v2 on v1

v2 whole, which is shorter than its diff:
```python
import functools

import jax
import jax.numpy as jnp
from jax import lax
from jax.experimental import pallas as pl
from jax.experimental.pallas import tpu as pltpu
from jax.sharding import Mesh, PartitionSpec as P

HEAD_DIM = 64
CAPACITY = 640
LONGEST = 512
PAIR = 2 * HEAD_DIM
TILE_Q = 256
MASKED = -1e30
epsilon = 1e-05
bf16 = jnp.bfloat16
f32 = jnp.float32
ALL = ("dp", "z", "c")
BLOCK = 256
FBLOCK = 512
NN = (((1,), (0,)), ((), ()))
NT = (((1,), (1,)), ((), ()))
TN = (((0,), (0,)), ((), ()))


def dot(a, b, dims=NN):
    return lax.dot_general(a, b, dims, preferred_element_type=f32)


def params(flops, moved, special=0):
    return dict(
        compiler_params=pltpu.CompilerParams(vmem_limit_bytes=58 << 20),
        cost_estimate=pl.CostEstimate(flops=2 * int(flops), bytes_accessed=int(moved), transcendentals=int(special)),
    )


def launch(kernel, name, grid, args, in_specs, out_specs, out_shape, scratch=(), scalars=(), after=(), work=(0, 0)):
    first, last = len(scalars) + len(args), len(scalars) + len(args) + len(after)

    def body(*refs):
        kernel(*refs[:first], *refs[last:])

    return pl.pallas_call(
        body,
        grid_spec=pltpu.PrefetchScalarGridSpec(
            num_scalar_prefetch=len(scalars),
            grid=grid,
            in_specs=[*in_specs, *[pl.BlockSpec(memory_space=pl.ANY)] * len(after)],
            out_specs=out_specs,
            scratch_shapes=list(scratch),
        ),
        out_shape=out_shape,
        **params(*work),
        name=name,
    )(*scalars, *args, *after)


def whole(*shape):
    return pl.BlockSpec(shape, lambda *_: (0,) * len(shape))


def shape_of(shape, dtype):
    return jax.ShapeDtypeStruct(shape, dtype)


def spans(rows):
    out = []
    for start in range(0, rows, TILE_Q):
        low = max(0, (start - LONGEST + 1) // TILE_Q * TILE_Q)
        out.append((start, low, start + TILE_Q))
    return out


def fill_bias(bias_refs, seg_col, seg_row, blocks):
    for bias, (start, low, high) in zip(bias_refs, blocks):
        shape = (high - low, TILE_Q)
        key = low + lax.broadcasted_iota(jnp.int32, shape, 0)
        query = start + lax.broadcasted_iota(jnp.int32, shape, 1)
        same = seg_col[low:high, :] == seg_row[:, start : start + TILE_Q]
        bias[...] = jnp.where((key <= query) & same, 0.0, MASKED)


def forward_kernel(blocks, seg_col, seg_row, q_ref, k_ref, v_ref, o_ref, lse_ref, *bias):
    @pl.when(pl.program_id(0) == 0)
    def _():
        fill_bias(bias, seg_col, seg_row, blocks)

    lane = lax.broadcasted_iota(jnp.int32, (TILE_Q, PAIR), 1)
    for masked, (start, low, high) in zip(bias, blocks):
        rows = slice(start, start + TILE_Q)
        q = q_ref[rows, :] * jnp.asarray(HEAD_DIM**-0.5, bf16)
        k = k_ref[low:high, :]
        v = v_ref[low:high, :]
        heads = []
        for head in range(2):
            mine = (lane < HEAD_DIM) == (head == 0)
            scores = dot(k, jnp.where(mine, q, jnp.zeros_like(q)), NT) + masked[...]
            top = jnp.max(scores, 0, keepdims=True)
            probs = jnp.exp(scores - top)
            total = jnp.sum(probs, 0, keepdims=True)
            out = dot(v, probs.astype(bf16), TN)
            heads.append(out[head * HEAD_DIM : (head + 1) * HEAD_DIM] * (1.0 / total))
            lse_ref[0, head : head + 1, rows] = top + jnp.log(total)
        o_ref[rows, :] = jnp.concatenate(heads, 0).T.astype(bf16)


def attention(qkv, seg_col, seg_row, after=()):
    rows, width = qkv.shape[0], qkv.shape[1] // 3
    pairs = width // PAIR
    blocks = spans(rows)
    return launch(
        functools.partial(forward_kernel, blocks),
        "attention_forward",
        (pairs,),
        (seg_col, seg_row, qkv, qkv, qkv),
        [
            whole(rows, 1),
            whole(1, rows),
            pl.BlockSpec((rows, PAIR), lambda p: (0, p)),
            pl.BlockSpec((rows, PAIR), lambda p: (0, pairs + p)),
            pl.BlockSpec((rows, PAIR), lambda p: (0, 2 * pairs + p)),
        ],
        (pl.BlockSpec((rows, PAIR), lambda p: (0, p)), pl.BlockSpec((1, 2, rows), lambda p: (p, 0, 0))),
        (shape_of((rows, width), bf16), shape_of((pairs, 2, rows), f32)),
        [pltpu.VMEM((high - low, TILE_Q), f32) for _, low, high in blocks],
        after=after,
        work=(16 * rows * rows * width, 8 * rows * width),
    )


def backward_kernel(
    blocks, first, seg_col, seg_row, q_ref, k_ref, v_ref, do_ref, lse_ref, d_ref, dk_sum, dv_sum, *bias
):
    @pl.when(pl.program_id(0) == 0)
    def _():
        fill_bias(bias, seg_col, seg_row, blocks)

    dk_sum[...] = jnp.zeros_like(dk_sum)
    dv_sum[...] = jnp.zeros_like(dv_sum)
    lane = lax.broadcasted_iota(jnp.int32, (TILE_Q, PAIR), 1)
    scale = HEAD_DIM**-0.5
    for masked, (start, low, high) in zip(bias, blocks):
        rows = slice(start, start + TILE_Q)
        q = q_ref[rows, :]
        do = do_ref[rows, :]
        k = k_ref[low:high, :]
        v = v_ref[low:high, :]
        scaled = q * jnp.asarray(scale, bf16)
        zero = jnp.zeros_like(q)
        dq, dk, dv = [], 0.0, 0.0
        for head in range(2):
            mine = (lane < HEAD_DIM) == (head == 0)
            do_head = jnp.where(mine, do, zero)
            scores = dot(k, jnp.where(mine, scaled, zero), NT) + masked[...]
            probs = jnp.exp(scores - lse_ref[0, head : head + 1, rows])
            weighted = probs * dot(v, do_head, NT)
            total = jnp.sum(weighted, 0, keepdims=True)
            ds = ((weighted - probs * total) * scale).astype(bf16)
            dv = dv + dot(probs.astype(bf16), do_head)
            dk = dk + dot(ds, jnp.where(mine, q, zero))
            dq.append(dot(k, ds, TN)[head * HEAD_DIM : (head + 1) * HEAD_DIM])
        d_ref[0, rows, :] = jnp.concatenate(dq, 0).T.astype(bf16)
        dk_sum[low:high, :] += dk
        dv_sum[low:high, :] += dv
    d_ref[1, ...] = dk_sum[...].astype(bf16)
    d_ref[2, ...] = dv_sum[...].astype(bf16)


def attention_grad(qkv, do, lse, seg_col, seg_row, half, after=()):
    rows, width = qkv.shape[0], qkv.shape[1] // 3
    pairs = width // PAIR
    count = pairs // 2
    blocks = spans(rows)
    first = jnp.reshape(half * count, (1,)).astype(jnp.int32)
    return launch(
        functools.partial(backward_kernel, blocks),
        "attention_backward",
        (count,),
        (seg_col, seg_row, qkv, qkv, qkv, do, lse),
        [
            whole(rows, 1),
            whole(1, rows),
            pl.BlockSpec((rows, PAIR), lambda p, b: (0, b[0] + p)),
            pl.BlockSpec((rows, PAIR), lambda p, b: (0, pairs + b[0] + p)),
            pl.BlockSpec((rows, PAIR), lambda p, b: (0, 2 * pairs + b[0] + p)),
            pl.BlockSpec((rows, PAIR), lambda p, b: (0, b[0] + p)),
            pl.BlockSpec((1, 2, rows), lambda p, b: (b[0] + p, 0, 0)),
        ],
        pl.BlockSpec((3, rows, PAIR), lambda p, b: (0, 0, p)),
        shape_of((3, rows, count * PAIR), bf16),
        [pltpu.VMEM((rows, PAIR), f32)] * 2 + [pltpu.VMEM((high - low, TILE_Q), f32) for _, low, high in blocks],
        scalars=(first,),
        after=after,
        work=(12 * rows * rows * width, 8 * rows * width),
    )


def norm_parts(values):
    centre = values - jnp.mean(values, -1, keepdims=True)
    inverse = lax.rsqrt(jnp.mean(centre * centre, -1, keepdims=True) + epsilon)
    return centre * inverse, inverse


def norm_grad(normed, inverse, gain, grad):
    scaled = grad * gain
    return inverse * (
        scaled - jnp.mean(scaled, -1, keepdims=True) - normed * jnp.mean(scaled * normed, -1, keepdims=True)
    )


def add_rows(ref, value):
    @pl.when(pl.program_id(0) == 0)
    def _():
        ref[...] = value

    @pl.when(pl.program_id(0) > 0)
    def _():
        ref[...] += value


def sides(core, mine, other):
    return (mine, core[0]), (other, 1 - core[0])


def project_kernel(core, x_ref, gain, shift, bias, mine_w, other_w, a_ref, qkv_ref):
    half = x_ref.shape[1] // 2
    normed, _ = norm_parts(x_ref[...].astype(f32))
    a = (normed * gain[...] + shift[...]).astype(bf16)
    a_ref[...] = a
    for w, side in sides(core, mine_w, other_w):
        out = dot(a, w[...])
        for j in range(3):
            at = pl.ds(pl.multiple_of(2 * half * j + half * side, half), half)
            qkv_ref[:, at] = (out[:, half * j : half * (j + 1)] + bias[:, at]).astype(bf16)


def project(core, x, gain, shift, bias, mine_w, other_w, after=()):
    rows, width = x.shape
    weight = whole(width, 3 * width // 2)
    return launch(
        project_kernel,
        "project",
        (rows // BLOCK,),
        (x, gain, shift, bias, mine_w, other_w),
        [
            pl.BlockSpec((BLOCK, width), lambda i, c: (i, 0)),
            whole(1, width),
            whole(1, width),
            whole(1, 3 * width),
            weight,
            weight,
        ],
        (
            pl.BlockSpec((BLOCK, width), lambda i, c: (i, 0)),
            pl.BlockSpec((BLOCK, 3 * width), lambda i, c: (i, 0)),
        ),
        (shape_of((rows, width), bf16), shape_of((rows, 3 * width), bf16)),
        scalars=(core,),
        after=after,
        work=(6 * rows * width * width, 6 * width * width + 10 * rows * width),
    )


def send_slots(acc, slot, values, keep_ref, away_ref):
    step = pl.program_id(0)
    chosen = lax.broadcasted_iota(jnp.int32, (2 * CAPACITY, BLOCK), 0) == slot[...]
    part = dot(chosen.astype(bf16), values)

    @pl.when(step == 0)
    def _():
        acc[...] = part

    @pl.when(step > 0)
    def _():
        acc[...] += part

    @pl.when(step == pl.num_programs(0) - 1)
    def _():
        keep_ref[...] = acc[:CAPACITY, :].astype(bf16)
        away_ref[...] = acc[CAPACITY:, :].astype(bf16)


def dispatch_kernel(slot, g_ref, keep_ref, away_ref, acc):
    send_slots(acc, slot, g_ref[...], keep_ref, away_ref)


def dispatch(slot_row, values, after=()):
    rows, width = values.shape
    return launch(
        dispatch_kernel,
        "dispatch",
        (rows // BLOCK,),
        (slot_row, values),
        [pl.BlockSpec((1, BLOCK), lambda i: (0, i)), pl.BlockSpec((BLOCK, width), lambda i: (i, 0))],
        (whole(CAPACITY, width),) * 2,
        (shape_of((CAPACITY, width), bf16),) * 2,
        [pltpu.VMEM((2 * CAPACITY, width), f32)],
        after=after,
        work=(4 * CAPACITY * rows * width, 2 * rows * width + 4 * CAPACITY * width),
    )


def middle_kernel(
    core, slot, x_ref, o_ref, mine_w, other_w, bias, gain, shift, mid_ref, keep_ref, away_ref, acc
):
    half = x_ref.shape[1] // 2
    for w, side in sides(core, mine_w, other_w):
        at = pl.ds(pl.multiple_of(half * side, half), half)
        mid_ref[:, at] = x_ref[:, at].astype(f32) + dot(o_ref[...], w[...]) + bias[:, at]
    normed, _ = norm_parts(mid_ref[...])
    send_slots(acc, slot, (normed * gain[...] + shift[...]).astype(bf16), keep_ref, away_ref)


def out_half(width):
    return pl.BlockSpec((width, width // 2), lambda *_: (0, 3))


def middle_part(core, slot_row, x, attended, mine_w, other_w, bias, gain, shift, after=()):
    rows, width = x.shape
    block = pl.BlockSpec((BLOCK, width), lambda i, c: (i, 0))
    return launch(
        middle_kernel,
        "middle",
        (rows // BLOCK,),
        (slot_row, x, attended, mine_w, other_w, bias, gain, shift),
        [
            pl.BlockSpec((1, BLOCK), lambda i, c: (0, i)),
            block,
            block,
            out_half(width),
            out_half(width),
            whole(1, width),
            whole(1, width),
            whole(1, width),
        ],
        (block, whole(CAPACITY, width), whole(CAPACITY, width)),
        (shape_of((rows, width), f32),) + (shape_of((CAPACITY, width), bf16),) * 2,
        [pltpu.VMEM((2 * CAPACITY, width), f32)],
        scalars=(core,),
        after=after,
        work=(4 * CAPACITY * rows * width + 2 * rows * width * width, 10 * rows * width + 4 * CAPACITY * width),
    )


def from_slots(slot, keep_ref, away_ref):
    chosen = lax.broadcasted_iota(jnp.int32, (BLOCK, 2 * CAPACITY), 1) == slot[...]
    chosen = chosen.astype(bf16)
    return dot(chosen[:, :CAPACITY], keep_ref[...]) + dot(chosen[:, CAPACITY:], away_ref[...])


def middle_grad_kernel(
    core, slot, keep_ref, away_ref, mid_ref, g_ref, mine_w, other_w, gain,
    dmid_ref, mine_ref, other_ref, do_ref, gain_ref, shift_ref, bias_ref, dproj_ref,
):
    half = mid_ref.shape[1] // 2
    grad = from_slots(slot, keep_ref, away_ref)
    normed, inverse = norm_parts(mid_ref[...])
    dmid = g_ref[...].astype(f32) + norm_grad(normed, inverse, gain[...], grad)
    dproj_ref[...] = dmid.astype(bf16)
    dmid_ref[...] = dmid
    back = 0.0
    for (w, side), part in zip(sides(core, mine_w, other_w), (mine_ref, other_ref)):
        part[...] = dproj_ref[:, pl.ds(pl.multiple_of(half * side, half), half)]
        back = back + dot(part[...], w[...], NT)
    do_ref[...] = back.astype(bf16)
    add_rows(gain_ref, jnp.sum(grad * normed, 0, keepdims=True))
    add_rows(shift_ref, jnp.sum(grad, 0, keepdims=True))
    add_rows(bias_ref, jnp.sum(dproj_ref[...].astype(f32), 0, keepdims=True))


def middle_grad(core, slot_col, keep, away, middle, g, mine_w, other_w, gain, after=()):
    rows, width = middle.shape
    block = pl.BlockSpec((BLOCK, width), lambda i, c: (i, 0))
    part = pl.BlockSpec((BLOCK, width // 2), lambda i, c: (i, 0))
    slots = whole(CAPACITY, width)
    row = whole(1, width)
    return launch(
        middle_grad_kernel,
        "middle_grad",
        (rows // BLOCK,),
        (slot_col, keep, away, middle, g, mine_w, other_w, gain),
        [pl.BlockSpec((BLOCK, 1), lambda i, c: (i, 0)), slots, slots, block, block]
        + [out_half(width), out_half(width), row],
        (block, part, part, block, row, row, row),
        (shape_of((rows, width), f32),)
        + (shape_of((rows, width // 2), bf16),) * 2
        + (shape_of((rows, width), bf16),)
        + (shape_of((1, width), f32),) * 3,
        [pltpu.VMEM((BLOCK, width), bf16)],
        scalars=(core,),
        after=after,
        work=(4 * CAPACITY * rows * width + 2 * rows * width * width, 16 * rows * width + 4 * CAPACITY * width),
    )


def output_kernel(slot, route, keep_ref, away_ref, mid_ref, bias, out_ref):
    token_bias = jnp.where(route[...] == 0, bias[0:1, :], bias[1:2, :])
    out_ref[...] = (mid_ref[...] + from_slots(slot, keep_ref, away_ref) + token_bias).astype(bf16)


def output(slot_col, route_col, keep, away, middle, bias, after=()):
    rows, width = middle.shape
    block = pl.BlockSpec((BLOCK, width), lambda i: (i, 0))
    column = pl.BlockSpec((BLOCK, 1), lambda i: (i, 0))
    return launch(
        output_kernel,
        "output",
        (rows // BLOCK,),
        (slot_col, route_col, keep, away, middle, bias),
        [column, column, whole(CAPACITY, width), whole(CAPACITY, width), block, whole(2, width)],
        block,
        shape_of((rows, width), bf16),
        after=after,
        work=(4 * CAPACITY * rows * width, 6 * rows * width + 4 * CAPACITY * width),
    )


def input_grad_kernel(
    mine_ref, away_ref, x_ref, dmid_ref, mine_w, other_w, gain, out_ref, gain_ref, shift_ref, bias_ref
):
    half = mine_ref.shape[2]
    grad = 0.0
    for ref, w in ((mine_ref, mine_w), (away_ref, other_w)):
        for j in range(3):
            grad = grad + dot(ref[j], w[:, half * j : half * (j + 1)], NT)
    normed, inverse = norm_parts(x_ref[...].astype(f32))
    out_ref[...] = dmid_ref[...] + norm_grad(normed, inverse, gain[...], grad)
    add_rows(gain_ref, jnp.sum(grad * normed, 0, keepdims=True))
    add_rows(shift_ref, jnp.sum(grad, 0, keepdims=True))
    rows = [jnp.sum(ref[j].astype(f32), 0, keepdims=True) for j in (0, 2) for ref in (mine_ref, away_ref)]
    add_rows(bias_ref, jnp.concatenate(rows, 0))


def input_grads(mine, away, x, dmid, mine_w, other_w, gain, after=()):
    rows, width = x.shape
    half = width // 2
    block = pl.BlockSpec((BLOCK, width), lambda i: (i, 0))
    part = pl.BlockSpec((3, BLOCK, half), lambda i: (0, i, 0))
    row, weight = whole(1, width), whole(width, 3 * half)
    return launch(
        input_grad_kernel,
        "input_grad",
        (rows // BLOCK,),
        (mine, away, x, dmid, mine_w, other_w, gain),
        [part, part, block, block, weight, weight, row],
        (block, row, row, whole(4, half)),
        (
            shape_of((rows, width), f32),
            shape_of((1, width), f32),
            shape_of((1, width), f32),
            shape_of((4, half), f32),
        ),
        after=after,
        work=(6 * rows * width * width, 16 * rows * width + 6 * width * width),
    )


def two_sum_kernel(at, n_dp, me, a1, b1, a2, b2, out_ref, far_x, far_y, t1, t2):
    step = pl.program_id(0)

    @pl.when(step == 0)
    def _():
        t1[...] = a1[...].T
        t2[...] = a2[...].T

    out_ref[...] = (dot(t1[...], b1[0]) + dot(t2[...], b2[0])).astype(bf16)
    rows = out_ref.shape[0] // n_dp
    far = pl.ds(pl.multiple_of((me[0] ^ (n_dp - 1)) * rows, rows), rows)

    @pl.when(step + at < 2)
    def _():
        far_x[...] = out_ref[far, :]

    @pl.when(step + at >= 2)
    def _():
        far_y[...] = out_ref[far, :]


def two_sum(me, n_dp, a1, b1, a2, b2, at, into=(), after=()):
    rows, width = a1.shape
    parts, _, columns = b1.shape
    left, right = whole(rows, width), pl.BlockSpec((1, rows, columns), lambda j, m: (j, 0, 0))
    count = 5 + len(into)

    def body(*refs):
        two_sum_kernel(at, n_dp, *refs[:5], *refs[count + len(after) :])

    far = (width // n_dp, columns)
    return pl.pallas_call(
        body,
        grid_spec=pltpu.PrefetchScalarGridSpec(
            num_scalar_prefetch=1,
            grid=(parts,),
            in_specs=[left, right, left, right] + [pl.BlockSpec(memory_space=pl.ANY)] * (len(into) + len(after)),
            out_specs=(
                pl.BlockSpec((width, columns), lambda j, m: (0, at + j)),
                pl.BlockSpec(far, lambda j, m: (0, jnp.minimum(at + j, 1))),
                pl.BlockSpec(far, lambda j, m: (0, jnp.maximum(at + j - 2, 0))),
            ),
            scratch_shapes=[pltpu.VMEM((width, rows), bf16)] * 2,
        ),
        out_shape=(
            shape_of((width, 4 * columns), bf16),
            shape_of((width // n_dp, 2 * columns), bf16),
            shape_of((width // n_dp, 2 * columns), bf16),
        ),
        input_output_aliases={5 + i: i for i in range(len(into))},
        **params(4 * rows * width * columns * parts, 4 * rows * (width + parts * columns)),
        name="two_sum",
    )(me, a1, b1, a2, b2, *into, *after)


def up_kernel(me, xk, xr, bias, w0, w1, w2, w3a, w3b, act_ref, slope_ref):
    step = pl.program_id(0)
    depth = w0.shape[0]
    far = jnp.where(step < pl.num_programs(0) // 2, w3a[...], w3b[...])
    root = 0.7978845608028654
    for part, x in enumerate((xk, xr)):
        inner = bias[...]
        for r, w in enumerate((w0[...], w1[...], w2[...], far)):
            at = pl.multiple_of((me[0] ^ r) * depth, depth)
            inner = inner + dot(x[:, pl.ds(at, depth)], w)
        square = inner * inner
        bent = jnp.tanh(inner * (root + (root * 0.044715) * square))
        rise = 0.5 + 0.5 * bent
        act = (inner * rise).astype(bf16)
        slope = rise + inner * rise * (1.0 - bent) * (root + (root * 3 * 0.044715) * square)
        rows = slice(part * x.shape[0], (part + 1) * x.shape[0])
        act_ref[rows, :] = act
        slope_ref[rows, :] = slope.astype(bf16)


def up(me, xk, xr, bias, pieces, after=()):
    slots, width = xk.shape
    depth, hidden = pieces[0].shape
    steps = hidden // FBLOCK
    last = steps // 2 - 1
    tokens = whole(slots, width)
    weight = pl.BlockSpec((depth, FBLOCK), lambda i, m: (0, i))
    return launch(
        up_kernel,
        "experts_up",
        (steps,),
        (xk, xr, bias, *pieces),
        [tokens] * 2
        + [pl.BlockSpec((1, FBLOCK), lambda i, m: (0, i))]
        + [weight] * 3
        + [
            pl.BlockSpec((depth, FBLOCK), lambda i, m: (0, jnp.minimum(i, last))),
            pl.BlockSpec((depth, FBLOCK), lambda i, m: (0, jnp.maximum(i - last - 1, 0))),
        ],
        (
            pl.BlockSpec((2 * slots, FBLOCK), lambda i, m: (0, i)),
            pl.BlockSpec((2 * slots, FBLOCK), lambda i, m: (0, i)),
        ),
        (shape_of((2 * slots, hidden), bf16), shape_of((2 * slots, hidden), bf16)),
        scalars=(me,),
        after=after,
        work=(4 * slots * width * hidden, 2 * width * hidden + 8 * slots * hidden),
    )


def outer_kernel(act_ref, gk, gr, out_ref, bias_ref, g):
    @pl.when(pl.program_id(0) == 0)
    def _():
        half = gk.shape[0]
        g[:half, :] = gk[...]
        g[half:, :] = gr[...]
        bias_ref[...] = jnp.sum(g[...].astype(f32), 0, keepdims=True)

    out_ref[...] = dot(act_ref[...], g[...], TN).astype(bf16)


def outer(act, gk, gr, after=()):
    slots, width = gk.shape
    hidden = act.shape[1]
    return launch(
        outer_kernel,
        "experts_outer",
        (hidden // FBLOCK,),
        (act, gk, gr),
        [pl.BlockSpec((2 * slots, FBLOCK), lambda i: (0, i)), whole(slots, width), whole(slots, width)],
        (pl.BlockSpec((FBLOCK, width), lambda i: (i, 0)), whole(1, width)),
        (shape_of((hidden, width), bf16), shape_of((1, width), f32)),
        [pltpu.VMEM((2 * slots, width), bf16)],
        after=after,
        work=(4 * slots * width * hidden, 2 * width * hidden + 4 * slots * hidden),
    )


def hold_block(held, per, pieces):
    w0, w1, w2, w3a, w3b = pieces
    which = pl.program_id(0) // per
    half = w3a.shape[1]
    for r, w in enumerate((w0, w1, w2)):

        @pl.when(which == r)
        def _(w=w):
            held[...] = w[...]

    @pl.when(which == 3)
    def _():
        held[:, :half] = w3a[...]
        held[:, half:] = w3b[...]


def down_grad_kernel(
    me, per, gk, gr, xk, xr, slope_ref, u0, u1, u2, u3a, u3b, w0, w1, w2, w3a, w3b,
    dk_ref, dr_ref, up_ref, far_x, far_y, bias_ref, held, acc, g, t,
):
    step = pl.program_id(0)
    slots = gk.shape[0]
    hold_block(held, per, (w0, w1, w2, w3a, w3b))

    @pl.when(step == 0)
    def _():
        g[:slots, :] = gk[...]
        g[slots:, :] = gr[...]
        t[:, :slots] = xk[...].T
        t[:, slots:] = xr[...].T
        acc[...] = jnp.zeros_like(acc)

    depth = u0.shape[0]
    early = (me[0] ^ (step // per)) * per + step % per < pl.num_programs(0) // 2
    u3 = jnp.where(early, u3a[...], u3b[...])
    inner = (dot(g[...], held[...], NT) * slope_ref[...].astype(f32)).astype(bf16)
    bias_ref[...] = jnp.sum(inner.astype(f32), 0, keepdims=True)
    up_ref[...] = dot(t[...], inner).astype(bf16)
    far = up_ref[pl.ds(pl.multiple_of((me[0] ^ 3) * depth, depth), depth), :]

    @pl.when(early)
    def _():
        far_x[...] = far

    @pl.when(jnp.logical_not(early))
    def _():
        far_y[...] = far

    for r, u in enumerate((u0[...], u1[...], u2[...], u3)):
        at = pl.multiple_of((me[0] ^ r) * depth, depth)
        acc[:, pl.ds(at, depth)] += dot(inner, u, NT)

    @pl.when(step == pl.num_programs(0) - 1)
    def _():
        dk_ref[...] = acc[:slots, :].astype(bf16)
        dr_ref[...] = acc[slots:, :].astype(bf16)


def piece_specs(width, per, which):
    def spec(r, columns):
        return pl.BlockSpec((FBLOCK, columns), lambda i, m: (jnp.clip(i - r * per, 0, per - 1), 0))

    return [spec(r, width // 2 if r == 3 else width) for r in which for _ in range(2 if r == 3 else 1)]


def down_grad(me, gk, gr, xk, xr, slope, up_pieces, down_pieces, after=()):
    slots, width = xk.shape
    depth, hidden = up_pieces[0].shape
    per = down_pieces[0].shape[0] // FBLOCK
    steps = hidden // FBLOCK
    half = steps // 2
    at = lambda i, m: (m[0] ^ (i // per)) * per + i % per

    def far(first):
        def block(i, m):
            low = jnp.where((m[0] < 2) == first, 0, half)
            return 0, at(jnp.clip(i, low, low + half - 1), m) - (0 if first else half)

        return pl.BlockSpec((depth, FBLOCK), block)

    tokens = whole(slots, width)
    weight = pl.BlockSpec((depth, FBLOCK), lambda i, m: (0, at(i, m)))
    return launch(
        lambda me, *refs: down_grad_kernel(me, per, *refs),
        "experts_grad",
        (steps,),
        (gk, gr, xk, xr, slope, *up_pieces, *down_pieces),
        [tokens] * 4
        + [pl.BlockSpec((2 * slots, FBLOCK), lambda i, m: (0, at(i, m)))]
        + [weight] * 3
        + [
            pl.BlockSpec((depth, FBLOCK), lambda i, m: (0, jnp.minimum(at(i, m), half - 1))),
            pl.BlockSpec((depth, FBLOCK), lambda i, m: (0, jnp.maximum(at(i, m) - half, 0))),
        ]
        + piece_specs(width, per, range(4)),
        (
            tokens,
            tokens,
            pl.BlockSpec((width, FBLOCK), lambda i, m: (0, at(i, m))),
            far(True),
            far(False),
            pl.BlockSpec((1, FBLOCK), lambda i, m: (0, at(i, m))),
        ),
        (
            shape_of((slots, width), bf16),
            shape_of((slots, width), bf16),
            shape_of((width, hidden), bf16),
            shape_of((depth, hidden // 2), bf16),
            shape_of((depth, hidden // 2), bf16),
            shape_of((1, hidden), f32),
        ),
        [
            pltpu.VMEM((FBLOCK, width), bf16),
            pltpu.VMEM((2 * slots, width), f32),
            pltpu.VMEM((2 * slots, width), bf16),
            pltpu.VMEM((width, 2 * slots), bf16),
        ],
        scalars=(me,),
        after=after,
        work=(12 * slots * width * hidden, 6 * width * hidden + 4 * slots * hidden),
    )


def down_near_kernel(me, act_ref, w0, w1, w2, out_ref, acc):
    step = pl.program_id(0)
    which = step // (pl.num_programs(0) // 3)
    w = jnp.where(which == 0, w0[...], jnp.where(which == 1, w1[...], w2[...]))
    part = dot(act_ref[...], w)

    @pl.when(step == 0)
    def _():
        acc[...] = part

    @pl.when(step > 0)
    def _():
        acc[...] += part

    @pl.when(step == pl.num_programs(0) - 1)
    def _():
        out_ref[...] = acc[...].astype(bf16)


def down_near(me, act, pieces, after=()):
    slots = act.shape[0]
    rows, width = pieces[0].shape
    per = rows // FBLOCK
    return launch(
        down_near_kernel,
        "down_near",
        (3 * per,),
        (act, *pieces),
        [pl.BlockSpec((slots, FBLOCK), lambda i, m: (0, (m[0] ^ (i // per)) * per + i % per))]
        + piece_specs(width, per, range(3)),
        whole(slots, width),
        shape_of((slots, width), bf16),
        [pltpu.VMEM((slots, width), f32)],
        scalars=(me,),
        after=after,
        work=(2 * slots * width * rows * 3, 2 * width * rows * 3 + 2 * slots * rows * 3),
    )


def down_far_kernel(me, act_ref, wa, wb, near_ref, keep_ref, away_ref, acc):
    half = wa.shape[1]

    @pl.when(pl.program_id(0) == 0)
    def _():
        acc[...] = near_ref[...].astype(f32)

    acc[:, :half] += dot(act_ref[...], wa[...])
    acc[:, half:] += dot(act_ref[...], wb[...])

    @pl.when(pl.program_id(0) == pl.num_programs(0) - 1)
    def _():
        slots = keep_ref.shape[0]
        keep_ref[...] = acc[:slots, :].astype(bf16)
        away_ref[...] = acc[slots:, :].astype(bf16)


def down_far(me, act, wa, wb, near, after=()):
    slots, width = near.shape
    per = wa.shape[0] // FBLOCK
    half = pl.BlockSpec((FBLOCK, width // 2), lambda i, m: (i, 0))
    return launch(
        down_far_kernel,
        "down_far",
        (per,),
        (act, wa, wb, near),
        [pl.BlockSpec((slots, FBLOCK), lambda i, m: (0, (m[0] ^ 3) * per + i)), half, half, whole(slots, width)],
        (whole(slots // 2, width),) * 2,
        (shape_of((slots // 2, width), bf16),) * 2,
        [pltpu.VMEM((slots, width), f32)],
        scalars=(me,),
        after=after,
        work=(2 * slots * width * wa.shape[0], 6 * slots * width),
    )


def place_kernel(at, *refs):
    out_ref = refs[-1]
    for r, piece in enumerate(refs[: 4 if len(refs) == 6 else -1]):

        @pl.when(pl.program_id(0) == r)
        def _(r=r, piece=piece):
            columns = piece.shape[1]
            out_ref[0, :, :columns] = piece[...]
            if columns < out_ref.shape[2]:
                out_ref[0, :, columns:] = refs[r + 1][...]


def place(at, pieces, after=()):
    rows, columns = pieces[0].shape
    count = sum(p.shape[1] for p in pieces) // columns
    return launch(
        place_kernel,
        "place",
        (count,),
        pieces,
        [whole(*p.shape) for p in pieces],
        pl.BlockSpec((1, rows, columns), lambda r, at: (at[0] ^ r, 0, 0)),
        shape_of((count, rows, columns), bf16),
        scalars=(at,),
        after=after,
        work=(0, 4 * count * rows * columns),
    ).reshape(count * rows, columns)


def pick(array, index, axis=0):
    return lax.dynamic_index_in_dim(array, index, axis, keepdims=False)


def swap(value, axis, size, mask):
    return lax.ppermute(value, axis, [(i, i ^ mask) for i in range(size)])


def swap_core(value):
    return swap(value, "c", 2, 1)


def by_core(core, mine, other, axis=0):
    return jnp.where(core == 0, jnp.stack([mine, other], axis), jnp.stack([other, mine], axis))


def add_kernel(me, part_x, part_y, by_x, by_y, next_x, next_y):
    first = pl.program_id(0) == 0
    more_x = jnp.where(first, 0.0, by_y[...].astype(f32))
    more_y = jnp.where(first, by_x[...].astype(f32), 0.0)
    next_x[...] = (part_x[0].astype(f32) + more_x).astype(bf16)
    next_y[...] = (part_y[0].astype(f32) + more_y).astype(bf16)


def scatter_next(me, partial, by_x, by_y, after=()):
    _, rows, columns = partial.shape
    half = columns // 2
    step = rows // 2
    block = lambda mask: pl.BlockSpec((1, step, half), lambda h, i, m: (m[0] ^ mask, i, h))
    next_x, next_y = launch(
        add_kernel,
        "far_add",
        (2, 2),
        (partial, partial, by_x, by_y),
        [
            block(1),
            block(2),
            pl.BlockSpec((step, half), lambda h, i, m: (jnp.where(h == 0, i, 1), 0)),
            pl.BlockSpec((step, half), lambda h, i, m: (jnp.where(h == 0, 0, i), 0)),
        ],
        (pl.BlockSpec((step, half), lambda h, i, m: (i, h)),) * 2,
        (shape_of((rows, columns), bf16),) * 2,
        scalars=(me,),
        after=after,
    )
    return next_x, next_y


def swap_near(x, y):
    return swap(x, "dp", 4, 1), swap(y, "dp", 4, 2)


def near_kernel(me, part, got_x, got_y, out_ref):
    out_ref[...] = (part[0].astype(f32) + got_x[...].astype(f32) + got_y[...].astype(f32)).astype(bf16)


def scatter_near(me, partial, got_x, got_y, after=()):
    _, rows, columns = partial.shape
    step = rows // 4
    block = pl.BlockSpec((step, columns), lambda i, m: (i, 0))
    return launch(
        near_kernel,
        "near_add",
        (4,),
        (partial, got_x, got_y),
        [pl.BlockSpec((1, step, columns), lambda i, m: (m[0], i, 0)), block, block],
        block,
        shape_of((rows, columns), bf16),
        scalars=(me,),
        after=after,
    )


def to_core(total):
    core = lax.axis_index("c")
    halves = total.reshape(2, total.shape[0] // 2, total.shape[1])
    return pick(halves, core), swap_core(pick(halves, 1 - core))


def gather_z(shard):
    return lax.all_gather(shard, "z", axis=0, tiled=True)


def scatter_z(block):
    return lax.psum_scatter(block, "z", scatter_dimension=0, tiled=True)


def later(value, after):
    def body(*refs):
        pass

    return pl.pallas_call(
        body,
        in_specs=[pl.BlockSpec(memory_space=pl.ANY)] * (1 + len(after)),
        out_specs=pl.BlockSpec(memory_space=pl.ANY),
        out_shape=shape_of(value.shape, value.dtype),
        input_output_aliases={0: 0},
        **params(0, 0),
        name="later",
    )(value, *after)


def halves_kernel(x_ref, y_ref, out_x, out_y):
    half = out_x.shape[1]
    out_x[...] = x_ref[:, :half]
    out_y[...] = y_ref[:, half:]


def cut_halves(by_x, by_y, after=()):
    rows, columns = by_x.shape
    step = rows // 2
    block = pl.BlockSpec((step, columns), lambda i: (i, 0))
    half = pl.BlockSpec((step, columns // 2), lambda i: (i, 0))
    return launch(
        halves_kernel,
        "cut_halves",
        (2,),
        (by_x, by_y),
        [block, block],
        (half, half),
        (shape_of((rows, columns // 2), bf16),) * 2,
        after=after,
    )


def gather_far(cut):
    return swap(cut[0], "dp", 4, 2), swap(cut[1], "dp", 4, 1)


def gather_pieces(own):
    full = lax.all_gather(own, "dp", axis=0, tiled=True)
    rows, columns = full.shape
    blocks = full.reshape(4, rows // 4, columns)
    return blocks[0], blocks[1], blocks[2], blocks[3, :, : columns // 2], blocks[3, :, columns // 2 :]


def shards(
    n_dp,
    n_z,
    tokens,
    segment_ids,
    expert_ids,
    ln1_gain,
    ln1_bias,
    qkv_weight,
    query_bias,
    value_bias,
    out_weight,
    out_bias,
    ln2_gain,
    ln2_bias,
    up_weight,
    up_bias,
    down_weight,
    down_bias,
    cotangent,
):
    rows, width = tokens.shape
    devices = n_dp * n_z * 2
    share = qkv_weight.shape[0]
    up_share = up_bias.shape[1]
    core = lax.axis_index("c")
    scalar = lambda v: jnp.reshape(v, (1,)).astype(jnp.int32)
    square = n_dp == 4
    me = scalar(lax.axis_index("dp") if square else 0)

    half = width // 2
    both_w = jnp.concatenate([qkv_weight, out_weight], 1).reshape(share, 4, 2, half)
    mine_w, other_w = (pick(both_w, side, 2).reshape(share, 4 * half) for side in (core, 1 - core))
    attn_shard = place(scalar(core), [mine_w, swap_core(other_w)])
    small = jnp.concatenate(
        [ln1_gain, ln1_bias, query_bias, value_bias, out_bias, ln2_gain, ln2_bias, up_bias.reshape(-1), down_bias.reshape(-1)]
    )
    small = jnp.broadcast_to(small, (devices, small.shape[0]))
    small = lax.all_to_all(small, ALL, 0, 0, tiled=True).astype(f32)
    gain_one, shift_one, bias_query, bias_value, bias_out, gain_two, shift_two = (
        small[:, i * share : (i + 1) * share].reshape(1, width) for i in range(7)
    )
    bias_up = small[:, 7 * share : 7 * share + 2 * up_share].reshape(devices, 2, up_share)
    bias_up = pick(bias_up, core, 1).reshape(1, -1)
    bias_down = small[:, 7 * share + 2 * up_share :].reshape(devices, 2, share)
    bias_down = jnp.swapaxes(bias_down, 0, 1).reshape(2, width)

    def expert_shard(weight, after):
        mine, other = pick(weight, core, 1), swap_core(pick(weight, 1 - core, 1))
        return place(scalar(core), [mine, other], after)

    route = expert_ids[:, 0]
    at = lax.iota(jnp.int32, rows)
    before = (route[:, None] == route[None, :]) & (at[None, :] < at[:, None])
    slot = jnp.sum(before.astype(jnp.int32), 1) + jnp.where(route == core, 0, CAPACITY)
    slot_row, slot_col = slot.reshape(1, rows), slot.reshape(rows, 1)

    grad_keep, grad_away = dispatch(slot_row, cotangent, (attn_shard,))
    grad_got = swap_core(grad_away)
    up_shard = expert_shard(up_weight, (grad_keep,))
    up_own = gather_z(up_shard)
    down_shard = expert_shard(down_weight, (up_shard,))
    attn_own = later(gather_z(attn_shard), (down_shard,))
    if square:
        attn_near = swap_near(attn_own, attn_own)
        attn_far = gather_far(cut_halves(*attn_near))
        mine_w = place(me, [attn_own, *attn_near, *attn_far], (up_own, down_shard, grad_got, bias_down))
        up_near = swap_near(up_own, up_own)
    else:
        mine_w = lax.all_gather(attn_own, "dp", axis=0, tiled=True)
    other_w = swap_core(mine_w)

    side = scalar(core)
    qkv_bias = jnp.concatenate([bias_query, jnp.zeros_like(bias_query), bias_value], 1)
    normed_one, qkv = project(side, tokens, gain_one, shift_one, qkv_bias, mine_w, other_w, (up_own,))
    other_normed_one = swap_core(normed_one)
    seg_row, seg_col = segment_ids, segment_ids.reshape(rows, 1)
    attended, lse = attention(qkv, seg_col, seg_row)
    other_attended = swap_core(attended)
    if square:
        up_cut = cut_halves(*up_near, (attended,))
        w_up = (up_own, *up_near, *gather_far(up_cut))
    else:
        up_cut, w_up = (), gather_pieces(up_own)
    middle, in_keep, in_away = middle_part(
        side, slot_row, tokens, attended, mine_w, other_w, bias_out, gain_two, shift_two, after=(*up_cut, other_normed_one)
    )
    down_own = later(gather_z(down_shard), (middle,))
    in_got = swap_core(later(in_away, (*w_up[3:], down_own)))

    if square:
        down_near_got = swap_near(down_own, down_own)
    act, slope = up(me, in_keep, in_got, bias_up, w_up)
    down_partial, down_bias_grad = outer(act, grad_keep, grad_got)
    if square:
        down_cut = cut_halves(*down_near_got, (down_partial,))
        w_down = (down_own, *down_near_got, *gather_far(down_cut))
    else:
        down_cut, w_down = (), gather_pieces(down_own)
    y_near = down_near(me, act, w_down[:3], down_cut)
    down_half = lax.psum_scatter(later(down_partial, (*w_down[3:], y_near)), "dp", scatter_dimension=0, tiled=True)
    back_keep, back_away, up_partial, up_out_x, up_out_y, up_bias_grad = down_grad(
        me, grad_keep, grad_got, in_keep, in_got, slope, w_up, w_down, after=(y_near,)
    )
    back_got = swap_core(back_away)
    if square:
        up_partial = up_partial.reshape(4, width // 4, -1)
        up_far = swap_near(up_out_x, up_out_y)

    middle_grads, mine_projected, other_projected, attended_grad, gain_two_grad, shift_two_grad, out_bias_grad = (
        middle_grad(side, slot_col, back_keep, back_got, middle, cotangent, mine_w, other_w, gain_two)
    )
    other_projected = swap_core(other_projected)
    qkv_away = attention_grad(qkv, attended_grad, lse, seg_col, seg_row, 1 - core)
    qkv_got = swap_core(qkv_away)
    up_next = scatter_next(me, up_partial, *up_far, after=(qkv_away,)) if square else ()
    partial = two_sum(
        me, 4, attended, mine_projected[None], other_attended, other_projected[None], 0, after=up_next
    )
    down_total = scatter_z(later(down_half, up_next))
    qkv_kept = attention_grad(qkv, attended_grad, lse, seg_col, seg_row, core, after=partial[:1])
    partial, out_x, out_y = two_sum(
        me, 4, normed_one, qkv_kept, other_normed_one, qkv_got, 1, into=partial, after=()
    )
    if square:
        partial = partial.reshape(4, width // 4, -1)
        far = swap_near(out_x, out_y)
        up_block = scatter_near(me, up_partial, *swap_near(*up_next), after=(out_x, down_total))
    else:
        up_block = lax.psum_scatter(up_partial, "dp", scatter_dimension=0, tiled=True)
    up_total = scatter_z(up_block)
    y_keep, y_away = down_far(me, act, *w_down[3:], y_near, after=(up_block,))
    y_got = swap_core(y_away)
    near = scatter_next(me, partial, *far, after=(y_keep,)) if square else ()
    input_grad, gain_one_grad, shift_one_grad, bias_sums = input_grads(
        qkv_kept, qkv_away, tokens, middle_grads, mine_w, other_w, gain_one, after=near
    )
    query_bias_grad = by_core(core, bias_sums[0], bias_sums[1])
    value_bias_grad = by_core(core, bias_sums[2], bias_sums[3])
    if square:
        last = scatter_near(me, partial, *swap_near(*near), after=(input_grad,))
    else:
        last = lax.psum_scatter(partial, "dp", scatter_dimension=0, tiled=True)

    vectors = [
        gain_one_grad,
        shift_one_grad,
        query_bias_grad,
        value_bias_grad,
        out_bias_grad,
        gain_two_grad,
        shift_two_grad,
        up_bias_grad,
        down_bias_grad,
    ]
    sent = later(jnp.concatenate([v.reshape(devices, -1) for v in vectors], 1), (last,))
    got = lax.all_to_all(sent, ALL, 0, 0, tiled=True).reshape(devices // 2, 2, -1)
    both = jnp.sum(got, 0)
    total = both[0] + both[1]
    sums = [total[i * share : (i + 1) * share] for i in range(7)]
    at = 7 * share
    up_bias_sum = both[:, at : at + up_share]
    down_bias_sum = both[:, at + up_share :]

    block_out = output(slot_col, expert_ids, y_keep, y_got, middle, bias_down, after=(sent,))
    down_weight_grad = by_core(core, *to_core(down_total.astype(f32)), 1)
    up_weight_grad = by_core(core, *to_core(up_total.astype(f32)), 1)
    last = later(scatter_z(last), (block_out, down_weight_grad, up_weight_grad))
    last = to_core(last.astype(f32))
    out_weight_grad = by_core(core, *(v[:, :half] for v in last), 1).reshape(share, width)
    qkv_weight_grad = by_core(core, *(v[:, half:].reshape(share, 3, half) for v in last), 2).reshape(share, 3 * width)
    return (
        block_out,
        input_grad,
        sums[0],
        sums[1],
        qkv_weight_grad,
        sums[2],
        sums[3],
        out_weight_grad,
        sums[4],
        sums[5],
        sums[6],
        up_weight_grad,
        up_bias_sum,
        down_weight_grad,
        down_bias_sum,
    )


def solution(mesh):
    n_dp, n_z = mesh.shape["dp"], mesh.shape["fsdp"] // 2
    split = Mesh(mesh.devices.reshape(n_dp, n_z, 2), ALL)
    row, flat, wide, cube = P(ALL, None), P(ALL), P(None, ALL), P(ALL, None, None)
    in_specs = (row, row, row, flat, flat, row, flat, flat, row, flat, flat, flat, cube, wide, cube, wide, row)
    out_specs = (row, row, flat, flat, row, flat, flat, row, flat, flat, flat, cube, wide, cube, wide)
    return jax.shard_map(
        functools.partial(shards, n_dp, n_z), mesh=split, in_specs=in_specs, out_specs=out_specs, check_vma=False
    )
```

time: 778 us -> 522 us (0.67)
  Pallas kernels: 73.9 us -> 322 us
  waiting for transfers between devices: 319 us -> 87.2 us
  matrix products: 187 us -> 0 us
  local copies, waits for them, and re-layouts: 89.5 us -> 39.9 us
  other arithmetic: 48.5 us -> 15.9 us
    pallas_call x3 -> x34, Pallas kernels: 73.9 us -> 322 us  [the longest x25 303 us: launch(): pl.pallas_call(body, grid_spec=pltpu.PrefetchScalarGridSpec(num_scalar_pr...]
    dot_general x22 -> x0, matrix products: 187 us -> none  [dot(): return lax.dot_general(a, b, dims, preferred_element_type=f32)]
    all_gather x3, waiting for transfers between devices: 192 us -> 11.3 us  [gather_z(): return lax.all_gather(shard, 'z', axis=0, tiled=True)]
    ppermute x42 -> x35, waiting for transfers between devices: 127 us -> 62.5 us  [swap(): return lax.ppermute(value, axis, [(i, i ^ mask) for i in range(size)])]
    slice x23 -> x4, local copies, waits for them, and re-layouts: 23.8 us -> 0.11 us  [the longest x1 0.08 us: shards(): small[:, i * share:(i + 1) * share].reshape(1, width)]
    convert_element_type x14 -> x0, other arithmetic: 13.6 us -> none  [the longest x4 9.75 us: scatter_dp(): (pick(partial, me).astype(f32) + got_x.astype(f32) + got_y.astype(f32)).a...]
    reduce_sum x9 -> x0, other arithmetic: 13.5 us -> none  [the longest x2 5.79 us: layer_norm(): return centre * lax.rsqrt(spread + epsilon) * gain + shift]
    unnamed x124 -> x114, local copies, waits for them, and re-layouts: 32.7 us -> 19.7 us
  transfers between devices with their start and end apart: 46 -> 44, of which waited for: 23 -> 24; matrix products, arithmetic and copies ran while one was open for 39% -> 7% of each run, Pallas kernels for 10% -> 60%
where the time goes in v2:
time: 522 us; the launch traced here: 513 us
  Pallas kernels  322 us (62%)
  waiting for transfers between devices  87.2 us (17%)
  local copies, waits for them, and re-layouts  39.9 us (8%)
  starting transfers between devices  32.2 us (6%)
  other arithmetic  15.9 us (3%)
  between operations  15.4 us (3%)
    pallas_call x25, Pallas kernels, launch(): pl.pallas_call(body, grid_spec=pltpu.PrefetchScalarGridSpec(num_scalar_pr...  303 us
    ppermute x35, waiting for transfers between devices, swap(): return lax.ppermute(value, axis, [(i, i ^ mask) for i in range(size)])  62.5 us
    ppermute x35, starting transfers between devices, swap(): return lax.ppermute(value, axis, [(i, i ^ mask) for i in range(size)])  26 us
    unnamed x114, local copies, waits for them, and re-layouts  19.7 us
    pallas_call x2, Pallas kernels, two_sum(): pl.pallas_call(body, grid_spec=pltpu.PrefetchScalarGridSpec(num_scalar_pr...  19.2 us
    all_gather x3, waiting for transfers between devices, gather_z(): return lax.all_gather(shard, 'z', axis=0, tiled=True)  11.3 us
  transfers between devices with their start and end apart: 44, of which 24 were waited for; matrix products, arithmetic and copies ran while one was open for 7% of the time, Pallas kernels for 60%

profile of v2, /device:TPU:0, one launch (start us, length us, event | category | flops | bytes accessed | tf_op | source)
XLA Modules:
  0.0 512.8 jit_solution(4801095742905114956)
XLA Ops:
  8.5 1.6 dynamic-slice_reduce_fusion
  12.3 1.7 place.4
  19.5 8.1 %dispatch.1 = (bf16[640,1024]{1,0:T(8,128)(2,1)}, bf16[640,1024]{1,0:T(8,128)(2,1)}) custom-call(s32[1,1024]{1,0:T(1,128)} %add.51.refs_0_.refs_1_, bf16[1024,1024]{1,0:T(8,128)(2,1)} %refs_5_.1, bf16[64,2048]{1,0:T(8,128)(2,1)} %bitcast.108), custom_call_target="tpu_custom_call" | custom-call | flops 5368709120 | bytes 4718592 | tf_op jit(solution)/shard_map/dispatch/pallas_call | solution.py:44
  28.3 1.8 place.5
  33.6 1.9 place.6
  35.5 9.2 %all-gather.4.cloned.1.call-done.refs_0_ = bf16[256,2048]{1,0:T(8,128)(2,1)} async-done(((bf16[64,2048]{1,0:T(8,128)(2,1)}), bf16[256,2048]{1,0:T(8,128)(2,1)}) %all-gather.4.cloned.1.call-update) | async-done | bytes 1048592 | tf_op jit(solution)/shard_map/all_gather | solution.py:899
  44.8 1.5 collective-permute-start.3
  47.8 22.0 %collective-permute-done.3.refs_0_.refs_2_ = bf16[256,2048]{1,0:T(8,128)(2,1)S(1)} collective-permute-done((bf16[256,2048]{1,0:T(8,128)(2,1)}, bf16[256,2048]{1,0:T(8,128)(2,1)S(1)}, u32[]{:S(2)}, u32[]{:S(2)}) %collective-permute-start.3) | collective-permute-done | bytes 1048608 | tf_op jit(solution)/shard_map/ppermute | solution.py:824
  72.0 2.4 cut_halves.3
  79.5 2.8 all-to-all-start
  82.3 7.9 %all-to-all-done = bf16[32,2,272]{2,1,0:T(2,128)(2,1)S(1)} async-done(((bf16[32,2,272]{2,1,0:T(2,128)(2,1)}), bf16[32,2,272]{2,1,0:T(2,128)(2,1)S(1)}, u32[]{:S(2)}, u32[]{:S(2)}) %all-to-all-start) | async-done | bytes 34848 | tf_op jit(solution)/shard_map/all_to_all | solution.py:993
  91.2 2.1 all-gather.6.cloned.1.call-done.refs_6_.refs_7_.refs_4_
  93.3 4.7 place.7
  101.5 1.5 collective-permute-start.10
  105.5 12.9 %project.1 = (bf16[1024,1024]{1,0:T(8,128)(2,1)}, bf16[1024,3072]{1,0:T(8,128)(2,1)}) custom-call(s32[1]{0:T(128)} %bitcast.3.refs_0_, bf16[1024,1024]{1,0:T(8,128)(2,1)} %refs_2_.7, f32[1,1024]{1,0:T(1,128)} %reshape.228.refs_2_.refs_6_, f32[1,1024]{1,0:T(1,128)} %reshape.229.refs_3_, f32[1,3072]{1,0:T(1,128)} %pad_maximum_fusion.1.refs_4_, ...), custom_call_target="tpu_custom_call" | custom-call | flops 12884901888 | bytes 16777216 | tf_op jit(solution)/shard_map/project/pallas_call | solution.py:44
  118.5 32.8 %attention_forward.1 = (bf16[1024,1024]{1,0:T(8,128)(2,1)}, f32[8,2,1024]{2,1,0:T(2,128)}) custom-call(s32[1024,1]{1,0:T(8,128)} %copy.140.refs_0_.refs_1_, s32[1,1024]{1,0:T(1,128)} %refs_2_.6, bf16[1024,3072]{1,0:T(8,128)(2,1)} %get-tuple-element.67.refs_2_.refs_3_.refs_4_.refs_5_, bf16[1024,3072]{1,0:T(8,128)(2,1)} %get-tuple-element.67.refs_2_.refs_3_.refs_4_.refs_5_, ...), custom_call_target="tpu_custom_call" | custom-call | flops 34359738368 | bytes 8388608 | tf_op jit(solution)/shard_map/attention_forward/pallas_call | solution.py:44
  153.3 3.2 cut_halves.4
  161.5 13.7 %middle.1 = (f32[1024,1024]{1,0:T(8,128)}, bf16[640,1024]{1,0:T(8,128)(2,1)}, bf16[640,1024]{1,0:T(8,128)(2,1)}) custom-call(s32[1]{0:T(128)} %bitcast.3.refs_0_, s32[1,1024]{1,0:T(1,128)} %add.51.refs_0_.refs_1_, bf16[1024,1024]{1,0:T(8,128)(2,1)} %refs_2_.7, bf16[1024,1024]{1,0:T(8,128)(2,1)} %get-tuple-element.68.refs_2_.refs_3_.refs_1_, ...), custom_call_target="tpu_custom_call" | custom-call | flops 9663676416 | bytes 13107200 | tf_op jit(solution)/shard_map/middle/pallas_call | solution.py:44
  175.2 7.0 %collective-permute-done.12.refs_1_.refs_7_.refs_9_ = bf16[256,2048]{1,0:T(8,128)(2,1)S(1)} collective-permute-done((bf16[256,2048]{1,0:T(8,128)(2,1)}, bf16[256,2048]{1,0:T(8,128)(2,1)S(1)}, u32[]{:S(2)}, u32[]{:S(2)}) %collective-permute-start.12) | collective-permute-done | bytes 1048608 | tf_op jit(solution)/shard_map/ppermute | solution.py:824
  185.9 1.5 collective-permute-start.15
  188.0 25.0 %experts_up.1 = (bf16[1280,4096]{1,0:T(8,128)(2,1)}, bf16[1280,4096]{1,0:T(8,128)(2,1)}) custom-call(s32[1]{0:T(128)} %bitcast.2.refs_0_, bf16[640,1024]{1,0:T(8,128)(2,1)} %get-tuple-element.72.refs_1_.refs_3_, bf16[640,1024]{1,0:T(8,128)(2,1)} %collective-permute-done.14.refs_2_.refs_4_, f32[1,4096]{1,0:T(1,128)} %dynamic-slice_bitcast_fusion.4.refs_3_, ...), custom_call_target="tpu_custom_call" | custom-call | flops 21474836480 | bytes 29360128 | tf_op jit(solution)/shard_map/experts_up/pallas_call | solution.py:44
  213.0 17.2 %experts_outer.1 = (bf16[4096,1024]{1,0:T(8,128)(2,1)}, f32[1,1024]{1,0:T(1,128)}) custom-call(bf16[1280,4096]{1,0:T(8,128)(2,1)} %get-tuple-element.75.refs_0_.refs_1_, bf16[640,1024]{1,0:T(8,128)(2,1)} %get-tuple-element.63.refs_3_.refs_1_, bf16[640,1024]{1,0:T(8,128)(2,1)} %copy-done.10), custom_call_target="tpu_custom_call" | custom-call | flops 21474836480 | bytes 18874368 | tf_op jit(solution)/shard_map/experts_outer/pallas_call | solution.py:44
  230.2 2.8 collective-permute-done.15.refs_0_.refs_3_.refs_12_
  234.4 3.2 cut_halves.5
  239.7 16.5 %down_near.1.refs_16_.refs_3_.refs_4_ = bf16[1280,1024]{1,0:T(8,128)(2,1)} custom-call(s32[1]{0:T(128)} %bitcast.2.refs_0_, bf16[1280,4096]{1,0:T(8,128)(2,1)} %get-tuple-element.75.refs_0_.refs_1_, bf16[1024,1024]{1,0:T(8,128)(2,1)} %later.8.refs_3_.refs_2_.refs_11_, bf16[1024,1024]{1,0:T(8,128)(2,1)} %copy-done.9, ...), custom_call_target="tpu_custom_call" | custom-call | flops 16106127360 | bytes 14155776 | tf_op jit(solution)/shard_map/down_near/pallas_call | solution.py:44
  256.3 5.4 %collective-permute-done.17.refs_14_.refs_1_.refs_2_ = bf16[1024,512]{1,0:T(8,128)(2,1)S(1)} collective-permute-done((bf16[1024,512]{1,0:T(8,128)(2,1)}, bf16[1024,512]{1,0:T(8,128)(2,1)S(1)}, u32[]{:S(2)}, u32[]{:S(2)}) %collective-permute-start.17) | collective-permute-done | bytes 1048608 | tf_op jit(solution)/shard_map/ppermute | solution.py:824
  263.8 50.9 %experts_grad.1 = (bf16[640,1024]{1,0:T(8,128)(2,1)}, bf16[640,1024]{1,0:T(8,128)(2,1)}, bf16[1024,4096]{1,0:T(8,128)(2,1)}, bf16[256,2048]{1,0:T(8,128)(2,1)}, ...) custom-call(s32[1]{0:T(128)} %bitcast.2.refs_0_, bf16[640,1024]{1,0:T(8,128)(2,1)} %get-tuple-element.63.refs_3_.refs_1_, ...), custom_call_target="tpu_custom_call" | custom-call | flops 64424509440 | bytes 35651584 | tf_op jit(solution)/shard_map/experts_grad/pallas_call | solution.py:44
  317.2 1.7 collective-permute-done.21.refs_3_
  320.0 14.8 %middle_grad.1 = (f32[1024,1024]{1,0:T(8,128)}, bf16[1024,512]{1,0:T(8,128)(2,1)}, bf16[1024,512]{1,0:T(8,128)(2,1)}, bf16[1024,1024]{1,0:T(8,128)(2,1)}, f32[1,...) custom-call(s32[1]{0:T(128)} %bitcast.3.refs_0_, s32[1024,1]{1,0:T(8,128)} %get-tuple-element.124.refs_1_.refs_0_, ...), custom_call_target="tpu_custom_call" | custom-call | flops 9663676416 | bytes 19398656 | tf_op jit(solution)/shard_map/middle_grad/pallas_call | solution.py:44
  335.0 21.6 %attention_backward.2.refs_5_.refs_1_ = bf16[3,1024,512]{2,1,0:T(8,128)(2,1)} custom-call(s32[1]{0:T(128)} %bitcast.18.refs_0_, s32[1024,1]{1,0:T(8,128)} %copy.140.refs_0_.refs_1_, s32[1,1024]{1,0:T(1,128)} %refs_2_.6, bf16[1024,3072]{1,0:T(8,128)(2,1)} %get-tuple-element.67.refs_2_.refs_3_.refs_4_.refs_5_, ...), custom_call_target="tpu_custom_call" | custom-call | flops 25769803776 | bytes 8388608 | tf_op jit(solution)/shard_map/attention_backward/pallas_call | solution.py:44
  357.6 2.2 collective-permute-done.20.refs_4_
  360.8 5.4 %far_add.2 = (bf16[256,4096]{1,0:T(8,128)(2,1)}, bf16[256,4096]{1,0:T(8,128)(2,1)}) custom-call(s32[1]{0:T(128)} %bitcast.2.refs_0_, bf16[4,256,4096]{2,1,0:T(8,128)(2,1)} %bitcast.86, bf16[4,256,4096]{2,1,0:T(8,128)(2,1)} %bitcast.87, bf16[256,2048]{1,0:T(8,128)(2,1)} %copy-done.11, bf16[256,2048]{1,0:T(8,128)(2,1)} %copy-done.12, ...), custom_call_target="tpu_custom_call" | custom-call | tf_op jit(solution)/shard_map/far_add/pallas_call | solution.py:44
  368.6 6.7 %two_sum.2 = (bf16[1024,2048]{1,0:T(8,128)(2,1)}, bf16[256,1024]{1,0:T(8,128)(2,1)}, bf16[256,1024]{1,0:T(8,128)(2,1)}) custom-call(s32[1]{0:T(128)} %bitcast.2.refs_0_, bf16[1024,1024]{1,0:T(8,128)(2,1)} %get-tuple-element.68.refs_2_.refs_3_.refs_1_, bf16[1,1024,512]{2,1,0:T(8,128)(2,1)} %bitcast.132, bf16[1024,1024]{1,0:T(8,128)(2,1)} %collective-permute-done.24.refs_3_, ...), custom_call_target="tpu_custom_call" | custom-call | flops 4294967296 | bytes 6291456 | tf_op jit(solution)/shard_map/two_sum/pallas_call | solution.py:490
  375.3 21.6 %attention_backward.3.refs_2_.refs_0_ = bf16[3,1024,512]{2,1,0:T(8,128)(2,1)} custom-call(s32[1]{0:T(128)} %bitcast.19.refs_0_, s32[1024,1]{1,0:T(8,128)} %copy.140.refs_0_.refs_1_, s32[1,1024]{1,0:T(1,128)} %refs_2_.6, bf16[1024,3072]{1,0:T(8,128)(2,1)} %get-tuple-element.67.refs_2_.refs_3_.refs_4_.refs_5_, ...), custom_call_target="tpu_custom_call" | custom-call | flops 25769803776 | bytes 8388608 | tf_op jit(solution)/shard_map/attention_backward/pallas_call | solution.py:44
  397.0 12.5 %two_sum.3 = (bf16[1024,2048]{1,0:T(8,128)(2,1)}, bf16[256,1024]{1,0:T(8,128)(2,1)}, bf16[256,1024]{1,0:T(8,128)(2,1)}) custom-call(s32[1]{0:T(128)} %bitcast.2.refs_0_, bf16[1024,1024]{1,0:T(8,128)(2,1)} %get-tuple-element.71.refs_1_, ...), custom_call_target="tpu_custom_call", output_to_operand_aliasing={{0}: (5, {}), {1}: (6, {}), {2}: (7, {})} | custom-call | flops 12884901888 | bytes 10485760 | tf_op jit(solution)/shard_map/two_sum/pallas_call | solution.py:490
  409.5 4.1 collective-permute-done.22.refs_2_
  414.0 4.8 near_add.2.refs_5_
  426.3 8.1 %down_far.1 = (bf16[640,1024]{1,0:T(8,128)(2,1)}, bf16[640,1024]{1,0:T(8,128)(2,1)}) custom-call(s32[1]{0:T(128)} %bitcast.2.refs_0_, bf16[1280,4096]{1,0:T(8,128)(2,1)} %get-tuple-element.75.refs_0_.refs_1_, bf16[1024,512]{1,0:T(8,128)(2,1)} %copy-done.17, bf16[1024,512]{1,0:T(8,128)(2,1)} %copy-done.18, ...), custom_call_target="tpu_custom_call" | custom-call | flops 5368709120 | bytes 7864320 | tf_op jit(solution)/shard_map/down_far/pallas_call | solution.py:44
  434.4 2.2 collective-permute-done.28.refs_3_
  437.8 4.2 far_add.3
  443.6 14.6 %input_grad.1 = (f32[1024,1024]{1,0:T(8,128)}, f32[1,1024]{1,0:T(1,128)}, f32[1,1024]{1,0:T(1,128)}, f32[4,512]{1,0:T(4,128)}) custom-call(bf16[3,1024,512]{2,1,0:T(8,128)(2,1)} %attention_backward.3.refs_2_.refs_0_, bf16[3,1024,512]{2,1,0:T(8,128)(2,1)} %attention_backward.2.refs_5_.refs_1_, bf16[1024,1024]{1,0:T(8,128)(2,1)} %refs_2_.7, ...), custom_call_target="tpu_custom_call" | custom-call | flops 12884901888 | bytes 23068672 | tf_op jit(solution)/shard_map/input_grad/pallas_call | solution.py:44
  458.2 7.2 %collective-permute-done.30.refs_2_ = bf16[256,2048]{1,0:T(8,128)(2,1)S(1)} collective-permute-done((bf16[256,2048]{1,0:T(8,128)(2,1)}, bf16[256,2048]{1,0:T(8,128)(2,1)S(1)}, u32[]{:S(2)}, u32[]{:S(2)}) %collective-permute-start.30) | collective-permute-done | bytes 1048608 | tf_op jit(solution)/shard_map/ppermute | solution.py:824
  466.8 3.9 near_add.3.refs_1_
  475.6 2.9 all-to-all-start.1
  478.4 2.5 maximum_select_fusion.refs_2_
  480.9 5.4 %all-to-all-done.1 = f32[32,1,384]{2,1,0:T(1,128)S(1)} async-done(((f32[32,1,384]{2,1,0:T(1,128)}), f32[32,1,384]{2,1,0:T(1,128)S(1)}, u32[]{:S(2)}, u32[]{:S(2)}) %all-to-all-start.1) | async-done | bytes 49184 | tf_op jit(solution)/shard_map/all_to_all | solution.py:1111
  488.2 8.0 %output.1.refs_1_ = bf16[1024,1024]{1,0:T(8,128)(2,1)} custom-call(s32[1024,1]{1,0:T(8,128)} %get-tuple-element.124.refs_1_.refs_0_, s32[1024,1]{1,0:T(8,128)} %copy.144.refs_1_, bf16[640,1024]{1,0:T(8,128)(2,1)} %get-tuple-element.95.refs_5_.refs_2_, bf16[640,1024]{1,0:T(8,128)(2,1)} %collective-permute-done.27.refs_3_, ...), custom_call_target="tpu_custom_call" | custom-call | flops 5368709120 | bytes 8912896 | tf_op jit(solution)/shard_map/output/pallas_call | solution.py:44
  497.3 2.5 maximum_select_fusion.1.refs_3_
  (277 shorter events, 79.3 us)
Async XLA Ops:
  7.2 37.5 %all-gather.4.cloned.1.call-start = ((), (), s32[]{:S(2)}) async-start(), calls=%async_computation.6 | async-start | bytes 1310720 | tf_op jit(solution)/shard_map/all_gather | solution.py:899
  10.1 1.5 collective-permute-start
  14.0 79.3 %all-gather.6.cloned.1.call-start = ((), (), s32[]{:S(2)}) async-start(), calls=%async_computation.7 | async-start | bytes 2621440 | tf_op jit(solution)/shard_map/all_gather | solution.py:899
  15.5 12.1 %collective-permute-start.2 = (bf16[32,4096]{1,0:T(8,128)(2,1)S(1)}, bf16[32,4096]{1,0:T(8,128)(2,1)S(1)}, u32[]{:S(2)}, u32[]{:S(2)}) collective-permute-start(bf16[32,4096]{1,0:T(8,128)(2,1)S(1)} %bitcast.118), channel_id=1, source_target_pairs={{0,1},{1,0},{2,3},{3,2},{4,5},{5,4},{6,7},{7,6},{8,9},{9,8},{10,11... | collective-permute-start | bytes 786440 | tf_op jit(solution)/shard_map/ppermute | solution.py:824
  31.3 1.6 collective-permute-start.1
  44.7 32.4 %copy-start.40 = (bf16[32]{0:T(256)(128)(2,1)S(1)}, bf16[32]{0:T(256)(128)(2,1)}, u32[]{:S(2)}) copy-start(bf16[32]{0:T(256)(128)(2,1)} %param.23) | copy-start | bytes 196
  44.7 32.4 %copy-start.41 = (bf16[32]{0:T(256)(128)(2,1)S(1)}, bf16[32]{0:T(256)(128)(2,1)}, u32[]{:S(2)}) copy-start(bf16[32]{0:T(256)(128)(2,1)} %param.24) | copy-start | bytes 196
  44.7 32.5 %copy-start.42 = (bf16[32]{0:T(256)(128)(2,1)S(1)}, bf16[32]{0:T(256)(128)(2,1)}, u32[]{:S(2)}) copy-start(bf16[32]{0:T(256)(128)(2,1)} %param.26) | copy-start | bytes 196
  44.8 25.0 %collective-permute-start.3 = (bf16[256,2048]{1,0:T(8,128)(2,1)}, bf16[256,2048]{1,0:T(8,128)(2,1)S(1)}, u32[]{:S(2)}, u32[]{:S(2)}) collective-permute-start(bf16[256,2048]{1,0:T(8,128)(2,1)} %later.7.refs_1_), channel_id=1, source_target_pairs={{0,8},{8,0},{16,24},{24,16},{1,9},{9,1},{17,25},{25,17},{2,10},{10... | collective-permute-start | bytes 3145736 | tf_op jit(solution)/shard_map/ppermute | solution.py:824
  46.3 24.7 %collective-permute-start.4 = (bf16[256,2048]{1,0:T(8,128)(2,1)}, bf16[256,2048]{1,0:T(8,128)(2,1)S(1)}, u32[]{:S(2)}, u32[]{:S(2)}) collective-permute-start(bf16[256,2048]{1,0:T(8,128)(2,1)} %later.7.refs_1_), channel_id=1, source_target_pairs={{0,16},{8,24},{16,0},{24,8},{1,17},{9,25},{17,1},{25,9},{2,18},{10... | collective-permute-start | bytes 3145736 | tf_op jit(solution)/shard_map/ppermute | solution.py:824
  47.8 43.4 %collective-permute-start.7 = (bf16[640,1024]{1,0:T(8,128)(2,1)}, bf16[640,1024]{1,0:T(8,128)(2,1)S(1)}, u32[]{:S(2)}, u32[]{:S(2)}) collective-permute-start(bf16[640,1024]{1,0:T(8,128)(2,1)} %get-tuple-element.66), channel_id=1, source_target_pairs={{0,1},{1,0},{2,3},{3,2},{4,5},{5,4},{6,7},{7,6},{8,9},{9,8},{10,11... | collective-permute-start | bytes 3932168 | tf_op jit(solution)/shard_map/ppermute | solution.py:824
  74.3 16.9 %collective-permute-start.5 = (bf16[256,1024]{1,0:T(8,128)(2,1)}, bf16[256,1024]{1,0:T(8,128)(2,1)S(1)}, u32[]{:S(2)}, u32[]{:S(2)}) collective-permute-start(bf16[256,1024]{1,0:T(8,128)(2,1)} %get-tuple-element.64), channel_id=1, source_target_pairs={{0,16},{8,24},{16,0},{24,8},{1,17},{9,25},{17,1},{25,9},{2,18},{10... | collective-permute-start | bytes 1572872 | tf_op jit(solution)/shard_map/ppermute | solution.py:824
  75.8 15.4 %collective-permute-start.6 = (bf16[256,1024]{1,0:T(8,128)(2,1)}, bf16[256,1024]{1,0:T(8,128)(2,1)S(1)}, u32[]{:S(2)}, u32[]{:S(2)}) collective-permute-start(bf16[256,1024]{1,0:T(8,128)(2,1)} %get-tuple-element.65), channel_id=1, source_target_pairs={{0,8},{8,0},{16,24},{24,16},{1,9},{9,1},{17,25},{25,17},{2,10},{10... | collective-permute-start | bytes 1572872 | tf_op jit(solution)/shard_map/ppermute | solution.py:824
  79.5 10.7 %all-to-all-start = ((bf16[32,2,272]{2,1,0:T(2,128)(2,1)}), bf16[32,2,272]{2,1,0:T(2,128)(2,1)S(1)}, u32[]{:S(2)}, u32[]{:S(2)}) async-start(bf16[32,2,272]{2,1,0:T(2,128)(2,1)} %reshape.323), calls=%async_computation | async-start | bytes 98304 | tf_op jit(solution)/shard_map/all_to_all | solution.py:993
  82.3 92.9 %all-gather.8.cloned.1.call-start = ((), (), s32[]{:S(2)}) async-start(), calls=%async_computation.8 | async-start | bytes 2621440 | tf_op jit(solution)/shard_map/all_gather | solution.py:899
  98.0 7.5 %collective-permute-start.8 = (bf16[1024,2048]{1,0:T(8,128)(2,1)}, bf16[1024,2048]{1,0:T(8,128)(2,1)}, u32[]{:S(2)}, u32[]{:S(2)}) collective-permute-start(bf16[1024,2048]{1,0:T(8,128)(2,1)} %bitcast.97), channel_id=1, source_target_pairs={{0,1},{1,0},{2,3},{3,2},{4,5},{5,4},{6,7},{7,6},{8,9},{9,8},{10,11... | collective-permute-start | bytes 12582920 | tf_op jit(solution)/shard_map/ppermute | solution.py:824
  101.3 264.9 %reduce-scatter.5.cloned.1.call-start = ((), (), s32[]{:S(2)}) async-start(), calls=%async_computation.9 | async-start | bytes 10485760 | tf_op jit(solution)/shard_map/reduce_scatter | solution.py:1055
  101.5 49.7 %collective-permute-start.10 = (bf16[256,4096]{1,0:T(8,128)(2,1)}, bf16[256,4096]{1,0:T(8,128)(2,1)S(1)}, u32[]{:S(2)}, u32[]{:S(2)}) collective-permute-start(bf16[256,4096]{1,0:T(8,128)(2,1)} %all-gather.6.cloned.1.call-done.refs_6_.refs_7_.refs_4_), channel_id=1, source_target_pairs={{0,16},{8,24},{16,0},{24,8},{1,17},{9,25},{17,1},{25,9},{2,18},{10... | collective-permute-start | bytes 6291464 | tf_op jit(solution)/shard_map/ppermute | solution.py:824
  103.1 48.2 %collective-permute-start.9 = (bf16[256,4096]{1,0:T(8,128)(2,1)}, bf16[256,4096]{1,0:T(8,128)(2,1)S(1)}, u32[]{:S(2)}, u32[]{:S(2)}) collective-permute-start(bf16[256,4096]{1,0:T(8,128)(2,1)} %all-gather.6.cloned.1.call-done.refs_6_.refs_7_.refs_4_), channel_id=1, source_target_pairs={{0,8},{8,0},{16,24},{24,16},{1,9},{9,1},{17,25},{25,17},{2,10},{10... | collective-permute-start | bytes 6291464 | tf_op jit(solution)/shard_map/ppermute | solution.py:824
  118.4 43.1 %collective-permute-start.11 = (bf16[1024,1024]{1,0:T(8,128)(2,1)}, bf16[1024,1024]{1,0:T(8,128)(2,1)}, u32[]{:S(2)}, u32[]{:S(2)}) collective-permute-start(bf16[1024,1024]{1,0:T(8,128)(2,1)} %get-tuple-element.71.refs_1_), channel_id=1, source_target_pairs={{0,1},{1,0},{2,3},{3,2},{4,5},{5,4},{6,7},{7,6},{8,9},{9,8},{10,11... | collective-permute-start | bytes 6291464 | tf_op jit(solution)/shard_map/ppermute | solution.py:824
  156.5 25.7 %collective-permute-start.12 = (bf16[256,2048]{1,0:T(8,128)(2,1)}, bf16[256,2048]{1,0:T(8,128)(2,1)S(1)}, u32[]{:S(2)}, u32[]{:S(2)}) collective-permute-start(bf16[256,2048]{1,0:T(8,128)(2,1)} %get-tuple-element.69.refs_9_), channel_id=1, source_target_pairs={{0,16},{8,24},{16,0},{24,8},{1,17},{9,25},{17,1},{25,9},{2,18},{10... | collective-permute-start | bytes 3145736 | tf_op jit(solution)/shard_map/ppermute | solution.py:824
  157.9 25.4 %collective-permute-start.13 = (bf16[256,2048]{1,0:T(8,128)(2,1)}, bf16[256,2048]{1,0:T(8,128)(2,1)S(1)}, u32[]{:S(2)}, u32[]{:S(2)}) collective-permute-start(bf16[256,2048]{1,0:T(8,128)(2,1)} %get-tuple-element.70.refs_10_), channel_id=1, source_target_pairs={{0,8},{8,0},{16,24},{24,16},{1,9},{9,1},{17,25},{25,17},{2,10},{10... | collective-permute-start | bytes 3145736 | tf_op jit(solution)/shard_map/ppermute | solution.py:824
  184.3 3.7 collective-permute-start.14
  185.9 47.2 %collective-permute-start.15 = (bf16[1024,1024]{1,0:T(8,128)(2,1)S(1)}, bf16[1024,1024]{1,0:T(8,128)(2,1)S(1)}, u32[]{:S(2)}, u32[]{:S(2)}) collective-permute-start(bf16[1024,1024]{1,0:T(8,128)(2,1)S(1)} %copy-done), channel_id=1, source_target_pairs={{0,8},{8,0},{16,24},{24,16},{1,9},{9,1},{17,25},{25,17},{2,10},{10... | collective-permute-start | bytes 6291464 | tf_op jit(solution)/shard_map/ppermute | solution.py:824
  187.4 47.0 %collective-permute-start.16 = (bf16[1024,1024]{1,0:T(8,128)(2,1)S(1)}, bf16[1024,1024]{1,0:T(8,128)(2,1)}, u32[]{:S(2)}, u32[]{:S(2)}) collective-permute-start(bf16[1024,1024]{1,0:T(8,128)(2,1)S(1)} %copy-done), channel_id=1, source_target_pairs={{0,16},{8,24},{16,0},{24,8},{1,17},{9,25},{17,1},{25,9},{2,18},{10... | collective-permute-start | bytes 6291464 | tf_op jit(solution)/shard_map/ppermute | solution.py:824
  237.6 24.1 %collective-permute-start.17 = (bf16[1024,512]{1,0:T(8,128)(2,1)}, bf16[1024,512]{1,0:T(8,128)(2,1)S(1)}, u32[]{:S(2)}, u32[]{:S(2)}) collective-permute-start(bf16[1024,512]{1,0:T(8,128)(2,1)} %get-tuple-element.77.refs_5_), channel_id=1, source_target_pairs={{0,16},{8,24},{16,0},{24,8},{1,17},{9,25},{17,1},{25,9},{2,18},{10... | collective-permute-start | bytes 3145736 | tf_op jit(solution)/shard_map/ppermute | solution.py:824
  238.2 23.8 %collective-permute-start.18 = (bf16[1024,512]{1,0:T(8,128)(2,1)}, bf16[1024,512]{1,0:T(8,128)(2,1)S(1)}, u32[]{:S(2)}, u32[]{:S(2)}) collective-permute-start(bf16[1024,512]{1,0:T(8,128)(2,1)} %get-tuple-element.78.refs_6_), channel_id=1, source_target_pairs={{0,8},{8,0},{16,24},{24,16},{1,9},{9,1},{17,25},{25,17},{2,10},{10... | collective-permute-start | bytes 3145736 | tf_op jit(solution)/shard_map/ppermute | solution.py:824
  263.7 150.3 %reduce-scatter.7.cloned.1.call-start = ((), (), s32[]{:S(2)}) async-start(), calls=%async_computation.10 | async-start | bytes 2621440 | tf_op jit(solution)/shard_map/reduce_scatter | solution.py:903
  263.8 51.0 %copy-start.3 = (bf16[1024,1024]{1,0:T(8,128)(2,1)S(1)}, bf16[1024,1024]{1,0:T(8,128)(2,1)}, u32[]{:S(2)}) copy-start(bf16[1024,1024]{1,0:T(8,128)(2,1)} %get-tuple-element.68.refs_2_.refs_3_.refs_1_) | copy-start | bytes 6291460
  314.7 4.3 collective-permute-start.21
  314.8 52.9 %collective-permute-start.24 = (bf16[1024,1024]{1,0:T(8,128)(2,1)S(1)}, bf16[1024,1024]{1,0:T(8,128)(2,1)}, u32[]{:S(2)}, u32[]{:S(2)}) collective-permute-start(bf16[1024,1024]{1,0:T(8,128)(2,1)S(1)} %copy-done.3), channel_id=1, source_target_pairs={{0,1},{1,0},{2,3},{3,2},{4,5},{5,4},{6,7},{7,6},{8,9},{9,8},{10,11... | collective-permute-start | bytes 6291464 | tf_op jit(solution)/shard_map/ppermute | solution.py:824
  315.3 42.4 %collective-permute-start.19 = (bf16[256,2048]{1,0:T(8,128)(2,1)}, bf16[256,2048]{1,0:T(8,128)(2,1)S(1)}, u32[]{:S(2)}, u32[]{:S(2)}) collective-permute-start(bf16[256,2048]{1,0:T(8,128)(2,1)} %get-tuple-element.81), channel_id=1, source_target_pairs={{0,8},{8,0},{16,24},{24,16},{1,9},{9,1},{17,25},{25,17},{2,10},{10... | collective-permute-start | bytes 3145736 | tf_op jit(solution)/shard_map/ppermute | solution.py:824
  316.5 43.3 %collective-permute-start.20 = (bf16[256,2048]{1,0:T(8,128)(2,1)}, bf16[256,2048]{1,0:T(8,128)(2,1)S(1)}, u32[]{:S(2)}, u32[]{:S(2)}) collective-permute-start(bf16[256,2048]{1,0:T(8,128)(2,1)} %get-tuple-element.82), channel_id=1, source_target_pairs={{0,16},{8,24},{16,0},{24,8},{1,17},{9,25},{17,1},{25,9},{2,18},{10... | collective-permute-start | bytes 3145736 | tf_op jit(solution)/shard_map/ppermute | solution.py:824
  334.8 32.8 %collective-permute-start.25 = (bf16[1024,512]{1,0:T(8,128)(2,1)}, bf16[1024,512]{1,0:T(8,128)(2,1)S(1)}, u32[]{:S(2)}, u32[]{:S(2)}) collective-permute-start(bf16[1024,512]{1,0:T(8,128)(2,1)} %get-tuple-element.90), channel_id=1, source_target_pairs={{0,1},{1,0},{2,3},{3,2},{4,5},{5,4},{6,7},{7,6},{8,9},{9,8},{10,11... | collective-permute-start | bytes 3145736 | tf_op jit(solution)/shard_map/ppermute | solution.py:824
  356.6 40.4 %collective-permute-start.26 = (bf16[3,1024,512]{2,1,0:T(8,128)(2,1)}, bf16[3,1024,512]{2,1,0:T(8,128)(2,1)}, u32[]{:S(2)}, u32[]{:S(2)}) collective-permute-start(bf16[3,1024,512]{2,1,0:T(8,128)(2,1)} %attention_backward.2.refs_5_.refs_1_), channel_id=1, source_target_pairs={{0,1},{1,0},{2,3},{3,2},{4,5},{5,4},{6,7},{7,6},{8,9},{9,8},{10,11... | collective-permute-start | bytes 9437192 | tf_op jit(solution)/shard_map/ppermute | solution.py:824
  366.2 120.3 %reduce-scatter.11.cloned.1.call-start = ((), (), s32[]{:S(2)}) async-start(), calls=%async_computation.12 | async-start | bytes 2621440 | tf_op jit(solution)/shard_map/reduce_scatter | solution.py:903
  366.3 47.2 %collective-permute-start.22 = (bf16[256,4096]{1,0:T(8,128)(2,1)}, bf16[256,4096]{1,0:T(8,128)(2,1)}, u32[]{:S(2)}, u32[]{:S(2)}) collective-permute-start(bf16[256,4096]{1,0:T(8,128)(2,1)} %get-tuple-element.87.refs_5_.refs_1_), channel_id=1, source_target_pairs={{0,8},{8,0},{16,24},{24,16},{1,9},{9,1},{17,25},{25,17},{2,10},{10... | collective-permute-start | bytes 6291464 | tf_op jit(solution)/shard_map/ppermute | solution.py:824
  366.6 47.4 %collective-permute-start.23 = (bf16[256,4096]{1,0:T(8,128)(2,1)}, bf16[256,4096]{1,0:T(8,128)(2,1)}, u32[]{:S(2)}, u32[]{:S(2)}) collective-permute-start(bf16[256,4096]{1,0:T(8,128)(2,1)} %get-tuple-element.88.refs_6_.refs_2_), channel_id=1, source_target_pairs={{0,16},{8,24},{16,0},{24,8},{1,17},{9,25},{17,1},{25,9},{2,18},{10... | collective-permute-start | bytes 6291464 | tf_op jit(solution)/shard_map/ppermute | solution.py:824
  419.0 80.8 %reduce-scatter.9.cloned.1.call-start = ((), (), s32[]{:S(2)}) async-start(), calls=%async_computation.11 | async-start | bytes 1310720 | tf_op jit(solution)/shard_map/reduce_scatter | solution.py:903
  424.1 12.5 %collective-permute-start.28 = (bf16[256,1024]{1,0:T(8,128)(2,1)S(1)}, bf16[256,1024]{1,0:T(8,128)(2,1)S(1)}, u32[]{:S(2)}, u32[]{:S(2)}) collective-permute-start(bf16[256,1024]{1,0:T(8,128)(2,1)S(1)} %copy-done.19), channel_id=1, source_target_pairs={{0,8},{8,0},{16,24},{24,16},{1,9},{9,1},{17,25},{25,17},{2,10},{10... | collective-permute-start | bytes 1572872 | tf_op jit(solution)/shard_map/ppermute | solution.py:824
  425.3 11.6 %collective-permute-start.29 = (bf16[256,1024]{1,0:T(8,128)(2,1)S(1)}, bf16[256,1024]{1,0:T(8,128)(2,1)S(1)}, u32[]{:S(2)}, u32[]{:S(2)}) collective-permute-start(bf16[256,1024]{1,0:T(8,128)(2,1)S(1)} %copy-done.49), channel_id=1, source_target_pairs={{0,16},{8,24},{16,0},{24,8},{1,17},{9,25},{17,1},{25,9},{2,18},{10... | collective-permute-start | bytes 1572872 | tf_op jit(solution)/shard_map/ppermute | solution.py:824
  426.2 47.5 %collective-permute-start.32 = (f32[128,1024]{1,0:T(8,128)S(1)}, f32[128,1024]{1,0:T(8,128)S(1)}, u32[]{:S(2)}, u32[]{:S(2)}) collective-permute-start(f32[128,1024]{1,0:T(8,128)S(1)} %get-tuple-element.116), channel_id=1, source_target_pairs={{0,1},{1,0},{2,3},{3,2},{4,5},{5,4},{6,7},{7,6},{8,9},{9,8},{10,11... | collective-permute-start | bytes 1572872 | tf_op jit(solution)/shard_map/ppermute | solution.py:824
  441.9 23.4 %collective-permute-start.30 = (bf16[256,2048]{1,0:T(8,128)(2,1)}, bf16[256,2048]{1,0:T(8,128)(2,1)S(1)}, u32[]{:S(2)}, u32[]{:S(2)}) collective-permute-start(bf16[256,2048]{1,0:T(8,128)(2,1)} %get-tuple-element.100.refs_7_), channel_id=1, source_target_pairs={{0,8},{8,0},{16,24},{24,16},{1,9},{9,1},{17,25},{25,17},{2,10},{10... | collective-permute-start | bytes 3145736 | tf_op jit(solution)/shard_map/ppermute | solution.py:824
  443.3 22.5 %collective-permute-start.31 = (bf16[256,2048]{1,0:T(8,128)(2,1)}, bf16[256,2048]{1,0:T(8,128)(2,1)S(1)}, u32[]{:S(2)}, u32[]{:S(2)}) collective-permute-start(bf16[256,2048]{1,0:T(8,128)(2,1)} %get-tuple-element.101.refs_8_), channel_id=1, source_target_pairs={{0,16},{8,24},{16,0},{24,8},{1,17},{9,25},{17,1},{25,9},{2,18},{10... | collective-permute-start | bytes 3145736 | tf_op jit(solution)/shard_map/ppermute | solution.py:824
  443.6 44.6 %collective-permute-start.27 = (bf16[640,1024]{1,0:T(8,128)(2,1)S(1)}, bf16[640,1024]{1,0:T(8,128)(2,1)}, u32[]{:S(2)}, u32[]{:S(2)}) collective-permute-start(bf16[640,1024]{1,0:T(8,128)(2,1)S(1)} %copy-done.46), channel_id=1, source_target_pairs={{0,1},{1,0},{2,3},{3,2},{4,5},{5,4},{6,7},{7,6},{8,9},{9,8},{10,11... | collective-permute-start | bytes 3932168 | tf_op jit(solution)/shard_map/ppermute | solution.py:824
  475.6 10.8 %all-to-all-start.1 = ((f32[32,1,384]{2,1,0:T(1,128)}), f32[32,1,384]{2,1,0:T(1,128)S(1)}, u32[]{:S(2)}, u32[]{:S(2)}) async-start(f32[32,1,384]{2,1,0:T(1,128)} %copy.145), calls=%async_computation.3 | async-start | bytes 98304 | tf_op jit(solution)/shard_map/all_to_all | solution.py:1111
  487.8 9.0 %collective-permute-start.33 = (f32[32,4096]{1,0:T(8,128)S(1)}, f32[32,4096]{1,0:T(8,128)S(1)}, u32[]{:S(2)}, u32[]{:S(2)}) collective-permute-start(f32[32,4096]{1,0:T(8,128)S(1)} %get-tuple-element.114), channel_id=1, source_target_pairs={{0,1},{1,0},{2,3},{3,2},{4,5},{5,4},{6,7},{7,6},{8,9},{9,8},{10,11... | collective-permute-start | bytes 1572872 | tf_op jit(solution)/shard_map/ppermute | solution.py:824
  500.8 2.3 collective-permute-start.34
  (47 other events, 292.2 us)
Sparse Core Ops, SparseCore 0:
  14.1 30.5 all-gather.3
  46.8 46.4 all-gather.5
  101.4 44.8 all-gather.7
  263.8 101.5 reduce-scatter.4
  367.7 40.6 reduce-scatter.6
  419.1 41.2 reduce-scatter.10
  470.9 25.8 reduce-scatter.8

commit v3 on v2

--- a/solution.py
+++ b/solution.py
@@ -87,22 +87,31 @@
         fill_bias(bias, seg_col, seg_row, blocks)
 
     lane = lax.broadcasted_iota(jnp.int32, (TILE_Q, PAIR), 1)
-    for masked, (start, low, high) in zip(bias, blocks):
+    work = [(block, head) for block in range(len(blocks)) for head in range(2)]
+
+    def raw_scores(block, head):
+        start, low, high = blocks[block]
+        q = q_ref[start : start + TILE_Q, :] * jnp.asarray(HEAD_DIM**-0.5, bf16)
+        mine = (lane < HEAD_DIM) == (head == 0)
+        return dot(k_ref[low:high, :], jnp.where(mine, q, jnp.zeros_like(q)), NT)
+
+    coming, heads = raw_scores(*work[0]), []
+    for number, (block, head) in enumerate(work):
+        start, low, high = blocks[block]
         rows = slice(start, start + TILE_Q)
-        q = q_ref[rows, :] * jnp.asarray(HEAD_DIM**-0.5, bf16)
-        k = k_ref[low:high, :]
-        v = v_ref[low:high, :]
-        heads = []
-        for head in range(2):
-            mine = (lane < HEAD_DIM) == (head == 0)
-            scores = dot(k, jnp.where(mine, q, jnp.zeros_like(q)), NT) + masked[...]
-            top = jnp.max(scores, 0, keepdims=True)
-            probs = jnp.exp(scores - top)
-            total = jnp.sum(probs, 0, keepdims=True)
-            out = dot(v, probs.astype(bf16), TN)
-            heads.append(out[head * HEAD_DIM : (head + 1) * HEAD_DIM] * (1.0 / total))
-            lse_ref[0, head : head + 1, rows] = top + jnp.log(total)
-        o_ref[rows, :] = jnp.concatenate(heads, 0).T.astype(bf16)
+        raw = coming
+        if number + 1 < len(work):
+            coming = raw_scores(*work[number + 1])
+        scores = raw + bias[block][...]
+        top = jnp.max(scores, 0, keepdims=True)
+        probs = jnp.exp(scores - top)
+        total = jnp.sum(probs, 0, keepdims=True)
+        out = dot(v_ref[low:high, :], probs.astype(bf16), TN)
+        heads.append(out[head * HEAD_DIM : (head + 1) * HEAD_DIM] * (1.0 / total))
+        lse_ref[0, head : head + 1, rows] = top + jnp.log(total)
+        if head == 1:
+            o_ref[rows, :] = jnp.concatenate(heads, 0).T.astype(bf16)
+            heads = []
 
 
 def attention(qkv, seg_col, seg_row, after=()):
@@ -140,29 +149,34 @@
     dv_sum[...] = jnp.zeros_like(dv_sum)
     lane = lax.broadcasted_iota(jnp.int32, (TILE_Q, PAIR), 1)
     scale = HEAD_DIM**-0.5
-    for masked, (start, low, high) in zip(bias, blocks):
+    work = [(block, head) for block in range(len(blocks)) for head in range(2)]
+
+    def products(block, head):
+        start, low, high = blocks[block]
         rows = slice(start, start + TILE_Q)
-        q = q_ref[rows, :]
-        do = do_ref[rows, :]
-        k = k_ref[low:high, :]
-        v = v_ref[low:high, :]
-        scaled = q * jnp.asarray(scale, bf16)
-        zero = jnp.zeros_like(q)
-        dq, dk, dv = [], 0.0, 0.0
-        for head in range(2):
-            mine = (lane < HEAD_DIM) == (head == 0)
-            do_head = jnp.where(mine, do, zero)
-            scores = dot(k, jnp.where(mine, scaled, zero), NT) + masked[...]
-            probs = jnp.exp(scores - lse_ref[0, head : head + 1, rows])
-            weighted = probs * dot(v, do_head, NT)
-            total = jnp.sum(weighted, 0, keepdims=True)
-            ds = ((weighted - probs * total) * scale).astype(bf16)
-            dv = dv + dot(probs.astype(bf16), do_head)
-            dk = dk + dot(ds, jnp.where(mine, q, zero))
-            dq.append(dot(k, ds, TN)[head * HEAD_DIM : (head + 1) * HEAD_DIM])
-        d_ref[0, rows, :] = jnp.concatenate(dq, 0).T.astype(bf16)
-        dk_sum[low:high, :] += dk
-        dv_sum[low:high, :] += dv
+        mine = (lane < HEAD_DIM) == (head == 0)
+        zero = jnp.zeros((TILE_Q, PAIR), bf16)
+        q = jnp.where(mine, q_ref[rows, :] * jnp.asarray(scale, bf16), zero)
+        do = jnp.where(mine, do_ref[rows, :], zero)
+        return q, do, dot(k_ref[low:high, :], q, NT), dot(v_ref[low:high, :], do, NT)
+
+    coming, dq = products(*work[0]), []
+    for number, (block, head) in enumerate(work):
+        start, low, high = blocks[block]
+        rows = slice(start, start + TILE_Q)
+        q, do, raw, grad = coming
+        if number + 1 < len(work):
+            coming = products(*work[number + 1])
+        probs = jnp.exp(raw + bias[block][...] - lse_ref[0, head : head + 1, rows])
+        weighted = probs * grad
+        total = jnp.sum(weighted, 0, keepdims=True)
+        ds = (weighted - probs * total).astype(bf16)
+        dv_sum[low:high, :] += dot(probs.astype(bf16), do)
+        dk_sum[low:high, :] += dot(ds, q)
+        dq.append(dot(k_ref[low:high, :], ds, TN)[head * HEAD_DIM : (head + 1) * HEAD_DIM] * scale)
+        if head == 1:
+            d_ref[0, rows, :] = jnp.concatenate(dq, 0).T.astype(bf16)
+            dq = []
     d_ref[1, ...] = dk_sum[...].astype(bf16)
     d_ref[2, ...] = dv_sum[...].astype(bf16)
 
@@ -223,40 +237,46 @@
     return (mine, core[0]), (other, 1 - core[0])
 
 
-def project_kernel(core, x_ref, gain, shift, bias, mine_w, other_w, a_ref, qkv_ref):
+def project_kernel(core, me, x_ref, gain, shift, bias, *refs):
+    pieces, (a_ref, qkv_ref) = refs[:10], refs[10:]
     half = x_ref.shape[1] // 2
     normed, _ = norm_parts(x_ref[...].astype(f32))
-    a = (normed * gain[...] + shift[...]).astype(bf16)
-    a_ref[...] = a
-    for w, side in sides(core, mine_w, other_w):
-        out = dot(a, w[...])
-        for j in range(3):
+    a_ref[...] = (normed * gain[...] + shift[...]).astype(bf16)
+    depth = pieces[0].shape[0]
+    for ws, side in sides(core, pieces[:5], pieces[5:]):
+        first, second = 0.0, 0.0
+        for r in range(4):
+            a = a_ref[:, pl.ds(pl.multiple_of((me[0] ^ r) * depth, depth), depth)]
+            first = first + dot(a, ws[r][:, : 2 * half])
+            second = second + dot(a, ws[4][...] if r == 3 else ws[r][:, 2 * half :])
+        for j, out in enumerate((first[:, :half], first[:, half:], second)):
             at = pl.ds(pl.multiple_of(2 * half * j + half * side, half), half)
-            qkv_ref[:, at] = (out[:, half * j : half * (j + 1)] + bias[:, at]).astype(bf16)
-
-
-def project(core, x, gain, shift, bias, mine_w, other_w, after=()):
+            qkv_ref[:, at] = (out + bias[:, at]).astype(bf16)
+
+
+def project(core, me, x, gain, shift, bias, mine_w, other_w, after=()):
     rows, width = x.shape
-    weight = whole(width, 3 * width // 2)
+    depth = mine_w[0].shape[0]
+    weight = [whole(depth, 3 * width // 2)] * 3 + [whole(depth, width), whole(depth, width // 2)]
     return launch(
         project_kernel,
         "project",
         (rows // BLOCK,),
-        (x, gain, shift, bias, mine_w, other_w),
+        (x, gain, shift, bias, *mine_w, *other_w),
         [
-            pl.BlockSpec((BLOCK, width), lambda i, c: (i, 0)),
+            pl.BlockSpec((BLOCK, width), lambda i, c, m: (i, 0)),
             whole(1, width),
             whole(1, width),
             whole(1, 3 * width),
-            weight,
-            weight,
+            *weight,
+            *weight,
         ],
         (
-            pl.BlockSpec((BLOCK, width), lambda i, c: (i, 0)),
-            pl.BlockSpec((BLOCK, 3 * width), lambda i, c: (i, 0)),
+            pl.BlockSpec((BLOCK, width), lambda i, c, m: (i, 0)),
+            pl.BlockSpec((BLOCK, 3 * width), lambda i, c, m: (i, 0)),
         ),
         (shape_of((rows, width), bf16), shape_of((rows, 3 * width), bf16)),
-        scalars=(core,),
+        scalars=(core, me),
         after=after,
         work=(6 * rows * width * width, 6 * width * width + 10 * rows * width),
     )
@@ -301,13 +321,16 @@
     )
 
 
-def middle_kernel(
-    core, slot, x_ref, o_ref, mine_w, other_w, bias, gain, shift, mid_ref, keep_ref, away_ref, acc
-):
+def middle_kernel(core, me, slot, x_ref, o_ref, *refs):
+    pieces, (bias, gain, shift, mid_ref, keep_ref, away_ref, acc) = refs[:8], refs[8:]
     half = x_ref.shape[1] // 2
-    for w, side in sides(core, mine_w, other_w):
+    depth = pieces[0].shape[0]
+    for ws, side in sides(core, pieces[:4], pieces[4:]):
         at = pl.ds(pl.multiple_of(half * side, half), half)
-        mid_ref[:, at] = x_ref[:, at].astype(f32) + dot(o_ref[...], w[...]) + bias[:, at]
+        out = x_ref[:, at].astype(f32) + bias[:, at]
+        for r, w in enumerate(ws):
+            out = out + dot(o_ref[:, pl.ds(pl.multiple_of((me[0] ^ r) * depth, depth), depth)], w[...])
+        mid_ref[:, at] = out
     normed, _ = norm_parts(mid_ref[...])
     send_slots(acc, slot, (normed * gain[...] + shift[...]).astype(bf16), keep_ref, away_ref)
 
@@ -316,20 +339,23 @@
     return pl.BlockSpec((width, width // 2), lambda *_: (0, 3))
 
 
-def middle_part(core, slot_row, x, attended, mine_w, other_w, bias, gain, shift, after=()):
+def middle_part(core, me, slot_row, x, attended, mine_w, other_w, bias, gain, shift, after=()):
     rows, width = x.shape
-    block = pl.BlockSpec((BLOCK, width), lambda i, c: (i, 0))
+    block = pl.BlockSpec((BLOCK, width), lambda i, c, m: (i, 0))
+    half, depth = width // 2, mine_w[0].shape[0]
+    out_columns = [pl.BlockSpec((depth, half), lambda *_: (0, 3))] * 3 + [pl.BlockSpec((depth, half), lambda *_: (0, 1))]
+    of = lambda w: (w[0], w[1], w[2], w[4])
     return launch(
         middle_kernel,
         "middle",
         (rows // BLOCK,),
-        (slot_row, x, attended, mine_w, other_w, bias, gain, shift),
+        (slot_row, x, attended, *of(mine_w), *of(other_w), bias, gain, shift),
         [
-            pl.BlockSpec((1, BLOCK), lambda i, c: (0, i)),
+            pl.BlockSpec((1, BLOCK), lambda i, c, m: (0, i)),
             block,
             block,
-            out_half(width),
-            out_half(width),
+            *out_columns,
+            *out_columns,
             whole(1, width),
             whole(1, width),
             whole(1, width),
@@ -337,7 +363,7 @@
         (block, whole(CAPACITY, width), whole(CAPACITY, width)),
         (shape_of((rows, width), f32),) + (shape_of((CAPACITY, width), bf16),) * 2,
         [pltpu.VMEM((2 * CAPACITY, width), f32)],
-        scalars=(core,),
+        scalars=(core, me),
         after=after,
         work=(4 * CAPACITY * rows * width + 2 * rows * width * width, 10 * rows * width + 4 * CAPACITY * width),
     )
@@ -589,29 +615,31 @@
     )
 
 
-def hold_block(held, per, pieces):
+def hold_block(held, per, pieces, right):
     w0, w1, w2, w3a, w3b = pieces
     which = pl.program_id(0) // per
-    half = w3a.shape[1]
+    half = held.shape[1] // 2
     for r, w in enumerate((w0, w1, w2)):
 
         @pl.when(which == r)
         def _(w=w):
-            held[...] = w[...]
+            held[:, :half] = w[...]
 
     @pl.when(which == 3)
     def _():
-        held[:, :half] = w3a[...]
-        held[:, half:] = w3b[...]
+        held[:, : half // 2] = w3a[...]
+        held[:, half // 2 : half] = w3b[...]
+
+    held[:, half:] = right[...].reshape(held.shape[0], half)
 
 
 def down_grad_kernel(
-    me, per, gk, gr, xk, xr, slope_ref, u0, u1, u2, u3a, u3b, w0, w1, w2, w3a, w3b,
+    me, per, gk, gr, xk, xr, slope_ref, u0, u1, u2, u3a, u3b, w0, w1, w2, w3a, w3b, right,
     dk_ref, dr_ref, up_ref, far_x, far_y, bias_ref, held, acc, g, t,
 ):
     step = pl.program_id(0)
     slots = gk.shape[0]
-    hold_block(held, per, (w0, w1, w2, w3a, w3b))
+    hold_block(held, per, (w0, w1, w2, w3a, w3b), right)
 
     @pl.when(step == 0)
     def _():
@@ -647,14 +675,19 @@
         dr_ref[...] = acc[slots:, :].astype(bf16)
 
 
-def piece_specs(width, per, which):
+def second_specs(pieces, right):
+    per = pieces[0].shape[0] // FBLOCK
+    _, _, rows, half = right.shape
+
     def spec(r, columns):
         return pl.BlockSpec((FBLOCK, columns), lambda i, m: (jnp.clip(i - r * per, 0, per - 1), 0))
 
-    return [spec(r, width // 2 if r == 3 else width) for r in which for _ in range(2 if r == 3 else 1)]
-
-
-def down_grad(me, gk, gr, xk, xr, slope, up_pieces, down_pieces, after=()):
+    return [spec(0, half), spec(1, half), spec(2, half), spec(3, half // 2), spec(3, half // 2)] + [
+        pl.BlockSpec((FBLOCK // rows, 1, rows, half), lambda i, m: (i % per, m[0] ^ (i // per), 0, 0))
+    ]
+
+
+def down_grad(me, gk, gr, xk, xr, slope, up_pieces, down_pieces, right, after=()):
     slots, width = xk.shape
     depth, hidden = up_pieces[0].shape
     per = down_pieces[0].shape[0] // FBLOCK
@@ -675,7 +708,7 @@
         lambda me, *refs: down_grad_kernel(me, per, *refs),
         "experts_grad",
         (steps,),
-        (gk, gr, xk, xr, slope, *up_pieces, *down_pieces),
+        (gk, gr, xk, xr, slope, *up_pieces, *down_pieces, right),
         [tokens] * 4
         + [pl.BlockSpec((2 * slots, FBLOCK), lambda i, m: (0, at(i, m)))]
         + [weight] * 3
@@ -683,7 +716,7 @@
             pl.BlockSpec((depth, FBLOCK), lambda i, m: (0, jnp.minimum(at(i, m), half - 1))),
             pl.BlockSpec((depth, FBLOCK), lambda i, m: (0, jnp.maximum(at(i, m) - half, 0))),
         ]
-        + piece_specs(width, per, range(4)),
+        + second_specs(down_pieces, right),
         (
             tokens,
             tokens,
@@ -712,54 +745,17 @@
     )
 
 
-def down_near_kernel(me, act_ref, w0, w1, w2, out_ref, acc):
-    step = pl.program_id(0)
-    which = step // (pl.num_programs(0) // 3)
-    w = jnp.where(which == 0, w0[...], jnp.where(which == 1, w1[...], w2[...]))
-    part = dot(act_ref[...], w)
-
-    @pl.when(step == 0)
+def down_kernel(me, per, act_ref, w0, w1, w2, w3a, w3b, right, keep_ref, away_ref, held, acc):
+    hold_block(held, per, (w0, w1, w2, w3a, w3b), right)
+    part = dot(act_ref[...], held[...])
+
+    @pl.when(pl.program_id(0) == 0)
     def _():
         acc[...] = part
 
-    @pl.when(step > 0)
+    @pl.when(pl.program_id(0) > 0)
     def _():
         acc[...] += part
-
-    @pl.when(step == pl.num_programs(0) - 1)
-    def _():
-        out_ref[...] = acc[...].astype(bf16)
-
-
-def down_near(me, act, pieces, after=()):
-    slots = act.shape[0]
-    rows, width = pieces[0].shape
-    per = rows // FBLOCK
-    return launch(
-        down_near_kernel,
-        "down_near",
-        (3 * per,),
-        (act, *pieces),
-        [pl.BlockSpec((slots, FBLOCK), lambda i, m: (0, (m[0] ^ (i // per)) * per + i % per))]
-        + piece_specs(width, per, range(3)),
-        whole(slots, width),
-        shape_of((slots, width), bf16),
-        [pltpu.VMEM((slots, width), f32)],
-        scalars=(me,),
-        after=after,
-        work=(2 * slots * width * rows * 3, 2 * width * rows * 3 + 2 * slots * rows * 3),
-    )
-
-
-def down_far_kernel(me, act_ref, wa, wb, near_ref, keep_ref, away_ref, acc):
-    half = wa.shape[1]
-
-    @pl.when(pl.program_id(0) == 0)
-    def _():
-        acc[...] = near_ref[...].astype(f32)
-
-    acc[:, :half] += dot(act_ref[...], wa[...])
-    acc[:, half:] += dot(act_ref[...], wb[...])
 
     @pl.when(pl.program_id(0) == pl.num_programs(0) - 1)
     def _():
@@ -768,22 +764,23 @@
         away_ref[...] = acc[slots:, :].astype(bf16)
 
 
-def down_far(me, act, wa, wb, near, after=()):
-    slots, width = near.shape
-    per = wa.shape[0] // FBLOCK
-    half = pl.BlockSpec((FBLOCK, width // 2), lambda i, m: (i, 0))
-    return launch(
-        down_far_kernel,
-        "down_far",
-        (per,),
-        (act, wa, wb, near),
-        [pl.BlockSpec((slots, FBLOCK), lambda i, m: (0, (m[0] ^ 3) * per + i)), half, half, whole(slots, width)],
+def down(me, act, pieces, right, after=()):
+    slots, hidden = act.shape
+    width = 2 * right.shape[3]
+    per = pieces[0].shape[0] // FBLOCK
+    return launch(
+        lambda me, *refs: down_kernel(me, per, *refs),
+        "experts_down",
+        (hidden // FBLOCK,),
+        (act, *pieces, right),
+        [pl.BlockSpec((slots, FBLOCK), lambda i, m: (0, (m[0] ^ (i // per)) * per + i % per))]
+        + second_specs(pieces, right),
         (whole(slots // 2, width),) * 2,
         (shape_of((slots // 2, width), bf16),) * 2,
-        [pltpu.VMEM((slots, width), f32)],
+        [pltpu.VMEM((FBLOCK, width), bf16), pltpu.VMEM((slots, width), f32)],
         scalars=(me,),
         after=after,
-        work=(2 * slots * width * wa.shape[0], 6 * slots * width),
+        work=(2 * slots * width * hidden, 2 * width * hidden + 2 * slots * hidden),
     )
 
 
@@ -918,25 +915,37 @@
     )(value, *after)
 
 
-def halves_kernel(x_ref, y_ref, out_x, out_y):
+def halves_kernel(x_ref, y_ref, out_x, out_y, held_x, held_y, sems):
     half = out_x.shape[1]
-    out_x[...] = x_ref[:, :half]
-    out_y[...] = y_ref[:, half:]
+    inward = [
+        pltpu.make_async_copy(x_ref.at[:, :half], held_x, sems.at[0]),
+        pltpu.make_async_copy(y_ref.at[:, half:], held_y, sems.at[1]),
+    ]
+    outward = [
+        pltpu.make_async_copy(held_x, out_x, sems.at[2]),
+        pltpu.make_async_copy(held_y, out_y, sems.at[3]),
+    ]
+    for copy in inward:
+        copy.start()
+    for arrived, copy in zip(inward, outward):
+        arrived.wait()
+        copy.start()
+    for copy in outward:
+        copy.wait()
 
 
 def cut_halves(by_x, by_y, after=()):
     rows, columns = by_x.shape
-    step = rows // 2
-    block = pl.BlockSpec((step, columns), lambda i: (i, 0))
-    half = pl.BlockSpec((step, columns // 2), lambda i: (i, 0))
+    place = pl.BlockSpec(memory_space=pltpu.HBM)
     return launch(
         halves_kernel,
         "cut_halves",
-        (2,),
+        (1,),
         (by_x, by_y),
-        [block, block],
-        (half, half),
+        [place, place],
+        (place, place),
         (shape_of((rows, columns // 2), bf16),) * 2,
+        [pltpu.VMEM((rows, columns // 2), bf16)] * 2 + [pltpu.SemaphoreType.DMA((4,))],
         after=after,
     )
 
@@ -950,6 +959,32 @@
     rows, columns = full.shape
     blocks = full.reshape(4, rows // 4, columns)
     return blocks[0], blocks[1], blocks[2], blocks[3, :, : columns // 2], blocks[3, :, columns // 2 :]
+
+
+def finish_kernel(core, mine_ref, other_ref, out_ref, qkv_ref):
+    half = out_ref.shape[1] // 2
+    for value, side in ((mine_ref[0], core[0]), (other_ref[...], 1 - core[0])):
+        value = value.astype(f32)
+        out_ref[:, pl.ds(pl.multiple_of(half * side, half), half)] = value[:, :half]
+        for j in range(3):
+            at = pl.ds(pl.multiple_of(2 * half * j + half * side, half), half)
+            qkv_ref[:, at] = value[:, half * (j + 1) : half * (j + 2)]
+
+
+def finish(core, total):
+    rows, columns = total.shape[0] // 2, total.shape[1]
+    halves = total.reshape(2, rows, columns)
+    other = swap_core(pick(halves, 1 - core[0]))
+    return launch(
+        finish_kernel,
+        "finish",
+        (1,),
+        (halves, other),
+        [pl.BlockSpec((1, rows, columns), lambda i, c: (c[0], 0, 0)), whole(rows, columns)],
+        (whole(rows, columns // 2), whole(rows, 3 * columns // 2)),
+        (shape_of((rows, columns // 2), f32), shape_of((rows, 3 * columns // 2), f32)),
+        scalars=(core,),
+    )
 
 
 def shards(
@@ -979,7 +1014,7 @@
     up_share = up_bias.shape[1]
     core = lax.axis_index("c")
     scalar = lambda v: jnp.reshape(v, (1,)).astype(jnp.int32)
-    square = n_dp == 4
+    square = n_dp == 4 and n_z == 4
     me = scalar(lax.axis_index("dp") if square else 0)
 
     half = width // 2
@@ -999,6 +1034,8 @@
     bias_down = small[:, 7 * share + 2 * up_share :].reshape(devices, 2, share)
     bias_down = jnp.swapaxes(bias_down, 0, 1).reshape(2, width)
 
+    qkv_bias = jnp.concatenate([bias_query, jnp.zeros_like(bias_query), bias_value], 1)
+
     def expert_shard(weight, after):
         mine, other = pick(weight, core, 1), swap_core(pick(weight, 1 - core, 1))
         return place(scalar(core), [mine, other], after)
@@ -1009,24 +1046,30 @@
     slot = jnp.sum(before.astype(jnp.int32), 1) + jnp.where(route == core, 0, CAPACITY)
     slot_row, slot_col = slot.reshape(1, rows), slot.reshape(rows, 1)
 
-    grad_keep, grad_away = dispatch(slot_row, cotangent, (attn_shard,))
+    right_shard = expert_shard(down_weight[:, :, half:], (attn_shard,))
+    up_shard = expert_shard(up_weight, (right_shard,))
+    up_own = gather_z(up_shard)
+    if square:
+        right_all = place(me, [right_shard] + [swap(right_shard, "dp", 4, mask) for mask in range(1, 4)], (up_shard,))
+        attn_own = later(gather_z(attn_shard), (right_all,))
+    else:
+        attn_own = gather_z(attn_shard)
+    grad_keep, grad_away = dispatch(slot_row, cotangent, (attn_own,))
     grad_got = swap_core(grad_away)
-    up_shard = expert_shard(up_weight, (grad_keep,))
-    up_own = gather_z(up_shard)
-    down_shard = expert_shard(down_weight, (up_shard,))
-    attn_own = later(gather_z(attn_shard), (down_shard,))
+    down_shard = expert_shard(down_weight[:, :, :half], (grad_keep,))
     if square:
+        right = lax.all_gather(right_all.reshape(4, -1, half), "z", axis=0)
         attn_near = swap_near(attn_own, attn_own)
-        attn_far = gather_far(cut_halves(*attn_near))
-        mine_w = place(me, [attn_own, *attn_near, *attn_far], (up_own, down_shard, grad_got, bias_down))
+        mine_p = (attn_own, *attn_near, *gather_far(cut_halves(*attn_near, (down_shard,))))
         up_near = swap_near(up_own, up_own)
     else:
-        mine_w = lax.all_gather(attn_own, "dp", axis=0, tiled=True)
-    other_w = swap_core(mine_w)
+        right = lax.all_gather(gather_z(right_shard), "dp", axis=0, tiled=True)
+        right = jnp.swapaxes(right.reshape(4, 4, -1, half), 0, 1)
+        mine_p = gather_pieces(attn_own)
+    other_p = tuple(swap_core(piece) for piece in mine_p)
 
     side = scalar(core)
-    qkv_bias = jnp.concatenate([bias_query, jnp.zeros_like(bias_query), bias_value], 1)
-    normed_one, qkv = project(side, tokens, gain_one, shift_one, qkv_bias, mine_w, other_w, (up_own,))
+    normed_one, qkv = project(side, me, tokens, gain_one, shift_one, qkv_bias, mine_p, other_p, (up_own, grad_got, bias_out, gain_two, shift_two))
     other_normed_one = swap_core(normed_one)
     seg_row, seg_col = segment_ids, segment_ids.reshape(rows, 1)
     attended, lse = attention(qkv, seg_col, seg_row)
@@ -1037,24 +1080,25 @@
     else:
         up_cut, w_up = (), gather_pieces(up_own)
     middle, in_keep, in_away = middle_part(
-        side, slot_row, tokens, attended, mine_w, other_w, bias_out, gain_two, shift_two, after=(*up_cut, other_normed_one)
-    )
+        side, me, slot_row, tokens, attended, mine_p, other_p, bias_out, gain_two, shift_two, after=(*up_cut, other_normed_one)
+    )
+    mine_w = place(me, mine_p, (middle,))
+    other_w = place(me, other_p, (mine_w,))
     down_own = later(gather_z(down_shard), (middle,))
-    in_got = swap_core(later(in_away, (*w_up[3:], down_own)))
+    in_got = swap_core(later(in_away, (*w_up[3:], down_own, other_w)))
 
     if square:
         down_near_got = swap_near(down_own, down_own)
     act, slope = up(me, in_keep, in_got, bias_up, w_up)
-    down_partial, down_bias_grad = outer(act, grad_keep, grad_got)
     if square:
-        down_cut = cut_halves(*down_near_got, (down_partial,))
+        down_cut = cut_halves(*down_near_got, (act,))
         w_down = (down_own, *down_near_got, *gather_far(down_cut))
     else:
         down_cut, w_down = (), gather_pieces(down_own)
-    y_near = down_near(me, act, w_down[:3], down_cut)
-    down_half = lax.psum_scatter(later(down_partial, (*w_down[3:], y_near)), "dp", scatter_dimension=0, tiled=True)
+    down_partial, down_bias_grad = outer(act, grad_keep, grad_got, (*down_cut, right))
+    down_half = lax.psum_scatter(later(down_partial, w_down[3:]), "dp", scatter_dimension=0, tiled=True)
     back_keep, back_away, up_partial, up_out_x, up_out_y, up_bias_grad = down_grad(
-        me, grad_keep, grad_got, in_keep, in_got, slope, w_up, w_down, after=(y_near,)
+        me, grad_keep, grad_got, in_keep, in_got, slope, w_up, w_down, right, after=(other_w,)
     )
     back_got = swap_core(back_away)
     if square:
@@ -1072,20 +1116,22 @@
         me, 4, attended, mine_projected[None], other_attended, other_projected[None], 0, after=up_next
     )
     down_total = scatter_z(later(down_half, up_next))
-    qkv_kept = attention_grad(qkv, attended_grad, lse, seg_col, seg_row, core, after=partial[:1])
+    y_keep, y_away = down(me, act, w_down, right, after=partial[:1])
+    y_got = swap_core(y_away)
+    qkv_kept = attention_grad(qkv, attended_grad, lse, seg_col, seg_row, core, after=(y_keep,))
+    if square:
+        up_block = scatter_near(me, up_partial, *swap_near(*up_next), after=(qkv_kept, down_total))
+    else:
+        up_block = lax.psum_scatter(up_partial, "dp", scatter_dimension=0, tiled=True)
+    up_total = scatter_z(up_block)
     partial, out_x, out_y = two_sum(
-        me, 4, normed_one, qkv_kept, other_normed_one, qkv_got, 1, into=partial, after=()
+        me, 4, normed_one, qkv_kept, other_normed_one, qkv_got, 1, into=partial, after=(up_block,)
     )
     if square:
         partial = partial.reshape(4, width // 4, -1)
         far = swap_near(out_x, out_y)
-        up_block = scatter_near(me, up_partial, *swap_near(*up_next), after=(out_x, down_total))
-    else:
-        up_block = lax.psum_scatter(up_partial, "dp", scatter_dimension=0, tiled=True)
-    up_total = scatter_z(up_block)
-    y_keep, y_away = down_far(me, act, *w_down[3:], y_near, after=(up_block,))
-    y_got = swap_core(y_away)
-    near = scatter_next(me, partial, *far, after=(y_keep,)) if square else ()
+    block_out = output(slot_col, expert_ids, y_keep, y_got, middle, bias_down, after=(out_x,))
+    near = scatter_next(me, partial, *far, after=(block_out,)) if square else ()
     input_grad, gain_one_grad, shift_one_grad, bias_sums = input_grads(
         qkv_kept, qkv_away, tokens, middle_grads, mine_w, other_w, gain_one, after=near
     )
@@ -1116,13 +1162,9 @@
     up_bias_sum = both[:, at : at + up_share]
     down_bias_sum = both[:, at + up_share :]
 
-    block_out = output(slot_col, expert_ids, y_keep, y_got, middle, bias_down, after=(sent,))
     down_weight_grad = by_core(core, *to_core(down_total.astype(f32)), 1)
     up_weight_grad = by_core(core, *to_core(up_total.astype(f32)), 1)
-    last = later(scatter_z(last), (block_out, down_weight_grad, up_weight_grad))
-    last = to_core(last.astype(f32))
-    out_weight_grad = by_core(core, *(v[:, :half] for v in last), 1).reshape(share, width)
-    qkv_weight_grad = by_core(core, *(v[:, half:].reshape(share, 3, half) for v in last), 2).reshape(share, 3 * width)
+    out_weight_grad, qkv_weight_grad = finish(side, later(scatter_z(last), (up_bias_sum, down_weight_grad, up_weight_grad)))
     return (
         block_out,
         input_grad,

time: 522 us -> 502 us (0.962)
  waiting for transfers between devices: 87.2 us -> 55 us
  starting transfers between devices: 32.2 us -> 40.5 us
    ppermute x35 -> x43, waiting for transfers between devices: 62.5 us -> 41.2 us  [swap(): return lax.ppermute(value, axis, [(i, i ^ mask) for i in range(size)])]
    all_gather x3, waiting for transfers between devices: 11.3 us -> 0.02 us  [gather_z(): return lax.all_gather(shard, 'z', axis=0, tiled=True)]
    ppermute x35 -> x43, starting transfers between devices: 26 us -> 32 us  [swap(): return lax.ppermute(value, axis, [(i, i ^ mask) for i in range(size)])]
    unnamed x114 -> x126, local copies, waits for them, and re-layouts: 19.7 us -> 24.4 us
    pallas_call x25 -> x28, Pallas kernels: 303 us -> 303 us  [launch(): pl.pallas_call(body, grid_spec=pltpu.PrefetchScalarGridSpec(num_scalar_pr...]
  transfers between devices with their start and end apart: 44 -> 53, of which waited for: 24 -> 19; matrix products, arithmetic and copies ran while one was open for 7% -> 8% of each run, Pallas kernels for 60% -> 65%
where the time goes in v3:
time: 502 us; the launch traced here: 492 us
  Pallas kernels  322 us (64%)
  waiting for transfers between devices  55 us (11%)
  local copies, waits for them, and re-layouts  44.3 us (9%)
  starting transfers between devices  40.5 us (8%)
  between operations  15.4 us (3%)
  other arithmetic  14.9 us (3%)
    pallas_call x28, Pallas kernels, launch(): pl.pallas_call(body, grid_spec=pltpu.PrefetchScalarGridSpec(num_scalar_pr...  303 us
    ppermute x43, waiting for transfers between devices, swap(): return lax.ppermute(value, axis, [(i, i ^ mask) for i in range(size)])  41.2 us
    ppermute x43, starting transfers between devices, swap(): return lax.ppermute(value, axis, [(i, i ^ mask) for i in range(size)])  32 us
    unnamed x126, local copies, waits for them, and re-layouts  24.4 us
    pallas_call x2, Pallas kernels, two_sum(): pl.pallas_call(body, grid_spec=pltpu.PrefetchScalarGridSpec(num_scalar_pr...  19.2 us
  transfers between devices with their start and end apart: 53, of which 19 were waited for; matrix products, arithmetic and copies ran while one was open for 8% of the time, Pallas kernels for 65%

profile of v3, /device:TPU:0, one launch (start us, length us, event | category | flops | bytes accessed | tf_op | source)
XLA Modules:
  0.0 492.1 jit_solution(13972848177285697405)
XLA Ops:
  8.5 1.6 dynamic-slice_reduce_fusion
  12.3 1.7 place.7
  19.5 1.7 place.8
  21.9 1.8 place.9
  24.8 2.7 collective-permute-start.2
  27.5 1.5 collective-permute-start.3
  30.1 4.5 collective-permute-done.2.refs_2_
  34.6 6.8 %collective-permute-done.3.refs_3_ = bf16[256,512]{1,0:T(8,128)(2,1)S(1)} collective-permute-done((bf16[256,512]{1,0:T(8,128)(2,1)S(1)}, bf16[256,512]{1,0:T(8,128)(2,1)S(1)}, u32[]{:S(2)}, u32[]{:S(2)}) %collective-permute-start.3) | collective-permute-done | bytes 262176 | tf_op jit(solution)/shard_map/ppermute | solution.py:821
  42.2 2.7 place.10
  46.2 1.5 collective-permute-start.7
  49.8 8.1 %dispatch.1 = (bf16[640,1024]{1,0:T(8,128)(2,1)}, bf16[640,1024]{1,0:T(8,128)(2,1)}) custom-call(s32[1,1024]{1,0:T(1,128)} %add.52.refs_0_.refs_2_, bf16[1024,1024]{1,0:T(8,128)(2,1)} %refs_5_.1, bf16[256,2048]{1,0:T(8,128)(2,1)} %later.7.refs_2_.refs_6_.refs_5_.refs_1_), custom_call_target="tpu_custom_call" | custom-call | flops 5368709120 | bytes 4718592 | tf_op jit(solution)/shard_map/dispatch/pallas_call | solution.py:44
  58.6 1.8 place.11
  61.0 8.7 %collective-permute-done.6.refs_0_.refs_7_.refs_6_.refs_2_ = bf16[256,2048]{1,0:T(8,128)(2,1)S(1)} collective-permute-done((bf16[256,2048]{1,0:T(8,128)(2,1)}, bf16[256,2048]{1,0:T(8,128)(2,1)S(1)}, u32[]{:S(2)}, u32[]{:S(2)}) %collective-permute-start.6) | collective-permute-done | bytes 1048608 | tf_op jit(solution)/shard_map/ppermute | solution.py:821
  71.9 2.1 cut_halves.3
  74.0 1.5 collective-permute-start.9
  79.7 4.0 all-to-all-start
  84.8 6.8 %all-to-all-done = bf16[32,2,272]{2,1,0:T(2,128)(2,1)S(1)} async-done(((bf16[32,2,272]{2,1,0:T(2,128)(2,1)}), bf16[32,2,272]{2,1,0:T(2,128)(2,1)S(1)}, u32[]{:S(2)}, u32[]{:S(2)}) %all-to-all-start) | async-done | bytes 34848 | tf_op jit(solution)/shard_map/all_to_all | solution.py:1028
  99.5 13.3 %project.1 = (bf16[1024,1024]{1,0:T(8,128)(2,1)}, bf16[1024,3072]{1,0:T(8,128)(2,1)}) custom-call(s32[1]{0:T(128)} %bitcast.3.refs_0_, s32[1]{0:T(128)} %bitcast.2.refs_0_.refs_1_, bf16[1024,1024]{1,0:T(8,128)(2,1)} %refs_2_.7, f32[1,1024]{1,0:T(1,128)} %reshape.225.refs_3_.refs_6_, f32[1,1024]{1,0:T(1,128)} %reshape.226.refs_4_, ...), custom_call_target="tpu_custom_call" | custom-call | flops 12884901888 | bytes 16777216 | tf_op jit(solution)/shard_map/project/pallas_call | solution.py:44
  113.1 32.8 %attention_forward.1 = (bf16[1024,1024]{1,0:T(8,128)(2,1)}, f32[8,2,1024]{2,1,0:T(2,128)}) custom-call(s32[1024,1]{1,0:T(8,128)} %copy.112.refs_0_.refs_1_, s32[1,1024]{1,0:T(1,128)} %refs_2_.6, bf16[1024,3072]{1,0:T(8,128)(2,1)} %get-tuple-element.69.refs_2_.refs_3_.refs_4_.refs_5_, bf16[1024,3072]{1,0:T(8,128)(2,1)} %get-tuple-element.69.refs_2_.refs_3_.refs_4_.refs_5_, ...), custom_call_target="tpu_custom_call" | custom-call | flops 34359738368 | bytes 8388608 | tf_op jit(solution)/shard_map/attention_forward/pallas_call | solution.py:44
  148.0 2.6 cut_halves.4
  152.8 13.8 %middle.1 = (f32[1024,1024]{1,0:T(8,128)}, bf16[640,1024]{1,0:T(8,128)(2,1)}, bf16[640,1024]{1,0:T(8,128)(2,1)}) custom-call(s32[1]{0:T(128)} %bitcast.3.refs_0_, s32[1]{0:T(128)} %bitcast.2.refs_0_.refs_1_, s32[1,1024]{1,0:T(1,128)} %add.52.refs_0_.refs_2_, bf16[1024,1024]{1,0:T(8,128)(2,1)} %refs_2_.7, ...), custom_call_target="tpu_custom_call" | custom-call | flops 9663676416 | bytes 13107200 | tf_op jit(solution)/shard_map/middle/pallas_call | solution.py:44
  166.6 4.7 place.12
  171.3 4.7 place.13
  181.6 25.0 %experts_up.1 = (bf16[1280,4096]{1,0:T(8,128)(2,1)}, bf16[1280,4096]{1,0:T(8,128)(2,1)}) custom-call(s32[1]{0:T(128)} %bitcast.2.refs_0_.refs_1_, bf16[640,1024]{1,0:T(8,128)(2,1)} %get-tuple-element.74.refs_1_.refs_3_, bf16[640,1024]{1,0:T(8,128)(2,1)} %collective-permute-done.22.refs_2_.refs_4_, f32[1,4096]{1,0:T(1,128)} %dynamic-slice_bitcast_fusion.3.refs_3_, ...), custom_call_target="tpu_custom_call" | custom-call | flops 21474836480 | bytes 29360128 | tf_op jit(solution)/shard_map/experts_up/pallas_call | solution.py:44
  207.9 2.1 cut_halves.5
  212.0 17.2 %experts_outer.1 = (bf16[4096,1024]{1,0:T(8,128)(2,1)}, f32[1,1024]{1,0:T(1,128)}) custom-call(bf16[1280,4096]{1,0:T(8,128)(2,1)} %get-tuple-element.77.refs_2_.refs_1_.refs_0_, bf16[640,1024]{1,0:T(8,128)(2,1)} %get-tuple-element.65.refs_3_.refs_1_, bf16[640,1024]{1,0:T(8,128)(2,1)} %collective-permute-done.16.refs_17_.refs_2_, ...), custom_call_target="tpu_custom_call" | custom-call | flops 21474836480 | bytes 18874368 | tf_op jit(solution)/shard_map/experts_outer/pallas_call | solution.py:44
  230.3 50.7 %experts_grad.1 = (bf16[640,1024]{1,0:T(8,128)(2,1)}, bf16[640,1024]{1,0:T(8,128)(2,1)}, bf16[1024,4096]{1,0:T(8,128)(2,1)}, bf16[256,2048]{1,0:T(8,128)(2,1)}, ...) custom-call(s32[1]{0:T(128)} %bitcast.2.refs_0_.refs_1_, bf16[640,1024]{1,0:T(8,128)(2,1)} %get-tuple-element.65.refs_3_.refs_1_, ...), custom_call_target="tpu_custom_call" | custom-call | flops 64424509440 | bytes 35651584 | tf_op jit(solution)/shard_map/experts_grad/pallas_call | solution.py:44
  283.3 2.0 collective-permute-done.27.refs_3_
  286.4 14.8 %middle_grad.1 = (f32[1024,1024]{1,0:T(8,128)}, bf16[1024,512]{1,0:T(8,128)(2,1)}, bf16[1024,512]{1,0:T(8,128)(2,1)}, bf16[1024,1024]{1,0:T(8,128)(2,1)}, f32[1,...) custom-call(s32[1]{0:T(128)} %bitcast.3.refs_0_, s32[1024,1]{1,0:T(8,128)} %get-tuple-element.130.refs_1_.refs_0_, ...), custom_call_target="tpu_custom_call" | custom-call | flops 9663676416 | bytes 19398656 | tf_op jit(solution)/shard_map/middle_grad/pallas_call | solution.py:44
  301.3 18.6 %attention_backward.2.refs_5_.refs_1_ = bf16[3,1024,512]{2,1,0:T(8,128)(2,1)} custom-call(s32[1]{0:T(128)} %bitcast.25.refs_0_, s32[1024,1]{1,0:T(8,128)} %copy.112.refs_0_.refs_1_, s32[1,1024]{1,0:T(1,128)} %refs_2_.6, bf16[1024,3072]{1,0:T(8,128)(2,1)} %get-tuple-element.69.refs_2_.refs_3_.refs_4_.refs_5_, ...), custom_call_target="tpu_custom_call" | custom-call | flops 25769803776 | bytes 8388608 | tf_op jit(solution)/shard_map/attention_backward/pallas_call | solution.py:44
  320.3 3.9 collective-permute-done.30.refs_3_
  326.4 5.4 %far_add.2 = (bf16[256,4096]{1,0:T(8,128)(2,1)}, bf16[256,4096]{1,0:T(8,128)(2,1)}) custom-call(s32[1]{0:T(128)} %bitcast.2.refs_0_.refs_1_, bf16[4,256,4096]{2,1,0:T(8,128)(2,1)} %bitcast.88, bf16[4,256,4096]{2,1,0:T(8,128)(2,1)} %bitcast.89, bf16[256,2048]{1,0:T(8,128)(2,1)} %copy-done.14, bf16[256,2048]{1,0:T(8,128)(2,1)} %copy-done.15, ...), custom_call_target="tpu_custom_call" | custom-call | tf_op jit(solution)/shard_map/far_add/pallas_call | solution.py:44
  334.8 6.4 %two_sum.2 = (bf16[1024,2048]{1,0:T(8,128)(2,1)}, bf16[256,1024]{1,0:T(8,128)(2,1)}, bf16[256,1024]{1,0:T(8,128)(2,1)}) custom-call(s32[1]{0:T(128)} %bitcast.2.refs_0_.refs_1_, bf16[1024,1024]{1,0:T(8,128)(2,1)} %get-tuple-element.70.refs_2_.refs_4_.refs_1_, bf16[1,1024,512]{2,1,0:T(8,128)(2,1)} %bitcast.146, ...), custom_call_target="tpu_custom_call" | custom-call | flops 4294967296 | bytes 6291456 | tf_op jit(solution)/shard_map/two_sum/pallas_call | solution.py:516
  341.3 21.6 %experts_down.1 = (bf16[640,1024]{1,0:T(8,128)(2,1)}, bf16[640,1024]{1,0:T(8,128)(2,1)}) custom-call(s32[1]{0:T(128)} %bitcast.2.refs_0_.refs_1_, bf16[1280,4096]{1,0:T(8,128)(2,1)} %get-tuple-element.77.refs_2_.refs_1_.refs_0_, bf16[1024,512]{1,0:T(8,128)(2,1)} %later.8.refs_3_.refs_11_.refs_2_, bf16[1024,512]{1,0:T(8,128)(2,1)} %copy-done.9, ...), custom_call_target="tpu_custom_call" | custom-call | flops 21474836480 | bytes 18874368 | tf_op jit(solution)/shard_map/experts_down/pallas_call | solution.py:44
  362.9 18.4 %attention_backward.3.refs_4_.refs_2_.refs_0_ = bf16[3,1024,512]{2,1,0:T(8,128)(2,1)} custom-call(s32[1]{0:T(128)} %bitcast.27.refs_0_, s32[1024,1]{1,0:T(8,128)} %copy.112.refs_0_.refs_1_, s32[1,1024]{1,0:T(1,128)} %refs_2_.6, bf16[1024,3072]{1,0:T(8,128)(2,1)} %get-tuple-element.69.refs_2_.refs_3_.refs_4_.refs_5_, ...), custom_call_target="tpu_custom_call" | custom-call | flops 25769803776 | bytes 8388608 | tf_op jit(solution)/shard_map/attention_backward/pallas_call | solution.py:44
  382.7 4.9 near_add.2.refs_8_
  388.9 12.8 %two_sum.3 = (bf16[1024,2048]{1,0:T(8,128)(2,1)}, bf16[256,1024]{1,0:T(8,128)(2,1)}, bf16[256,1024]{1,0:T(8,128)(2,1)}) custom-call(s32[1]{0:T(128)} %bitcast.2.refs_0_.refs_1_, bf16[1024,1024]{1,0:T(8,128)(2,1)} %get-tuple-element.73.refs_1_, ...), custom_call_target="tpu_custom_call", output_to_operand_aliasing={{0}: (5, {}), {1}: (6, {}), {2}: (7, {})} | custom-call | flops 12884901888 | bytes 10485760 | tf_op jit(solution)/shard_map/two_sum/pallas_call | solution.py:516
  401.7 1.5 collective-permute-start.36
  407.3 8.0 %output.1.refs_5_ = bf16[1024,1024]{1,0:T(8,128)(2,1)} custom-call(s32[1024,1]{1,0:T(8,128)} %get-tuple-element.130.refs_1_.refs_0_, s32[1024,1]{1,0:T(8,128)} %copy.117.refs_1_, bf16[640,1024]{1,0:T(8,128)(2,1)} %get-tuple-element.93.refs_8_.refs_2_, bf16[640,1024]{1,0:T(8,128)(2,1)} %collective-permute-done.32.refs_3_, ...), custom_call_target="tpu_custom_call" | custom-call | flops 5368709120 | bytes 8912896 | tf_op jit(solution)/shard_map/output/pallas_call | solution.py:44
  418.2 4.1 far_add.3
  424.2 14.6 %input_grad.1 = (f32[1024,1024]{1,0:T(8,128)}, f32[1,1024]{1,0:T(1,128)}, f32[1,1024]{1,0:T(1,128)}, f32[4,512]{1,0:T(4,128)}) custom-call(bf16[3,1024,512]{2,1,0:T(8,128)(2,1)} %attention_backward.3.refs_4_.refs_2_.refs_0_, bf16[3,1024,512]{2,1,0:T(8,128)(2,1)} %attention_backward.2.refs_5_.refs_1_, bf16[1024,1024]{1,0:T(8,128)(2,1)} %refs_2_.7, ...), custom_call_target="tpu_custom_call" | custom-call | flops 12884901888 | bytes 23068672 | tf_op jit(solution)/shard_map/input_grad/pallas_call | solution.py:44
  438.8 8.2 %collective-permute-done.38.refs_2_ = bf16[256,2048]{1,0:T(8,128)(2,1)S(1)} collective-permute-done((bf16[256,2048]{1,0:T(8,128)(2,1)}, bf16[256,2048]{1,0:T(8,128)(2,1)S(1)}, u32[]{:S(2)}, u32[]{:S(2)}) %collective-permute-start.38) | collective-permute-done | bytes 1048608 | tf_op jit(solution)/shard_map/ppermute | solution.py:821
  448.6 3.9 near_add.3.refs_1_
  463.0 3.9 all-to-all-start.1
  466.9 2.5 maximum_select_fusion.refs_2_
  469.4 5.5 %all-to-all-done.1 = f32[32,1,384]{2,1,0:T(1,128)S(1)} async-done(((f32[32,1,384]{2,1,0:T(1,128)}), f32[32,1,384]{2,1,0:T(1,128)S(1)}, u32[]{:S(2)}, u32[]{:S(2)}) %all-to-all-start.1) | async-done | bytes 49184 | tf_op jit(solution)/shard_map/all_to_all | solution.py:1157
  477.4 2.5 maximum_select_fusion.1.refs_3_
  482.9 1.8 finish.1
  (301 shorter events, 85.1 us)
Async XLA Ops:
  7.2 37.7 %all-gather.6.cloned.1.call-start = ((), (), s32[]{:S(2)}) async-start(), calls=%async_computation.6 | async-start | bytes 1310720 | tf_op jit(solution)/shard_map/all_gather | solution.py:896
  14.0 82.8 %all-gather.8.cloned.1.call-start = ((), (), s32[]{:S(2)}) async-start(), calls=%async_computation.7 | async-start | bytes 2621440 | tf_op jit(solution)/shard_map/all_gather | solution.py:896
  15.6 5.6 %collective-permute-start.5 = (bf16[32,4096]{1,0:T(8,128)(2,1)S(1)}, bf16[32,4096]{1,0:T(8,128)(2,1)S(1)}, u32[]{:S(2)}, u32[]{:S(2)}) collective-permute-start(bf16[32,4096]{1,0:T(8,128)(2,1)S(1)} %bitcast.129), channel_id=1, source_target_pairs={{0,1},{1,0},{2,3},{3,2},{4,5},{5,4},{6,7},{7,6},{8,9},{9,8},{10,11... | collective-permute-start | bytes 786440 | tf_op jit(solution)/shard_map/ppermute | solution.py:821
  23.8 147.5 %all-gather.10.cloned.1.call-start = ((), (), s32[]{:S(2)}) async-start(), calls=%async_computation.8 | async-start | bytes 1310720 | tf_op jit(solution)/shard_map/all_gather | solution.py:896
  24.4 33.5 %collective-permute-start.8 = (bf16[128,512]{1,0:T(8,128)(2,1)S(1)}, bf16[128,512]{1,0:T(8,128)(2,1)S(1)}, u32[]{:S(2)}, u32[]{:S(2)}) collective-permute-start(bf16[128,512]{1,0:T(8,128)(2,1)S(1)} %bitcast.130), channel_id=1, source_target_pairs={{0,1},{1,0},{2,3},{3,2},{4,5},{5,4},{6,7},{7,6},{8,9},{9,8},{10,11... | collective-permute-start | bytes 393224 | tf_op jit(solution)/shard_map/ppermute | solution.py:821
  24.8 9.8 %collective-permute-start.2 = (bf16[256,512]{1,0:T(8,128)(2,1)S(1)}, bf16[256,512]{1,0:T(8,128)(2,1)S(1)}, u32[]{:S(2)}, u32[]{:S(2)}) collective-permute-start(bf16[256,512]{1,0:T(8,128)(2,1)S(1)} %bitcast.110), channel_id=1, source_target_pairs={{0,8},{8,0},{16,24},{24,16},{1,9},{9,1},{17,25},{25,17},{2,10},{10... | collective-permute-start | bytes 786440 | tf_op jit(solution)/shard_map/ppermute | solution.py:821
  27.5 13.9 %collective-permute-start.3 = (bf16[256,512]{1,0:T(8,128)(2,1)S(1)}, bf16[256,512]{1,0:T(8,128)(2,1)S(1)}, u32[]{:S(2)}, u32[]{:S(2)}) collective-permute-start(bf16[256,512]{1,0:T(8,128)(2,1)S(1)} %bitcast.111), channel_id=1, source_target_pairs={{0,16},{8,24},{16,0},{24,8},{1,17},{9,25},{17,1},{25,9},{2,18},{10... | collective-permute-start | bytes 786440 | tf_op jit(solution)/shard_map/ppermute | solution.py:821
  29.0 12.4 %collective-permute-start.4 = (bf16[256,512]{1,0:T(8,128)(2,1)S(1)}, bf16[256,512]{1,0:T(8,128)(2,1)S(1)}, u32[]{:S(2)}, u32[]{:S(2)}) collective-permute-start(bf16[256,512]{1,0:T(8,128)(2,1)S(1)} %bitcast.112), channel_id=1, source_target_pairs={{0,24},{8,16},{16,8},{24,0},{1,25},{9,17},{17,9},{25,1},{2,26},{10... | collective-permute-start | bytes 786440 | tf_op jit(solution)/shard_map/ppermute | solution.py:821
  44.9 24.7 %collective-permute-start.6 = (bf16[256,2048]{1,0:T(8,128)(2,1)}, bf16[256,2048]{1,0:T(8,128)(2,1)S(1)}, u32[]{:S(2)}, u32[]{:S(2)}) collective-permute-start(bf16[256,2048]{1,0:T(8,128)(2,1)} %later.7.refs_2_.refs_6_.refs_5_.refs_1_), channel_id=1, source_target_pairs={{0,8},{8,0},{16,24},{24,16},{1,9},{9,1},{17,25},{25,17},{2,10},{10... | collective-permute-start | bytes 3145736 | tf_op jit(solution)/shard_map/ppermute | solution.py:821
  46.2 24.7 %collective-permute-start.7 = (bf16[256,2048]{1,0:T(8,128)(2,1)}, bf16[256,2048]{1,0:T(8,128)(2,1)S(1)}, u32[]{:S(2)}, u32[]{:S(2)}) collective-permute-start(bf16[256,2048]{1,0:T(8,128)(2,1)} %later.7.refs_2_.refs_6_.refs_5_.refs_1_), channel_id=1, source_target_pairs={{0,16},{8,24},{16,0},{24,8},{1,17},{9,25},{17,1},{25,9},{2,18},{10... | collective-permute-start | bytes 3145736 | tf_op jit(solution)/shard_map/ppermute | solution.py:821
  47.6 29.1 %collective-permute-start.11 = (bf16[256,2048]{1,0:T(8,128)(2,1)}, bf16[256,2048]{1,0:T(8,128)(2,1)}, u32[]{:S(2)}, u32[]{:S(2)}) collective-permute-start(bf16[256,2048]{1,0:T(8,128)(2,1)} %later.7.refs_2_.refs_6_.refs_5_.refs_1_), channel_id=1, source_target_pairs={{0,1},{1,0},{2,3},{3,2},{4,5},{5,4},{6,7},{7,6},{8,9},{9,8},{10,11... | collective-permute-start | bytes 3145736 | tf_op jit(solution)/shard_map/ppermute | solution.py:821
  60.4 36.4 %collective-permute-start.16 = (bf16[640,1024]{1,0:T(8,128)(2,1)}, bf16[640,1024]{1,0:T(8,128)(2,1)}, u32[]{:S(2)}, u32[]{:S(2)}) collective-permute-start(bf16[640,1024]{1,0:T(8,128)(2,1)} %get-tuple-element.68), channel_id=1, source_target_pairs={{0,1},{1,0},{2,3},{3,2},{4,5},{5,4},{6,7},{7,6},{8,9},{9,8},{10,11... | collective-permute-start | bytes 3932168 | tf_op jit(solution)/shard_map/ppermute | solution.py:821
  74.0 21.4 %collective-permute-start.9 = (bf16[256,1024]{1,0:T(8,128)(2,1)}, bf16[256,1024]{1,0:T(8,128)(2,1)S(1)}, u32[]{:S(2)}, u32[]{:S(2)}) collective-permute-start(bf16[256,1024]{1,0:T(8,128)(2,1)} %get-tuple-element.66), channel_id=1, source_target_pairs={{0,16},{8,24},{16,0},{24,8},{1,17},{9,25},{17,1},{25,9},{2,18},{10... | collective-permute-start | bytes 1572872 | tf_op jit(solution)/shard_map/ppermute | solution.py:821
  75.5 20.2 %collective-permute-start.10 = (bf16[256,1024]{1,0:T(8,128)(2,1)}, bf16[256,1024]{1,0:T(8,128)(2,1)}, u32[]{:S(2)}, u32[]{:S(2)}) collective-permute-start(bf16[256,1024]{1,0:T(8,128)(2,1)} %get-tuple-element.67), channel_id=1, source_target_pairs={{0,8},{8,0},{16,24},{24,16},{1,9},{9,1},{17,25},{25,17},{2,10},{10... | collective-permute-start | bytes 1572872 | tf_op jit(solution)/shard_map/ppermute | solution.py:821
  76.7 21.7 %collective-permute-start.12 = (bf16[256,2048]{1,0:T(8,128)(2,1)}, bf16[256,2048]{1,0:T(8,128)(2,1)S(1)}, u32[]{:S(2)}, u32[]{:S(2)}) collective-permute-start(bf16[256,2048]{1,0:T(8,128)(2,1)} %copy-done), channel_id=1, source_target_pairs={{0,1},{1,0},{2,3},{3,2},{4,5},{5,4},{6,7},{7,6},{8,9},{9,8},{10,11... | collective-permute-start | bytes 3145736 | tf_op jit(solution)/shard_map/ppermute | solution.py:821
  76.7 21.7 %collective-permute-start.13 = (bf16[256,2048]{1,0:T(8,128)(2,1)}, bf16[256,2048]{1,0:T(8,128)(2,1)}, u32[]{:S(2)}, u32[]{:S(2)}) collective-permute-start(bf16[256,2048]{1,0:T(8,128)(2,1)} %copy-done.1), channel_id=1, source_target_pairs={{0,1},{1,0},{2,3},{3,2},{4,5},{5,4},{6,7},{7,6},{8,9},{9,8},{10,11... | collective-permute-start | bytes 3145736 | tf_op jit(solution)/shard_map/ppermute | solution.py:821
  79.7 12.0 %all-to-all-start = ((bf16[32,2,272]{2,1,0:T(2,128)(2,1)}), bf16[32,2,272]{2,1,0:T(2,128)(2,1)S(1)}, u32[]{:S(2)}, u32[]{:S(2)}) async-start(bf16[32,2,272]{2,1,0:T(2,128)(2,1)} %reshape.321), calls=%async_computation | async-start | bytes 98304 | tf_op jit(solution)/shard_map/all_to_all | solution.py:1028
  83.7 128.3 %all-gather.12.cloned.1.call-start = ((), (), s32[]{:S(2)}) async-start(), calls=%async_computation.13 | async-start | bytes 5242880 | tf_op jit(solution)/shard_map/all_gather | solution.py:1061
  96.5 244.7 %reduce-scatter.5.cloned.1.call-start = ((), (), s32[]{:S(2)}) async-start(), calls=%async_computation.9 | async-start | bytes 10485760 | tf_op jit(solution)/shard_map/reduce_scatter | solution.py:1099
  96.8 49.1 %collective-permute-start.17 = (bf16[256,4096]{1,0:T(8,128)(2,1)}, bf16[256,4096]{1,0:T(8,128)(2,1)S(1)}, u32[]{:S(2)}, u32[]{:S(2)}) collective-permute-start(bf16[256,4096]{1,0:T(8,128)(2,1)} %all-gather.8.cloned.1.call-done.refs_16_.refs_4_.refs_6_), channel_id=1, source_target_pairs={{0,8},{8,0},{16,24},{24,16},{1,9},{9,1},{17,25},{25,17},{2,10},{10... | collective-permute-start | bytes 6291464 | tf_op jit(solution)/shard_map/ppermute | solution.py:821
  97.7 48.2 %collective-permute-start.18 = (bf16[256,4096]{1,0:T(8,128)(2,1)}, bf16[256,4096]{1,0:T(8,128)(2,1)S(1)}, u32[]{:S(2)}, u32[]{:S(2)}) collective-permute-start(bf16[256,4096]{1,0:T(8,128)(2,1)} %all-gather.8.cloned.1.call-done.refs_16_.refs_4_.refs_6_), channel_id=1, source_target_pairs={{0,16},{8,24},{16,0},{24,8},{1,17},{9,25},{17,1},{25,9},{2,18},{10... | collective-permute-start | bytes 6291464 | tf_op jit(solution)/shard_map/ppermute | solution.py:821
  112.8 40.0 %collective-permute-start.19 = (bf16[1024,1024]{1,0:T(8,128)(2,1)}, bf16[1024,1024]{1,0:T(8,128)(2,1)}, u32[]{:S(2)}, u32[]{:S(2)}) collective-permute-start(bf16[1024,1024]{1,0:T(8,128)(2,1)} %get-tuple-element.73.refs_1_), channel_id=1, source_target_pairs={{0,1},{1,0},{2,3},{3,2},{4,5},{5,4},{6,7},{7,6},{8,9},{9,8},{10,11... | collective-permute-start | bytes 6291464 | tf_op jit(solution)/shard_map/ppermute | solution.py:821
  150.6 25.6 %collective-permute-start.20 = (bf16[256,2048]{1,0:T(8,128)(2,1)}, bf16[256,2048]{1,0:T(8,128)(2,1)S(1)}, u32[]{:S(2)}, u32[]{:S(2)}) collective-permute-start(bf16[256,2048]{1,0:T(8,128)(2,1)} %get-tuple-element.71.refs_16_), channel_id=1, source_target_pairs={{0,16},{8,24},{16,0},{24,8},{1,17},{9,25},{17,1},{25,9},{2,18},{10... | collective-permute-start | bytes 3145736 | tf_op jit(solution)/shard_map/ppermute | solution.py:821
  151.7 25.5 %collective-permute-start.21 = (bf16[256,2048]{1,0:T(8,128)(2,1)}, bf16[256,2048]{1,0:T(8,128)(2,1)S(1)}, u32[]{:S(2)}, u32[]{:S(2)}) collective-permute-start(bf16[256,2048]{1,0:T(8,128)(2,1)} %get-tuple-element.72.refs_17_), channel_id=1, source_target_pairs={{0,8},{8,0},{16,24},{24,16},{1,9},{9,1},{17,25},{25,17},{2,10},{10... | collective-permute-start | bytes 3145736 | tf_op jit(solution)/shard_map/ppermute | solution.py:821
  178.2 3.4 collective-permute-start.22
  179.4 27.1 %collective-permute-start.23 = (bf16[1024,512]{1,0:T(8,128)(2,1)S(1)}, bf16[1024,512]{1,0:T(8,128)(2,1)S(1)}, u32[]{:S(2)}, u32[]{:S(2)}) collective-permute-start(bf16[1024,512]{1,0:T(8,128)(2,1)S(1)} %copy-done.2), channel_id=1, source_target_pairs={{0,8},{8,0},{16,24},{24,16},{1,9},{9,1},{17,25},{25,17},{2,10},{10... | collective-permute-start | bytes 3145736 | tf_op jit(solution)/shard_map/ppermute | solution.py:821
  180.6 26.0 %collective-permute-start.24 = (bf16[1024,512]{1,0:T(8,128)(2,1)S(1)}, bf16[1024,512]{1,0:T(8,128)(2,1)S(1)}, u32[]{:S(2)}, u32[]{:S(2)}) collective-permute-start(bf16[1024,512]{1,0:T(8,128)(2,1)S(1)} %copy-done.2), channel_id=1, source_target_pairs={{0,16},{8,24},{16,0},{24,8},{1,17},{9,25},{17,1},{25,9},{2,18},{10... | collective-permute-start | bytes 3145736 | tf_op jit(solution)/shard_map/ppermute | solution.py:821
  210.0 19.2 %collective-permute-start.25 = (bf16[1024,256]{1,0:T(8,128)(2,1)}, bf16[1024,256]{1,0:T(8,128)(2,1)S(1)}, u32[]{:S(2)}, u32[]{:S(2)}) collective-permute-start(bf16[1024,256]{1,0:T(8,128)(2,1)} %get-tuple-element.78.refs_3_), channel_id=1, source_target_pairs={{0,16},{8,24},{16,0},{24,8},{1,17},{9,25},{17,1},{25,9},{2,18},{10... | collective-permute-start | bytes 1572872 | tf_op jit(solution)/shard_map/ppermute | solution.py:821
  211.1 18.2 %collective-permute-start.26 = (bf16[1024,256]{1,0:T(8,128)(2,1)}, bf16[1024,256]{1,0:T(8,128)(2,1)S(1)}, u32[]{:S(2)}, u32[]{:S(2)}) collective-permute-start(bf16[1024,256]{1,0:T(8,128)(2,1)} %get-tuple-element.79.refs_4_), channel_id=1, source_target_pairs={{0,8},{8,0},{16,24},{24,16},{1,9},{9,1},{17,25},{25,17},{2,10},{10... | collective-permute-start | bytes 1572872 | tf_op jit(solution)/shard_map/ppermute | solution.py:821
  230.3 152.4 %reduce-scatter.7.cloned.1.call-start = ((), (), s32[]{:S(2)}) async-start(), calls=%async_computation.10 | async-start | bytes 2621440 | tf_op jit(solution)/shard_map/reduce_scatter | solution.py:900
  281.0 4.3 collective-permute-start.27
  281.1 52.7 %collective-permute-start.28 = (bf16[1024,1024]{1,0:T(8,128)(2,1)S(1)}, bf16[1024,1024]{1,0:T(8,128)(2,1)}, u32[]{:S(2)}, u32[]{:S(2)}) collective-permute-start(bf16[1024,1024]{1,0:T(8,128)(2,1)S(1)} %copy-done.4), channel_id=1, source_target_pairs={{0,1},{1,0},{2,3},{3,2},{4,5},{5,4},{6,7},{7,6},{8,9},{9,8},{10,11... | collective-permute-start | bytes 6291464 | tf_op jit(solution)/shard_map/ppermute | solution.py:821
  281.6 42.6 %collective-permute-start.30 = (bf16[256,2048]{1,0:T(8,128)(2,1)}, bf16[256,2048]{1,0:T(8,128)(2,1)S(1)}, u32[]{:S(2)}, u32[]{:S(2)}) collective-permute-start(bf16[256,2048]{1,0:T(8,128)(2,1)} %get-tuple-element.86), channel_id=1, source_target_pairs={{0,8},{8,0},{16,24},{24,16},{1,9},{9,1},{17,25},{25,17},{2,10},{10... | collective-permute-start | bytes 3145736 | tf_op jit(solution)/shard_map/ppermute | solution.py:821
  282.3 43.1 %collective-permute-start.31 = (bf16[256,2048]{1,0:T(8,128)(2,1)}, bf16[256,2048]{1,0:T(8,128)(2,1)S(1)}, u32[]{:S(2)}, u32[]{:S(2)}) collective-permute-start(bf16[256,2048]{1,0:T(8,128)(2,1)} %get-tuple-element.87), channel_id=1, source_target_pairs={{0,16},{8,24},{16,0},{24,8},{1,17},{9,25},{17,1},{25,9},{2,18},{10... | collective-permute-start | bytes 3145736 | tf_op jit(solution)/shard_map/ppermute | solution.py:821
  301.1 32.7 %collective-permute-start.29 = (bf16[1024,512]{1,0:T(8,128)(2,1)}, bf16[1024,512]{1,0:T(8,128)(2,1)S(1)}, u32[]{:S(2)}, u32[]{:S(2)}) collective-permute-start(bf16[1024,512]{1,0:T(8,128)(2,1)} %get-tuple-element.84), channel_id=1, source_target_pairs={{0,1},{1,0},{2,3},{3,2},{4,5},{5,4},{6,7},{7,6},{8,9},{9,8},{10,11... | collective-permute-start | bytes 3145736 | tf_op jit(solution)/shard_map/ppermute | solution.py:821
  319.8 69.0 %collective-permute-start.33 = (bf16[3,1024,512]{2,1,0:T(8,128)(2,1)}, bf16[3,1024,512]{2,1,0:T(8,128)(2,1)}, u32[]{:S(2)}, u32[]{:S(2)}) collective-permute-start(bf16[3,1024,512]{2,1,0:T(8,128)(2,1)} %attention_backward.2.refs_5_.refs_1_), channel_id=1, source_target_pairs={{0,1},{1,0},{2,3},{3,2},{4,5},{5,4},{6,7},{7,6},{8,9},{9,8},{10,11... | collective-permute-start | bytes 9437192 | tf_op jit(solution)/shard_map/ppermute | solution.py:821
  331.7 49.5 %collective-permute-start.34 = (bf16[256,4096]{1,0:T(8,128)(2,1)}, bf16[256,4096]{1,0:T(8,128)(2,1)}, u32[]{:S(2)}, u32[]{:S(2)}) collective-permute-start(bf16[256,4096]{1,0:T(8,128)(2,1)} %get-tuple-element.90.refs_5_.refs_1_), channel_id=1, source_target_pairs={{0,8},{8,0},{16,24},{24,16},{1,9},{9,1},{17,25},{25,17},{2,10},{10... | collective-permute-start | bytes 6291464 | tf_op jit(solution)/shard_map/ppermute | solution.py:821
  332.9 48.4 %collective-permute-start.35 = (bf16[256,4096]{1,0:T(8,128)(2,1)}, bf16[256,4096]{1,0:T(8,128)(2,1)}, u32[]{:S(2)}, u32[]{:S(2)}) collective-permute-start(bf16[256,4096]{1,0:T(8,128)(2,1)} %get-tuple-element.91.refs_6_.refs_2_), channel_id=1, source_target_pairs={{0,16},{8,24},{16,0},{24,8},{1,17},{9,25},{17,1},{25,9},{2,18},{10... | collective-permute-start | bytes 6291464 | tf_op jit(solution)/shard_map/ppermute | solution.py:821
  341.2 115.7 %reduce-scatter.11.cloned.1.call-start = ((), (), s32[]{:S(2)}) async-start(), calls=%async_computation.12 | async-start | bytes 2621440 | tf_op jit(solution)/shard_map/reduce_scatter | solution.py:900
  387.6 92.3 %reduce-scatter.9.cloned.1.call-start = ((), (), s32[]{:S(2)}) async-start(), calls=%async_computation.11 | async-start | bytes 1310720 | tf_op jit(solution)/shard_map/reduce_scatter | solution.py:900
  388.9 18.4 %collective-permute-start.32 = (bf16[640,1024]{1,0:T(8,128)(2,1)S(1)}, bf16[640,1024]{1,0:T(8,128)(2,1)}, u32[]{:S(2)}, u32[]{:S(2)}) collective-permute-start(bf16[640,1024]{1,0:T(8,128)(2,1)S(1)} %copy-done.52), channel_id=1, source_target_pairs={{0,1},{1,0},{2,3},{3,2},{4,5},{5,4},{6,7},{7,6},{8,9},{9,8},{10,11... | collective-permute-start | bytes 3932168 | tf_op jit(solution)/shard_map/ppermute | solution.py:821
  401.7 14.5 %collective-permute-start.36 = (bf16[256,1024]{1,0:T(8,128)(2,1)}, bf16[256,1024]{1,0:T(8,128)(2,1)S(1)}, u32[]{:S(2)}, u32[]{:S(2)}) collective-permute-start(bf16[256,1024]{1,0:T(8,128)(2,1)} %get-tuple-element.98.refs_6_), channel_id=1, source_target_pairs={{0,8},{8,0},{16,24},{24,16},{1,9},{9,1},{17,25},{25,17},{2,10},{10... | collective-permute-start | bytes 1572872 | tf_op jit(solution)/shard_map/ppermute | solution.py:821
  403.2 14.3 %collective-permute-start.37 = (bf16[256,1024]{1,0:T(8,128)(2,1)}, bf16[256,1024]{1,0:T(8,128)(2,1)S(1)}, u32[]{:S(2)}, u32[]{:S(2)}) collective-permute-start(bf16[256,1024]{1,0:T(8,128)(2,1)} %get-tuple-element.101), channel_id=1, source_target_pairs={{0,16},{8,24},{16,0},{24,8},{1,17},{9,25},{17,1},{25,9},{2,18},{10... | collective-permute-start | bytes 1572872 | tf_op jit(solution)/shard_map/ppermute | solution.py:821
  422.3 24.8 %collective-permute-start.38 = (bf16[256,2048]{1,0:T(8,128)(2,1)}, bf16[256,2048]{1,0:T(8,128)(2,1)S(1)}, u32[]{:S(2)}, u32[]{:S(2)}) collective-permute-start(bf16[256,2048]{1,0:T(8,128)(2,1)} %get-tuple-element.102.refs_7_), channel_id=1, source_target_pairs={{0,8},{8,0},{16,24},{24,16},{1,9},{9,1},{17,25},{25,17},{2,10},{10... | collective-permute-start | bytes 3145736 | tf_op jit(solution)/shard_map/ppermute | solution.py:821
  422.8 24.7 %collective-permute-start.39 = (bf16[256,2048]{1,0:T(8,128)(2,1)}, bf16[256,2048]{1,0:T(8,128)(2,1)S(1)}, u32[]{:S(2)}, u32[]{:S(2)}) collective-permute-start(bf16[256,2048]{1,0:T(8,128)(2,1)} %get-tuple-element.103.refs_8_), channel_id=1, source_target_pairs={{0,16},{8,24},{16,0},{24,8},{1,17},{9,25},{17,1},{25,9},{2,18},{10... | collective-permute-start | bytes 3145736 | tf_op jit(solution)/shard_map/ppermute | solution.py:821
  456.2 4.9 collective-permute-start.40
  458.2 18.6 %collective-permute-start.41 = (f32[32,4096]{1,0:T(8,128)S(1)}, f32[32,4096]{1,0:T(8,128)S(1)}, u32[]{:S(2)}, u32[]{:S(2)}) collective-permute-start(f32[32,4096]{1,0:T(8,128)S(1)} %get-tuple-element.118), channel_id=1, source_target_pairs={{0,1},{1,0},{2,3},{3,2},{4,5},{5,4},{6,7},{7,6},{8,9},{9,8},{10,11... | collective-permute-start | bytes 1572872 | tf_op jit(solution)/shard_map/ppermute | solution.py:821
  463.0 11.9 %all-to-all-start.1 = ((f32[32,1,384]{2,1,0:T(1,128)}), f32[32,1,384]{2,1,0:T(1,128)S(1)}, u32[]{:S(2)}, u32[]{:S(2)}) async-start(f32[32,1,384]{2,1,0:T(1,128)} %copy.118), calls=%async_computation.3 | async-start | bytes 98304 | tf_op jit(solution)/shard_map/all_to_all | solution.py:1157
  (61 other events, 460.6 us)
Sparse Core Ops, SparseCore 0:
  14.1 30.5 all-gather.5
  46.8 46.4 all-gather.7
  95.5 26.6 all-gather.9
  124.2 80.2 all-gather.11
  230.4 100.8 reduce-scatter.4
  341.3 41.2 reduce-scatter.6
  387.7 43.1 reduce-scatter.10
  452.7 26.9 reduce-scatter.8

commit v4 on v3

--- a/solution.py
+++ b/solution.py
@@ -438,7 +438,7 @@
         block,
         shape_of((rows, width), bf16),
         after=after,
-        work=(4 * CAPACITY * rows * width, 6 * rows * width + 4 * CAPACITY * width),
+        work=(0, 2 * rows * width),
     )
 
 
@@ -478,7 +478,7 @@
             shape_of((4, half), f32),
         ),
         after=after,
-        work=(6 * rows * width * width, 16 * rows * width + 6 * width * width),
+        work=(0, 2 * rows * width),
     )
 
 
@@ -886,10 +886,27 @@
     )
 
 
-def to_core(total):
-    core = lax.axis_index("c")
-    halves = total.reshape(2, total.shape[0] // 2, total.shape[1])
-    return pick(halves, core), swap_core(pick(halves, 1 - core))
+def pair_kernel(core, mine_ref, other_ref, out_ref):
+    mine, other = mine_ref[0].astype(f32), other_ref[...].astype(f32)
+    out_ref[:, 0, :] = jnp.where(core[0] == 0, mine, other)
+    out_ref[:, 1, :] = jnp.where(core[0] == 0, other, mine)
+
+
+def pair(core, total):
+    rows, columns = total.shape[0] // 2, total.shape[1]
+    halves = total.reshape(2, rows, columns)
+    other = swap_core(pick(halves, 1 - core[0]))
+    return launch(
+        pair_kernel,
+        "pair",
+        (1,),
+        (halves, other),
+        [pl.BlockSpec((1, rows, columns), lambda i, c: (c[0], 0, 0)), whole(rows, columns)],
+        whole(rows, 2, columns),
+        shape_of((rows, 2, columns), f32),
+        scalars=(core,),
+        work=(0, 2 * rows * columns),
+    )
 
 
 def gather_z(shard):
@@ -1111,60 +1128,60 @@
     other_projected = swap_core(other_projected)
     qkv_away = attention_grad(qkv, attended_grad, lse, seg_col, seg_row, 1 - core)
     qkv_got = swap_core(qkv_away)
-    up_next = scatter_next(me, up_partial, *up_far, after=(qkv_away,)) if square else ()
     partial = two_sum(
-        me, 4, attended, mine_projected[None], other_attended, other_projected[None], 0, after=up_next
-    )
+        me, 4, attended, mine_projected[None], other_attended, other_projected[None], 0, after=(qkv_away,)
+    )
+    up_next = scatter_next(me, up_partial, *up_far, after=partial[:1]) if square else partial[:1]
     down_total = scatter_z(later(down_half, up_next))
-    y_keep, y_away = down(me, act, w_down, right, after=partial[:1])
-    y_got = swap_core(y_away)
-    qkv_kept = attention_grad(qkv, attended_grad, lse, seg_col, seg_row, core, after=(y_keep,))
-    if square:
-        up_block = scatter_near(me, up_partial, *swap_near(*up_next), after=(qkv_kept, down_total))
-    else:
-        up_block = lax.psum_scatter(up_partial, "dp", scatter_dimension=0, tiled=True)
-    up_total = scatter_z(up_block)
-    partial, out_x, out_y = two_sum(
-        me, 4, normed_one, qkv_kept, other_normed_one, qkv_got, 1, into=partial, after=(up_block,)
+    qkv_kept = attention_grad(qkv, attended_grad, lse, seg_col, seg_row, core, after=up_next)
+    partial, out_x, out_y = two_sum(me, 4, normed_one, qkv_kept, other_normed_one, qkv_got, 1, into=partial)
+    input_grad, gain_one_grad, shift_one_grad, bias_sums = input_grads(
+        qkv_kept, qkv_away, tokens, middle_grads, mine_w, other_w, gain_one, after=(out_x,)
     )
     if square:
         partial = partial.reshape(4, width // 4, -1)
         far = swap_near(out_x, out_y)
-    block_out = output(slot_col, expert_ids, y_keep, y_got, middle, bias_down, after=(out_x,))
-    near = scatter_next(me, partial, *far, after=(block_out,)) if square else ()
-    input_grad, gain_one_grad, shift_one_grad, bias_sums = input_grads(
-        qkv_kept, qkv_away, tokens, middle_grads, mine_w, other_w, gain_one, after=near
-    )
+        up_block = scatter_near(me, up_partial, *swap_near(*up_next), after=(input_grad, down_total))
+        up_block = later(up_block, far)
+        near = scatter_next(me, partial, *far, after=(up_block,))
+        near_got = swap_near(*near)
+    else:
+        near = ()
+        up_block = lax.psum_scatter(up_partial, "dp", scatter_dimension=0, tiled=True)
+    up_total = scatter_z(up_block)
+    down_weight_grad = pair(side, down_total)
+    y_keep, y_away = down(me, act, w_down, right, after=(*near, down_weight_grad))
+    y_got = swap_core(y_away)
+    if square:
+        last = scatter_near(me, partial, *near_got, after=(y_keep,))
+    else:
+        last = lax.psum_scatter(partial, "dp", scatter_dimension=0, tiled=True)
+    block_out = output(slot_col, expert_ids, y_keep, y_got, middle, bias_down, after=(last,))
     query_bias_grad = by_core(core, bias_sums[0], bias_sums[1])
     value_bias_grad = by_core(core, bias_sums[2], bias_sums[3])
-    if square:
-        last = scatter_near(me, partial, *swap_near(*near), after=(input_grad,))
-    else:
-        last = lax.psum_scatter(partial, "dp", scatter_dimension=0, tiled=True)
 
     vectors = [
         gain_one_grad,
         shift_one_grad,
-        query_bias_grad,
-        value_bias_grad,
+        query_bias_grad.reshape(1, width),
+        value_bias_grad.reshape(1, width),
         out_bias_grad,
         gain_two_grad,
         shift_two_grad,
-        up_bias_grad,
         down_bias_grad,
     ]
-    sent = later(jnp.concatenate([v.reshape(devices, -1) for v in vectors], 1), (last,))
+    vectors = jnp.concatenate([v.reshape(1, width) for v in vectors], 0).reshape(8, devices, share)
+    vectors = jnp.swapaxes(vectors, 0, 1).reshape(devices, 8 * share)
+    sent = later(jnp.concatenate([vectors, up_bias_grad.reshape(devices, up_share)], 1), (last,))
     got = lax.all_to_all(sent, ALL, 0, 0, tiled=True).reshape(devices // 2, 2, -1)
     both = jnp.sum(got, 0)
     total = both[0] + both[1]
     sums = [total[i * share : (i + 1) * share] for i in range(7)]
-    at = 7 * share
-    up_bias_sum = both[:, at : at + up_share]
-    down_bias_sum = both[:, at + up_share :]
-
-    down_weight_grad = by_core(core, *to_core(down_total.astype(f32)), 1)
-    up_weight_grad = by_core(core, *to_core(up_total.astype(f32)), 1)
-    out_weight_grad, qkv_weight_grad = finish(side, later(scatter_z(last), (up_bias_sum, down_weight_grad, up_weight_grad)))
+    down_bias_sum = both[:, 7 * share : 8 * share]
+    up_bias_sum = both[:, 8 * share :]
+
+    up_weight_grad = pair(side, up_total)
+    out_weight_grad, qkv_weight_grad = finish(side, later(scatter_z(last), (up_bias_sum, down_weight_grad, up_weight_grad, block_out)))
     return (
         block_out,
         input_grad,

time: 502 us -> 487 us (0.970)
  waiting for transfers between devices: 55 us -> 42.9 us
  other arithmetic: 14.9 us -> 9.3 us
    ppermute x43, waiting for transfers between devices: 41.2 us -> 30.6 us  [swap(): return lax.ppermute(value, axis, [(i, i ^ mask) for i in range(size)])]
    pallas_call x28 -> x30, Pallas kernels: 303 us -> 308 us  [launch(): pl.pallas_call(body, grid_spec=pltpu.PrefetchScalarGridSpec(num_scalar_pr...]
    unnamed x126 -> x130, local copies, waits for them, and re-layouts: 24.4 us -> 26.6 us
  transfers between devices with their start and end apart: 53 -> 53, of which waited for: 19 -> 17; matrix products, arithmetic and copies ran while one was open for 8% -> 6% of each run, Pallas kernels for 65% -> 68%
where the time goes in v4:
time: 487 us; the launch traced here: 477 us
  Pallas kernels  327 us (67%)
  local copies, waits for them, and re-layouts  45.9 us (9%)
  waiting for transfers between devices  42.9 us (9%)
  starting transfers between devices  36.9 us (8%)
  between operations  15.2 us (3%)
  other arithmetic  9.3 us (2%)
    pallas_call x30, Pallas kernels, launch(): pl.pallas_call(body, grid_spec=pltpu.PrefetchScalarGridSpec(num_scalar_pr...  308 us
    ppermute x43, waiting for transfers between devices, swap(): return lax.ppermute(value, axis, [(i, i ^ mask) for i in range(size)])  30.6 us
    ppermute x43, starting transfers between devices, swap(): return lax.ppermute(value, axis, [(i, i ^ mask) for i in range(size)])  29.8 us
    unnamed x130, local copies, waits for them, and re-layouts  26.6 us
    pallas_call x2, Pallas kernels, two_sum(): pl.pallas_call(body, grid_spec=pltpu.PrefetchScalarGridSpec(num_scalar_pr...  19 us
  transfers between devices with their start and end apart: 53, of which 17 were waited for; matrix products, arithmetic and copies ran while one was open for 6% of the time, Pallas kernels for 68%

profile of v4, /device:TPU:0, one launch (start us, length us, event | category | flops | bytes accessed | tf_op | source)
XLA Modules:
  0.0 477.1 jit_solution(2637371830177213925)
XLA Ops:
  8.5 1.6 dynamic-slice_reduce_fusion
  12.3 1.7 place.7
  19.5 1.7 place.8
  21.9 1.8 place.9
  24.8 2.7 collective-permute-start.2
  27.5 1.5 collective-permute-start.3
  30.1 4.5 collective-permute-done.2.refs_2_
  34.6 6.8 %collective-permute-done.3.refs_3_ = bf16[256,512]{1,0:T(8,128)(2,1)S(1)} collective-permute-done((bf16[256,512]{1,0:T(8,128)(2,1)S(1)}, bf16[256,512]{1,0:T(8,128)(2,1)S(1)}, u32[]{:S(2)}, u32[]{:S(2)}) %collective-permute-start.3) | collective-permute-done | bytes 262176 | tf_op jit(solution)/shard_map/ppermute | solution.py:821
  42.2 2.7 place.10
  46.2 1.5 collective-permute-start.7
  49.8 8.1 %dispatch.1 = (bf16[640,1024]{1,0:T(8,128)(2,1)}, bf16[640,1024]{1,0:T(8,128)(2,1)}) custom-call(s32[1,1024]{1,0:T(1,128)} %add.50.refs_0_.refs_2_, bf16[1024,1024]{1,0:T(8,128)(2,1)} %refs_5_.1, bf16[256,2048]{1,0:T(8,128)(2,1)} %later.8.refs_2_.refs_6_.refs_5_.refs_1_), custom_call_target="tpu_custom_call" | custom-call | flops 5368709120 | bytes 4718592 | tf_op jit(solution)/shard_map/dispatch/pallas_call | solution.py:44
  58.7 1.8 place.11
  61.0 8.7 %collective-permute-done.6.refs_0_.refs_7_.refs_6_.refs_2_ = bf16[256,2048]{1,0:T(8,128)(2,1)S(1)} collective-permute-done((bf16[256,2048]{1,0:T(8,128)(2,1)}, bf16[256,2048]{1,0:T(8,128)(2,1)S(1)}, u32[]{:S(2)}, u32[]{:S(2)}) %collective-permute-start.6) | collective-permute-done | bytes 1048608 | tf_op jit(solution)/shard_map/ppermute | solution.py:821
  71.9 2.1 cut_halves.3
  74.0 1.5 collective-permute-start.9
  79.7 4.0 all-to-all-start
  84.8 6.8 %all-to-all-done = bf16[32,2,272]{2,1,0:T(2,128)(2,1)S(1)} async-done(((bf16[32,2,272]{2,1,0:T(2,128)(2,1)}), bf16[32,2,272]{2,1,0:T(2,128)(2,1)S(1)}, u32[]{:S(2)}, u32[]{:S(2)}) %all-to-all-start) | async-done | bytes 34848 | tf_op jit(solution)/shard_map/all_to_all | solution.py:1045
  99.4 13.3 %project.1 = (bf16[1024,1024]{1,0:T(8,128)(2,1)}, bf16[1024,3072]{1,0:T(8,128)(2,1)}) custom-call(s32[1]{0:T(128)} %bitcast.3.refs_0_, s32[1]{0:T(128)} %bitcast.2.refs_0_.refs_1_, bf16[1024,1024]{1,0:T(8,128)(2,1)} %refs_2_.7, f32[1,1024]{1,0:T(1,128)} %reshape.209.refs_3_.refs_6_, f32[1,1024]{1,0:T(1,128)} %reshape.210.refs_4_, ...), custom_call_target="tpu_custom_call" | custom-call | flops 12884901888 | bytes 16777216 | tf_op jit(solution)/shard_map/project/pallas_call | solution.py:44
  113.1 32.8 %attention_forward.1 = (bf16[1024,1024]{1,0:T(8,128)(2,1)}, f32[8,2,1024]{2,1,0:T(2,128)}) custom-call(s32[1024,1]{1,0:T(8,128)} %copy.136.refs_0_.refs_1_, s32[1,1024]{1,0:T(1,128)} %refs_2_.6, bf16[1024,3072]{1,0:T(8,128)(2,1)} %get-tuple-element.69.refs_2_.refs_3_.refs_4_.refs_5_, bf16[1024,3072]{1,0:T(8,128)(2,1)} %get-tuple-element.69.refs_2_.refs_3_.refs_4_.refs_5_, ...), custom_call_target="tpu_custom_call" | custom-call | flops 34359738368 | bytes 8388608 | tf_op jit(solution)/shard_map/attention_forward/pallas_call | solution.py:44
  147.9 2.7 cut_halves.4
  152.8 13.9 %middle.1 = (f32[1024,1024]{1,0:T(8,128)}, bf16[640,1024]{1,0:T(8,128)(2,1)}, bf16[640,1024]{1,0:T(8,128)(2,1)}) custom-call(s32[1]{0:T(128)} %bitcast.3.refs_0_, s32[1]{0:T(128)} %bitcast.2.refs_0_.refs_1_, s32[1,1024]{1,0:T(1,128)} %add.50.refs_0_.refs_2_, bf16[1024,1024]{1,0:T(8,128)(2,1)} %refs_2_.7, ...), custom_call_target="tpu_custom_call" | custom-call | flops 9663676416 | bytes 13107200 | tf_op jit(solution)/shard_map/middle/pallas_call | solution.py:44
  166.7 4.7 place.12
  171.3 4.7 place.13
  181.5 25.0 %experts_up.1 = (bf16[1280,4096]{1,0:T(8,128)(2,1)}, bf16[1280,4096]{1,0:T(8,128)(2,1)}) custom-call(s32[1]{0:T(128)} %bitcast.2.refs_0_.refs_1_, bf16[640,1024]{1,0:T(8,128)(2,1)} %get-tuple-element.74.refs_1_.refs_3_, bf16[640,1024]{1,0:T(8,128)(2,1)} %collective-permute-done.22.refs_2_.refs_4_, f32[1,4096]{1,0:T(1,128)} %dynamic-slice_bitcast_fusion.3.refs_3_, ...), custom_call_target="tpu_custom_call" | custom-call | flops 21474836480 | bytes 29360128 | tf_op jit(solution)/shard_map/experts_up/pallas_call | solution.py:44
  207.9 2.0 cut_halves.5
  212.0 17.0 %experts_outer.1 = (bf16[4096,1024]{1,0:T(8,128)(2,1)}, f32[1,1024]{1,0:T(1,128)}) custom-call(bf16[1280,4096]{1,0:T(8,128)(2,1)} %get-tuple-element.77.refs_2_.refs_0_.refs_1_, bf16[640,1024]{1,0:T(8,128)(2,1)} %get-tuple-element.65.refs_3_.refs_1_, bf16[640,1024]{1,0:T(8,128)(2,1)} %collective-permute-done.16.refs_17_.refs_2_, ...), custom_call_target="tpu_custom_call" | custom-call | flops 21474836480 | bytes 18874368 | tf_op jit(solution)/shard_map/experts_outer/pallas_call | solution.py:44
  230.0 50.7 %experts_grad.1 = (bf16[640,1024]{1,0:T(8,128)(2,1)}, bf16[640,1024]{1,0:T(8,128)(2,1)}, bf16[1024,4096]{1,0:T(8,128)(2,1)}, bf16[256,2048]{1,0:T(8,128)(2,1)}, ...) custom-call(s32[1]{0:T(128)} %bitcast.2.refs_0_.refs_1_, bf16[640,1024]{1,0:T(8,128)(2,1)} %get-tuple-element.65.refs_3_.refs_1_, ...), custom_call_target="tpu_custom_call" | custom-call | flops 64424509440 | bytes 35651584 | tf_op jit(solution)/shard_map/experts_grad/pallas_call | solution.py:44
  283.0 2.0 collective-permute-done.27.refs_3_
  286.2 14.8 %middle_grad.1 = (f32[1024,1024]{1,0:T(8,128)}, bf16[1024,512]{1,0:T(8,128)(2,1)}, bf16[1024,512]{1,0:T(8,128)(2,1)}, bf16[1024,1024]{1,0:T(8,128)(2,1)}, f32[1,...) custom-call(s32[1]{0:T(128)} %bitcast.3.refs_0_, s32[1024,1]{1,0:T(8,128)} %get-tuple-element.126.refs_1_.refs_0_, ...), custom_call_target="tpu_custom_call" | custom-call | flops 9663676416 | bytes 19398656 | tf_op jit(solution)/shard_map/middle_grad/pallas_call | solution.py:44
  301.1 18.8 %attention_backward.2.refs_5_.refs_1_ = bf16[3,1024,512]{2,1,0:T(8,128)(2,1)} custom-call(s32[1]{0:T(128)} %bitcast.26.refs_0_, s32[1024,1]{1,0:T(8,128)} %copy.136.refs_0_.refs_1_, s32[1,1024]{1,0:T(1,128)} %refs_2_.6, bf16[1024,3072]{1,0:T(8,128)(2,1)} %get-tuple-element.69.refs_2_.refs_3_.refs_4_.refs_5_, ...), custom_call_target="tpu_custom_call" | custom-call | flops 25769803776 | bytes 8388608 | tf_op jit(solution)/shard_map/attention_backward/pallas_call | solution.py:44
  321.5 6.4 %two_sum.2 = (bf16[1024,2048]{1,0:T(8,128)(2,1)}, bf16[256,1024]{1,0:T(8,128)(2,1)}, bf16[256,1024]{1,0:T(8,128)(2,1)}) custom-call(s32[1]{0:T(128)} %bitcast.2.refs_0_.refs_1_, bf16[1024,1024]{1,0:T(8,128)(2,1)} %get-tuple-element.70.refs_2_.refs_4_.refs_1_, bf16[1,1024,512]{2,1,0:T(8,128)(2,1)} %bitcast.154, ...), custom_call_target="tpu_custom_call" | custom-call | flops 4294967296 | bytes 6291456 | tf_op jit(solution)/shard_map/two_sum/pallas_call | solution.py:516
  329.2 5.3 %far_add.2 = (bf16[256,4096]{1,0:T(8,128)(2,1)}, bf16[256,4096]{1,0:T(8,128)(2,1)}) custom-call(s32[1]{0:T(128)} %bitcast.2.refs_0_.refs_1_, bf16[4,256,4096]{2,1,0:T(8,128)(2,1)} %bitcast.87, bf16[4,256,4096]{2,1,0:T(8,128)(2,1)} %bitcast.88, bf16[256,2048]{1,0:T(8,128)(2,1)} %copy-done.17, bf16[256,2048]{1,0:T(8,128)(2,1)} %copy-done.18, ...), custom_call_target="tpu_custom_call" | custom-call | tf_op jit(solution)/shard_map/far_add/pallas_call | solution.py:44
  335.6 18.8 %attention_backward.3.refs_2_.refs_0_ = bf16[3,1024,512]{2,1,0:T(8,128)(2,1)} custom-call(s32[1]{0:T(128)} %bitcast.22.refs_0_, s32[1024,1]{1,0:T(8,128)} %copy.136.refs_0_.refs_1_, s32[1,1024]{1,0:T(1,128)} %refs_2_.6, bf16[1024,3072]{1,0:T(8,128)(2,1)} %get-tuple-element.69.refs_2_.refs_3_.refs_4_.refs_5_, ...), custom_call_target="tpu_custom_call" | custom-call | flops 25769803776 | bytes 8388608 | tf_op jit(solution)/shard_map/attention_backward/pallas_call | solution.py:44
  354.4 12.6 %two_sum.3 = (bf16[1024,2048]{1,0:T(8,128)(2,1)}, bf16[256,1024]{1,0:T(8,128)(2,1)}, bf16[256,1024]{1,0:T(8,128)(2,1)}) custom-call(s32[1]{0:T(128)} %bitcast.2.refs_0_.refs_1_, bf16[1024,1024]{1,0:T(8,128)(2,1)} %get-tuple-element.73.refs_1_, ...), custom_call_target="tpu_custom_call", output_to_operand_aliasing={{0}: (5, {}), {1}: (6, {}), {2}: (7, {})} | custom-call | flops 12884901888 | bytes 10485760 | tf_op jit(solution)/shard_map/two_sum/pallas_call | solution.py:516
  367.9 2.1 collective-permute-start.34
  370.0 14.6 %input_grad.1 = (f32[1024,1024]{1,0:T(8,128)}, f32[1,1024]{1,0:T(1,128)}, f32[1,1024]{1,0:T(1,128)}, f32[4,512]{1,0:T(4,128)}) custom-call(bf16[3,1024,512]{2,1,0:T(8,128)(2,1)} %attention_backward.3.refs_2_.refs_0_, bf16[3,1024,512]{2,1,0:T(8,128)(2,1)} %attention_backward.2.refs_5_.refs_1_, bf16[1024,1024]{1,0:T(8,128)(2,1)} %refs_2_.7, ...), custom_call_target="tpu_custom_call" | custom-call | bytes 2097152 | tf_op jit(solution)/shard_map/input_grad/pallas_call | solution.py:44
  384.7 4.9 %near_add.2.refs_0_ = bf16[256,4096]{1,0:T(8,128)(2,1)} custom-call(s32[1]{0:T(128)} %bitcast.2.refs_0_.refs_1_, bf16[4,256,4096]{2,1,0:T(8,128)(2,1)} %bitcast.89, bf16[256,4096]{1,0:T(8,128)(2,1)} %collective-permute-done.35.refs_2_, bf16[256,4096]{1,0:T(8,128)(2,1)} %collective-permute-done.36.refs_3_, f32[1024,1024]{1,0:T(8,128)} %get-tuple-element.51.refs_4_, ...), custom_call_target="tpu_custom_call" | custom-call | tf_op jit(solution)/shard_map/near_add/pallas_call | solution.py:44
  389.5 4.1 collective-permute-done.33.refs_1_.refs_3_
  396.4 4.4 far_add.3
  402.7 2.3 pair.2.refs_10_.refs_2_
  405.0 21.3 %experts_down.1 = (bf16[640,1024]{1,0:T(8,128)(2,1)}, bf16[640,1024]{1,0:T(8,128)(2,1)}) custom-call(s32[1]{0:T(128)} %bitcast.2.refs_0_.refs_1_, bf16[1280,4096]{1,0:T(8,128)(2,1)} %get-tuple-element.77.refs_2_.refs_0_.refs_1_, bf16[1024,512]{1,0:T(8,128)(2,1)} %later.9.refs_3_.refs_11_.refs_2_, bf16[1024,512]{1,0:T(8,128)(2,1)} %copy-done.12, ...), custom_call_target="tpu_custom_call" | custom-call | flops 21474836480 | bytes 18874368 | tf_op jit(solution)/shard_map/experts_down/pallas_call | solution.py:44
  428.3 4.0 near_add.3.refs_6_.refs_1_
  439.9 2.6 all-to-all-start.1
  446.5 3.7 all-to-all-done.1
  452.6 7.9 %output.1.refs_4_ = bf16[1024,1024]{1,0:T(8,128)(2,1)} custom-call(s32[1024,1]{1,0:T(8,128)} %get-tuple-element.126.refs_1_.refs_0_, s32[1024,1]{1,0:T(8,128)} %copy.141.refs_1_, bf16[640,1024]{1,0:T(8,128)(2,1)} %get-tuple-element.103.refs_4_.refs_2_, bf16[640,1024]{1,0:T(8,128)(2,1)} %copy-done.11, f32[1024,1024]{1,0:T(8,128)} %get-tuple-element.76.refs_1_.refs_6_.refs_4_, ...), custom_call_target="tpu_custom_call" | custom-call | bytes 2097152 | tf_op jit(solution)/shard_map/output/pallas_call | solution.py:44
  461.2 2.3 pair.3.refs_3_
  463.5 1.7 reduce-scatter.9.cloned.1.call-done.refs_0_
  468.2 1.8 finish.1
  (304 shorter events, 79.2 us)
Async XLA Ops:
  7.2 37.8 %all-gather.6.cloned.1.call-start = ((), (), s32[]{:S(2)}) async-start(), calls=%async_computation.6 | async-start | bytes 1310720 | tf_op jit(solution)/shard_map/all_gather | solution.py:913
  14.0 82.8 %all-gather.8.cloned.1.call-start = ((), (), s32[]{:S(2)}) async-start(), calls=%async_computation.7 | async-start | bytes 2621440 | tf_op jit(solution)/shard_map/all_gather | solution.py:913
  15.6 5.6 %collective-permute-start.5 = (bf16[32,4096]{1,0:T(8,128)(2,1)S(1)}, bf16[32,4096]{1,0:T(8,128)(2,1)S(1)}, u32[]{:S(2)}, u32[]{:S(2)}) collective-permute-start(bf16[32,4096]{1,0:T(8,128)(2,1)S(1)} %bitcast.129), channel_id=1, source_target_pairs={{0,1},{1,0},{2,3},{3,2},{4,5},{5,4},{6,7},{7,6},{8,9},{9,8},{10,11... | collective-permute-start | bytes 786440 | tf_op jit(solution)/shard_map/ppermute | solution.py:821
  23.8 147.5 %all-gather.10.cloned.1.call-start = ((), (), s32[]{:S(2)}) async-start(), calls=%async_computation.8 | async-start | bytes 1310720 | tf_op jit(solution)/shard_map/all_gather | solution.py:913
  24.4 33.5 %collective-permute-start.8 = (bf16[128,512]{1,0:T(8,128)(2,1)S(1)}, bf16[128,512]{1,0:T(8,128)(2,1)S(1)}, u32[]{:S(2)}, u32[]{:S(2)}) collective-permute-start(bf16[128,512]{1,0:T(8,128)(2,1)S(1)} %bitcast.130), channel_id=1, source_target_pairs={{0,1},{1,0},{2,3},{3,2},{4,5},{5,4},{6,7},{7,6},{8,9},{9,8},{10,11... | collective-permute-start | bytes 393224 | tf_op jit(solution)/shard_map/ppermute | solution.py:821
  24.8 9.8 %collective-permute-start.2 = (bf16[256,512]{1,0:T(8,128)(2,1)S(1)}, bf16[256,512]{1,0:T(8,128)(2,1)S(1)}, u32[]{:S(2)}, u32[]{:S(2)}) collective-permute-start(bf16[256,512]{1,0:T(8,128)(2,1)S(1)} %bitcast.111), channel_id=1, source_target_pairs={{0,8},{8,0},{16,24},{24,16},{1,9},{9,1},{17,25},{25,17},{2,10},{10... | collective-permute-start | bytes 786440 | tf_op jit(solution)/shard_map/ppermute | solution.py:821
  27.5 13.9 %collective-permute-start.3 = (bf16[256,512]{1,0:T(8,128)(2,1)S(1)}, bf16[256,512]{1,0:T(8,128)(2,1)S(1)}, u32[]{:S(2)}, u32[]{:S(2)}) collective-permute-start(bf16[256,512]{1,0:T(8,128)(2,1)S(1)} %bitcast.112), channel_id=1, source_target_pairs={{0,16},{8,24},{16,0},{24,8},{1,17},{9,25},{17,1},{25,9},{2,18},{10... | collective-permute-start | bytes 786440 | tf_op jit(solution)/shard_map/ppermute | solution.py:821
  29.0 12.4 %collective-permute-start.4 = (bf16[256,512]{1,0:T(8,128)(2,1)S(1)}, bf16[256,512]{1,0:T(8,128)(2,1)S(1)}, u32[]{:S(2)}, u32[]{:S(2)}) collective-permute-start(bf16[256,512]{1,0:T(8,128)(2,1)S(1)} %bitcast.113), channel_id=1, source_target_pairs={{0,24},{8,16},{16,8},{24,0},{1,25},{9,17},{17,9},{25,1},{2,26},{10... | collective-permute-start | bytes 786440 | tf_op jit(solution)/shard_map/ppermute | solution.py:821
  45.0 24.7 %collective-permute-start.6 = (bf16[256,2048]{1,0:T(8,128)(2,1)}, bf16[256,2048]{1,0:T(8,128)(2,1)S(1)}, u32[]{:S(2)}, u32[]{:S(2)}) collective-permute-start(bf16[256,2048]{1,0:T(8,128)(2,1)} %later.8.refs_2_.refs_6_.refs_5_.refs_1_), channel_id=1, source_target_pairs={{0,8},{8,0},{16,24},{24,16},{1,9},{9,1},{17,25},{25,17},{2,10},{10... | collective-permute-start | bytes 3145736 | tf_op jit(solution)/shard_map/ppermute | solution.py:821
  46.2 24.7 %collective-permute-start.7 = (bf16[256,2048]{1,0:T(8,128)(2,1)}, bf16[256,2048]{1,0:T(8,128)(2,1)S(1)}, u32[]{:S(2)}, u32[]{:S(2)}) collective-permute-start(bf16[256,2048]{1,0:T(8,128)(2,1)} %later.8.refs_2_.refs_6_.refs_5_.refs_1_), channel_id=1, source_target_pairs={{0,16},{8,24},{16,0},{24,8},{1,17},{9,25},{17,1},{25,9},{2,18},{10... | collective-permute-start | bytes 3145736 | tf_op jit(solution)/shard_map/ppermute | solution.py:821
  47.6 29.1 %collective-permute-start.11 = (bf16[256,2048]{1,0:T(8,128)(2,1)}, bf16[256,2048]{1,0:T(8,128)(2,1)}, u32[]{:S(2)}, u32[]{:S(2)}) collective-permute-start(bf16[256,2048]{1,0:T(8,128)(2,1)} %later.8.refs_2_.refs_6_.refs_5_.refs_1_), channel_id=1, source_target_pairs={{0,1},{1,0},{2,3},{3,2},{4,5},{5,4},{6,7},{7,6},{8,9},{9,8},{10,11... | collective-permute-start | bytes 3145736 | tf_op jit(solution)/shard_map/ppermute | solution.py:821
  60.4 36.3 %collective-permute-start.16 = (bf16[640,1024]{1,0:T(8,128)(2,1)}, bf16[640,1024]{1,0:T(8,128)(2,1)}, u32[]{:S(2)}, u32[]{:S(2)}) collective-permute-start(bf16[640,1024]{1,0:T(8,128)(2,1)} %get-tuple-element.68), channel_id=1, source_target_pairs={{0,1},{1,0},{2,3},{3,2},{4,5},{5,4},{6,7},{7,6},{8,9},{9,8},{10,11... | collective-permute-start | bytes 3932168 | tf_op jit(solution)/shard_map/ppermute | solution.py:821
  74.0 21.4 %collective-permute-start.9 = (bf16[256,1024]{1,0:T(8,128)(2,1)}, bf16[256,1024]{1,0:T(8,128)(2,1)S(1)}, u32[]{:S(2)}, u32[]{:S(2)}) collective-permute-start(bf16[256,1024]{1,0:T(8,128)(2,1)} %get-tuple-element.66), channel_id=1, source_target_pairs={{0,16},{8,24},{16,0},{24,8},{1,17},{9,25},{17,1},{25,9},{2,18},{10... | collective-permute-start | bytes 1572872 | tf_op jit(solution)/shard_map/ppermute | solution.py:821
  75.5 20.2 %collective-permute-start.10 = (bf16[256,1024]{1,0:T(8,128)(2,1)}, bf16[256,1024]{1,0:T(8,128)(2,1)}, u32[]{:S(2)}, u32[]{:S(2)}) collective-permute-start(bf16[256,1024]{1,0:T(8,128)(2,1)} %get-tuple-element.67), channel_id=1, source_target_pairs={{0,8},{8,0},{16,24},{24,16},{1,9},{9,1},{17,25},{25,17},{2,10},{10... | collective-permute-start | bytes 1572872 | tf_op jit(solution)/shard_map/ppermute | solution.py:821
  76.7 21.7 %collective-permute-start.12 = (bf16[256,2048]{1,0:T(8,128)(2,1)}, bf16[256,2048]{1,0:T(8,128)(2,1)S(1)}, u32[]{:S(2)}, u32[]{:S(2)}) collective-permute-start(bf16[256,2048]{1,0:T(8,128)(2,1)} %copy-done), channel_id=1, source_target_pairs={{0,1},{1,0},{2,3},{3,2},{4,5},{5,4},{6,7},{7,6},{8,9},{9,8},{10,11... | collective-permute-start | bytes 3145736 | tf_op jit(solution)/shard_map/ppermute | solution.py:821
  76.8 21.7 %collective-permute-start.13 = (bf16[256,2048]{1,0:T(8,128)(2,1)}, bf16[256,2048]{1,0:T(8,128)(2,1)}, u32[]{:S(2)}, u32[]{:S(2)}) collective-permute-start(bf16[256,2048]{1,0:T(8,128)(2,1)} %copy-done.1), channel_id=1, source_target_pairs={{0,1},{1,0},{2,3},{3,2},{4,5},{5,4},{6,7},{7,6},{8,9},{9,8},{10,11... | collective-permute-start | bytes 3145736 | tf_op jit(solution)/shard_map/ppermute | solution.py:821
  79.7 11.9 %all-to-all-start = ((bf16[32,2,272]{2,1,0:T(2,128)(2,1)}), bf16[32,2,272]{2,1,0:T(2,128)(2,1)S(1)}, u32[]{:S(2)}, u32[]{:S(2)}) async-start(bf16[32,2,272]{2,1,0:T(2,128)(2,1)} %reshape.292), calls=%async_computation | async-start | bytes 98304 | tf_op jit(solution)/shard_map/all_to_all | solution.py:1045
  83.7 128.2 %all-gather.12.cloned.1.call-start = ((), (), s32[]{:S(2)}) async-start(), calls=%async_computation.13 | async-start | bytes 5242880 | tf_op jit(solution)/shard_map/all_gather | solution.py:1078
  96.5 238.0 %reduce-scatter.5.cloned.1.call-start = ((), (), s32[]{:S(2)}) async-start(), calls=%async_computation.9 | async-start | bytes 10485760 | tf_op jit(solution)/shard_map/reduce_scatter | solution.py:1116
  96.8 49.1 %collective-permute-start.17 = (bf16[256,4096]{1,0:T(8,128)(2,1)}, bf16[256,4096]{1,0:T(8,128)(2,1)S(1)}, u32[]{:S(2)}, u32[]{:S(2)}) collective-permute-start(bf16[256,4096]{1,0:T(8,128)(2,1)} %all-gather.8.cloned.1.call-done.refs_16_.refs_4_.refs_6_), channel_id=1, source_target_pairs={{0,8},{8,0},{16,24},{24,16},{1,9},{9,1},{17,25},{25,17},{2,10},{10... | collective-permute-start | bytes 6291464 | tf_op jit(solution)/shard_map/ppermute | solution.py:821
  97.7 48.2 %collective-permute-start.18 = (bf16[256,4096]{1,0:T(8,128)(2,1)}, bf16[256,4096]{1,0:T(8,128)(2,1)S(1)}, u32[]{:S(2)}, u32[]{:S(2)}) collective-permute-start(bf16[256,4096]{1,0:T(8,128)(2,1)} %all-gather.8.cloned.1.call-done.refs_16_.refs_4_.refs_6_), channel_id=1, source_target_pairs={{0,16},{8,24},{16,0},{24,8},{1,17},{9,25},{17,1},{25,9},{2,18},{10... | collective-permute-start | bytes 6291464 | tf_op jit(solution)/shard_map/ppermute | solution.py:821
  112.8 40.0 %collective-permute-start.19 = (bf16[1024,1024]{1,0:T(8,128)(2,1)}, bf16[1024,1024]{1,0:T(8,128)(2,1)}, u32[]{:S(2)}, u32[]{:S(2)}) collective-permute-start(bf16[1024,1024]{1,0:T(8,128)(2,1)} %get-tuple-element.73.refs_1_), channel_id=1, source_target_pairs={{0,1},{1,0},{2,3},{3,2},{4,5},{5,4},{6,7},{7,6},{8,9},{9,8},{10,11... | collective-permute-start | bytes 6291464 | tf_op jit(solution)/shard_map/ppermute | solution.py:821
  150.6 25.5 %collective-permute-start.20 = (bf16[256,2048]{1,0:T(8,128)(2,1)}, bf16[256,2048]{1,0:T(8,128)(2,1)S(1)}, u32[]{:S(2)}, u32[]{:S(2)}) collective-permute-start(bf16[256,2048]{1,0:T(8,128)(2,1)} %get-tuple-element.71.refs_16_), channel_id=1, source_target_pairs={{0,16},{8,24},{16,0},{24,8},{1,17},{9,25},{17,1},{25,9},{2,18},{10... | collective-permute-start | bytes 3145736 | tf_op jit(solution)/shard_map/ppermute | solution.py:821
  151.7 25.5 %collective-permute-start.21 = (bf16[256,2048]{1,0:T(8,128)(2,1)}, bf16[256,2048]{1,0:T(8,128)(2,1)S(1)}, u32[]{:S(2)}, u32[]{:S(2)}) collective-permute-start(bf16[256,2048]{1,0:T(8,128)(2,1)} %get-tuple-element.72.refs_17_), channel_id=1, source_target_pairs={{0,8},{8,0},{16,24},{24,16},{1,9},{9,1},{17,25},{25,17},{2,10},{10... | collective-permute-start | bytes 3145736 | tf_op jit(solution)/shard_map/ppermute | solution.py:821
  178.1 3.4 collective-permute-start.22
  179.4 27.2 %collective-permute-start.23 = (bf16[1024,512]{1,0:T(8,128)(2,1)S(1)}, bf16[1024,512]{1,0:T(8,128)(2,1)S(1)}, u32[]{:S(2)}, u32[]{:S(2)}) collective-permute-start(bf16[1024,512]{1,0:T(8,128)(2,1)S(1)} %copy-done.2), channel_id=1, source_target_pairs={{0,8},{8,0},{16,24},{24,16},{1,9},{9,1},{17,25},{25,17},{2,10},{10... | collective-permute-start | bytes 3145736 | tf_op jit(solution)/shard_map/ppermute | solution.py:821
  180.5 26.1 %collective-permute-start.24 = (bf16[1024,512]{1,0:T(8,128)(2,1)S(1)}, bf16[1024,512]{1,0:T(8,128)(2,1)S(1)}, u32[]{:S(2)}, u32[]{:S(2)}) collective-permute-start(bf16[1024,512]{1,0:T(8,128)(2,1)S(1)} %copy-done.2), channel_id=1, source_target_pairs={{0,16},{8,24},{16,0},{24,8},{1,17},{9,25},{17,1},{25,9},{2,18},{10... | collective-permute-start | bytes 3145736 | tf_op jit(solution)/shard_map/ppermute | solution.py:821
  209.9 19.1 %collective-permute-start.25 = (bf16[1024,256]{1,0:T(8,128)(2,1)}, bf16[1024,256]{1,0:T(8,128)(2,1)S(1)}, u32[]{:S(2)}, u32[]{:S(2)}) collective-permute-start(bf16[1024,256]{1,0:T(8,128)(2,1)} %get-tuple-element.78.refs_3_), channel_id=1, source_target_pairs={{0,16},{8,24},{16,0},{24,8},{1,17},{9,25},{17,1},{25,9},{2,18},{10... | collective-permute-start | bytes 1572872 | tf_op jit(solution)/shard_map/ppermute | solution.py:821
  211.0 18.0 %collective-permute-start.26 = (bf16[1024,256]{1,0:T(8,128)(2,1)}, bf16[1024,256]{1,0:T(8,128)(2,1)S(1)}, u32[]{:S(2)}, u32[]{:S(2)}) collective-permute-start(bf16[1024,256]{1,0:T(8,128)(2,1)} %get-tuple-element.79.refs_4_), channel_id=1, source_target_pairs={{0,8},{8,0},{16,24},{24,16},{1,9},{9,1},{17,25},{25,17},{2,10},{10... | collective-permute-start | bytes 1572872 | tf_op jit(solution)/shard_map/ppermute | solution.py:821
  230.0 154.7 %reduce-scatter.7.cloned.1.call-start = ((), (), s32[]{:S(2)}) async-start(), calls=%async_computation.10 | async-start | bytes 2621440 | tf_op jit(solution)/shard_map/reduce_scatter | solution.py:917
  280.7 4.3 collective-permute-start.27
  280.8 39.7 %collective-permute-start.30 = (bf16[1024,1024]{1,0:T(8,128)(2,1)S(1)}, bf16[1024,1024]{1,0:T(8,128)(2,1)}, u32[]{:S(2)}, u32[]{:S(2)}) collective-permute-start(bf16[1024,1024]{1,0:T(8,128)(2,1)S(1)} %copy-done.5), channel_id=1, source_target_pairs={{0,1},{1,0},{2,3},{3,2},{4,5},{5,4},{6,7},{7,6},{8,9},{9,8},{10,11... | collective-permute-start | bytes 6291464 | tf_op jit(solution)/shard_map/ppermute | solution.py:821
  281.3 46.6 %collective-permute-start.28 = (bf16[256,2048]{1,0:T(8,128)(2,1)}, bf16[256,2048]{1,0:T(8,128)(2,1)S(1)}, u32[]{:S(2)}, u32[]{:S(2)}) collective-permute-start(bf16[256,2048]{1,0:T(8,128)(2,1)} %get-tuple-element.86), channel_id=1, source_target_pairs={{0,8},{8,0},{16,24},{24,16},{1,9},{9,1},{17,25},{25,17},{2,10},{10... | collective-permute-start | bytes 3145736 | tf_op jit(solution)/shard_map/ppermute | solution.py:821
  282.0 45.9 %collective-permute-start.29 = (bf16[256,2048]{1,0:T(8,128)(2,1)}, bf16[256,2048]{1,0:T(8,128)(2,1)S(1)}, u32[]{:S(2)}, u32[]{:S(2)}) collective-permute-start(bf16[256,2048]{1,0:T(8,128)(2,1)} %get-tuple-element.87), channel_id=1, source_target_pairs={{0,16},{8,24},{16,0},{24,8},{1,17},{9,25},{17,1},{25,9},{2,18},{10... | collective-permute-start | bytes 3145736 | tf_op jit(solution)/shard_map/ppermute | solution.py:821
  300.9 19.6 %collective-permute-start.31 = (bf16[1024,512]{1,0:T(8,128)(2,1)}, bf16[1024,512]{1,0:T(8,128)(2,1)S(1)}, u32[]{:S(2)}, u32[]{:S(2)}) collective-permute-start(bf16[1024,512]{1,0:T(8,128)(2,1)} %get-tuple-element.89), channel_id=1, source_target_pairs={{0,1},{1,0},{2,3},{3,2},{4,5},{5,4},{6,7},{7,6},{8,9},{9,8},{10,11... | collective-permute-start | bytes 3145736 | tf_op jit(solution)/shard_map/ppermute | solution.py:821
  320.0 34.4 %collective-permute-start.32 = (bf16[3,1024,512]{2,1,0:T(8,128)(2,1)}, bf16[3,1024,512]{2,1,0:T(8,128)(2,1)}, u32[]{:S(2)}, u32[]{:S(2)}) collective-permute-start(bf16[3,1024,512]{2,1,0:T(8,128)(2,1)} %attention_backward.2.refs_5_.refs_1_), channel_id=1, source_target_pairs={{0,1},{1,0},{2,3},{3,2},{4,5},{5,4},{6,7},{7,6},{8,9},{9,8},{10,11... | collective-permute-start | bytes 9437192 | tf_op jit(solution)/shard_map/ppermute | solution.py:821
  334.6 108.0 %reduce-scatter.11.cloned.1.call-start = ((), (), s32[]{:S(2)}) async-start(), calls=%async_computation.12 | async-start | bytes 2621440 | tf_op jit(solution)/shard_map/reduce_scatter | solution.py:917
  334.6 50.0 %collective-permute-start.35 = (bf16[256,4096]{1,0:T(8,128)(2,1)}, bf16[256,4096]{1,0:T(8,128)(2,1)}, u32[]{:S(2)}, u32[]{:S(2)}) collective-permute-start(bf16[256,4096]{1,0:T(8,128)(2,1)} %get-tuple-element.91.refs_8_.refs_1_), channel_id=1, source_target_pairs={{0,8},{8,0},{16,24},{24,16},{1,9},{9,1},{17,25},{25,17},{2,10},{10... | collective-permute-start | bytes 6291464 | tf_op jit(solution)/shard_map/ppermute | solution.py:821
  334.7 49.9 %collective-permute-start.36 = (bf16[256,4096]{1,0:T(8,128)(2,1)}, bf16[256,4096]{1,0:T(8,128)(2,1)}, u32[]{:S(2)}, u32[]{:S(2)}) collective-permute-start(bf16[256,4096]{1,0:T(8,128)(2,1)} %get-tuple-element.92.refs_9_.refs_2_), channel_id=1, source_target_pairs={{0,16},{8,24},{16,0},{24,8},{1,17},{9,25},{17,1},{25,9},{2,18},{10... | collective-permute-start | bytes 6291464 | tf_op jit(solution)/shard_map/ppermute | solution.py:821
  367.0 26.7 %collective-permute-start.33 = (bf16[256,1024]{1,0:T(8,128)(2,1)}, bf16[256,1024]{1,0:T(8,128)(2,1)S(1)}, u32[]{:S(2)}, u32[]{:S(2)}) collective-permute-start(bf16[256,1024]{1,0:T(8,128)(2,1)} %get-tuple-element.96.refs_7_), channel_id=1, source_target_pairs={{0,8},{8,0},{16,24},{24,16},{1,9},{9,1},{17,25},{25,17},{2,10},{10... | collective-permute-start | bytes 1572872 | tf_op jit(solution)/shard_map/ppermute | solution.py:821
  367.9 25.8 %collective-permute-start.34 = (bf16[256,1024]{1,0:T(8,128)(2,1)}, bf16[256,1024]{1,0:T(8,128)(2,1)S(1)}, u32[]{:S(2)}, u32[]{:S(2)}) collective-permute-start(bf16[256,1024]{1,0:T(8,128)(2,1)} %get-tuple-element.97), channel_id=1, source_target_pairs={{0,16},{8,24},{16,0},{24,8},{1,17},{9,25},{17,1},{25,9},{2,18},{10... | collective-permute-start | bytes 1572872 | tf_op jit(solution)/shard_map/ppermute | solution.py:821
  395.3 69.9 %reduce-scatter.9.cloned.1.call-start = ((), (), s32[]{:S(2)}) async-start(), calls=%async_computation.11 | async-start | bytes 1310720 | tf_op jit(solution)/shard_map/reduce_scatter | solution.py:917
  396.3 5.7 %collective-permute-start.37 = (bf16[128,1024]{1,0:T(8,128)(2,1)S(1)}, bf16[128,1024]{1,0:T(8,128)(2,1)S(1)}, u32[]{:S(2)}, u32[]{:S(2)}) collective-permute-start(bf16[128,1024]{1,0:T(8,128)(2,1)S(1)} %dynamic-slice_bitcast_fusion.1), channel_id=1, source_target_pairs={{0,1},{1,0},{2,3},{3,2},{4,5},{5,4},{6,7},{7,6},{8,9},{9,8},{10,11... | collective-permute-start | bytes 786440 | tf_op jit(solution)/shard_map/ppermute | solution.py:821
  400.8 25.7 %collective-permute-start.39 = (bf16[256,2048]{1,0:T(8,128)(2,1)}, bf16[256,2048]{1,0:T(8,128)(2,1)S(1)}, u32[]{:S(2)}, u32[]{:S(2)}) collective-permute-start(bf16[256,2048]{1,0:T(8,128)(2,1)} %get-tuple-element.101.refs_8_), channel_id=1, source_target_pairs={{0,8},{8,0},{16,24},{24,16},{1,9},{9,1},{17,25},{25,17},{2,10},{10... | collective-permute-start | bytes 3145736 | tf_op jit(solution)/shard_map/ppermute | solution.py:821
  401.8 25.4 %collective-permute-start.40 = (bf16[256,2048]{1,0:T(8,128)(2,1)}, bf16[256,2048]{1,0:T(8,128)(2,1)S(1)}, u32[]{:S(2)}, u32[]{:S(2)}) collective-permute-start(bf16[256,2048]{1,0:T(8,128)(2,1)} %get-tuple-element.102.refs_9_), channel_id=1, source_target_pairs={{0,16},{8,24},{16,0},{24,8},{1,17},{9,25},{17,1},{25,9},{2,18},{10... | collective-permute-start | bytes 3145736 | tf_op jit(solution)/shard_map/ppermute | solution.py:821
  432.3 19.2 %collective-permute-start.38 = (bf16[640,1024]{1,0:T(8,128)(2,1)S(1)}, bf16[640,1024]{1,0:T(8,128)(2,1)S(1)}, u32[]{:S(2)}, u32[]{:S(2)}) collective-permute-start(bf16[640,1024]{1,0:T(8,128)(2,1)S(1)} %copy-done.55), channel_id=1, source_target_pairs={{0,1},{1,0},{2,3},{3,2},{4,5},{5,4},{6,7},{7,6},{8,9},{9,8},{10,11... | collective-permute-start | bytes 3932168 | tf_op jit(solution)/shard_map/ppermute | solution.py:821
  439.9 10.2 %all-to-all-start.1 = ((f32[32,1,384]{2,1,0:T(1,128)}), f32[32,1,384]{2,1,0:T(1,128)S(1)}, u32[]{:S(2)}, u32[]{:S(2)}) async-start(f32[32,1,384]{2,1,0:T(1,128)} %copy.150), calls=%async_computation.3 | async-start | bytes 98304 | tf_op jit(solution)/shard_map/all_to_all | solution.py:1176
  443.5 17.0 %collective-permute-start.41 = (bf16[32,4096]{1,0:T(8,128)(2,1)S(1)}, bf16[32,4096]{1,0:T(8,128)(2,1)S(1)}, u32[]{:S(2)}, u32[]{:S(2)}) collective-permute-start(bf16[32,4096]{1,0:T(8,128)(2,1)S(1)} %dynamic-slice_bitcast_fusion), channel_id=1, source_target_pairs={{0,1},{1,0},{2,3},{3,2},{4,5},{5,4},{6,7},{7,6},{8,9},{9,8},{10,11... | collective-permute-start | bytes 786440 | tf_op jit(solution)/shard_map/ppermute | solution.py:821
  (64 other events, 480.7 us)
Sparse Core Ops, SparseCore 0:
  14.1 30.5 all-gather.5
  46.8 46.4 all-gather.7
  95.5 26.6 all-gather.9
  124.2 80.2 all-gather.11
  230.1 100.8 reduce-scatter.4
  334.7 40.1 reduce-scatter.6
  395.4 40.5 reduce-scatter.10
  438.4 26.7 reduce-scatter.8

commit v5 on v4

--- a/solution.py
+++ b/solution.py
@@ -18,6 +18,7 @@
 f32 = jnp.float32
 ALL = ("dp", "z", "c")
 BLOCK = 256
+WIDE = 512
 FBLOCK = 512
 NN = (((1,), (0,)), ((), ()))
 NT = (((1,), (1,)), ((), ()))
@@ -284,7 +285,7 @@
 
 def send_slots(acc, slot, values, keep_ref, away_ref):
     step = pl.program_id(0)
-    chosen = lax.broadcasted_iota(jnp.int32, (2 * CAPACITY, BLOCK), 0) == slot[...]
+    chosen = lax.broadcasted_iota(jnp.int32, (2 * CAPACITY, values.shape[0]), 0) == slot[...]
     part = dot(chosen.astype(bf16), values)
 
     @pl.when(step == 0)
@@ -310,9 +311,9 @@
     return launch(
         dispatch_kernel,
         "dispatch",
-        (rows // BLOCK,),
+        (rows // WIDE,),
         (slot_row, values),
-        [pl.BlockSpec((1, BLOCK), lambda i: (0, i)), pl.BlockSpec((BLOCK, width), lambda i: (i, 0))],
+        [pl.BlockSpec((1, WIDE), lambda i: (0, i)), pl.BlockSpec((WIDE, width), lambda i: (i, 0))],
         (whole(CAPACITY, width),) * 2,
         (shape_of((CAPACITY, width), bf16),) * 2,
         [pltpu.VMEM((2 * CAPACITY, width), f32)],
@@ -341,17 +342,17 @@
 
 def middle_part(core, me, slot_row, x, attended, mine_w, other_w, bias, gain, shift, after=()):
     rows, width = x.shape
-    block = pl.BlockSpec((BLOCK, width), lambda i, c, m: (i, 0))
+    block = pl.BlockSpec((WIDE, width), lambda i, c, m: (i, 0))
     half, depth = width // 2, mine_w[0].shape[0]
     out_columns = [pl.BlockSpec((depth, half), lambda *_: (0, 3))] * 3 + [pl.BlockSpec((depth, half), lambda *_: (0, 1))]
     of = lambda w: (w[0], w[1], w[2], w[4])
     return launch(
         middle_kernel,
         "middle",
-        (rows // BLOCK,),
+        (rows // WIDE,),
         (slot_row, x, attended, *of(mine_w), *of(other_w), bias, gain, shift),
         [
-            pl.BlockSpec((1, BLOCK), lambda i, c, m: (0, i)),
+            pl.BlockSpec((1, WIDE), lambda i, c, m: (0, i)),
             block,
             block,
             *out_columns,
@@ -370,7 +371,7 @@
 
 
 def from_slots(slot, keep_ref, away_ref):
-    chosen = lax.broadcasted_iota(jnp.int32, (BLOCK, 2 * CAPACITY), 1) == slot[...]
+    chosen = lax.broadcasted_iota(jnp.int32, (slot.shape[0], 2 * CAPACITY), 1) == slot[...]
     chosen = chosen.astype(bf16)
     return dot(chosen[:, :CAPACITY], keep_ref[...]) + dot(chosen[:, CAPACITY:], away_ref[...])
 
@@ -427,12 +428,12 @@
 
 def output(slot_col, route_col, keep, away, middle, bias, after=()):
     rows, width = middle.shape
-    block = pl.BlockSpec((BLOCK, width), lambda i: (i, 0))
-    column = pl.BlockSpec((BLOCK, 1), lambda i: (i, 0))
+    block = pl.BlockSpec((WIDE, width), lambda i: (i, 0))
+    column = pl.BlockSpec((WIDE, 1), lambda i: (i, 0))
     return launch(
         output_kernel,
         "output",
-        (rows // BLOCK,),
+        (rows // WIDE,),
         (slot_col, route_col, keep, away, middle, bias),
         [column, column, whole(CAPACITY, width), whole(CAPACITY, width), block, whole(2, width)],
         block,

time: 487 us -> 486 us (level)
  transfers between devices with their start and end apart: 53 -> 53, of which waited for: 17 -> 18; matrix products, arithmetic and copies ran while one was open for 6% -> 6% of each run, Pallas kernels for 68% -> 67%
where the time goes in v5:
time: 486 us; the launch traced here: 477 us
  Pallas kernels  324 us (67%)
  waiting for transfers between devices  46.2 us (10%)
  local copies, waits for them, and re-layouts  45.9 us (9%)
  starting transfers between devices  36.7 us (8%)
  between operations  15.2 us (3%)
  other arithmetic  9.3 us (2%)
    pallas_call x30, Pallas kernels, launch(): pl.pallas_call(body, grid_spec=pltpu.PrefetchScalarGridSpec(num_scalar_pr...  305 us
    ppermute x43, waiting for transfers between devices, swap(): return lax.ppermute(value, axis, [(i, i ^ mask) for i in range(size)])  33.4 us
    ppermute x43, starting transfers between devices, swap(): return lax.ppermute(value, axis, [(i, i ^ mask) for i in range(size)])  29.6 us
    unnamed x130, local copies, waits for them, and re-layouts  26.6 us
    pallas_call x2, Pallas kernels, two_sum(): pl.pallas_call(body, grid_spec=pltpu.PrefetchScalarGridSpec(num_scalar_pr...  19 us
  transfers between devices with their start and end apart: 53, of which 18 were waited for; matrix products, arithmetic and copies ran while one was open for 6% of the time, Pallas kernels for 67%

profile of v5, /device:TPU:0, one launch (start us, length us, event | category | flops | bytes accessed | tf_op | source)
XLA Modules:
  0.0 476.8 jit_solution(3173061248572086929)
XLA Ops:
  8.5 1.6 dynamic-slice_reduce_fusion
  12.3 1.7 place.7
  19.5 1.7 place.8
  21.9 1.8 place.9
  24.8 2.7 collective-permute-start.2
  27.5 1.5 collective-permute-start.3
  30.1 4.5 collective-permute-done.2.refs_2_
  34.6 6.8 %collective-permute-done.3.refs_3_ = bf16[256,512]{1,0:T(8,128)(2,1)S(1)} collective-permute-done((bf16[256,512]{1,0:T(8,128)(2,1)S(1)}, bf16[256,512]{1,0:T(8,128)(2,1)S(1)}, u32[]{:S(2)}, u32[]{:S(2)}) %collective-permute-start.3) | collective-permute-done | bytes 262176 | tf_op jit(solution)/shard_map/ppermute | solution.py:822
  42.2 2.7 place.10
  49.8 6.9 %dispatch.1 = (bf16[640,1024]{1,0:T(8,128)(2,1)}, bf16[640,1024]{1,0:T(8,128)(2,1)}) custom-call(s32[1,1024]{1,0:T(1,128)} %add.50.refs_0_.refs_2_, bf16[1024,1024]{1,0:T(8,128)(2,1)} %refs_5_.1, bf16[256,2048]{1,0:T(8,128)(2,1)} %later.8.refs_2_.refs_6_.refs_5_.refs_1_), custom_call_target="tpu_custom_call" | custom-call | flops 5368709120 | bytes 4718592 | tf_op jit(solution)/shard_map/dispatch/pallas_call | solution.py:45
  57.4 1.8 place.11
  59.8 9.9 %collective-permute-done.6.refs_0_.refs_7_.refs_6_.refs_2_ = bf16[256,2048]{1,0:T(8,128)(2,1)S(1)} collective-permute-done((bf16[256,2048]{1,0:T(8,128)(2,1)}, bf16[256,2048]{1,0:T(8,128)(2,1)S(1)}, u32[]{:S(2)}, u32[]{:S(2)}) %collective-permute-start.6) | collective-permute-done | bytes 1048608 | tf_op jit(solution)/shard_map/ppermute | solution.py:822
  71.9 2.1 cut_halves.3
  74.0 1.5 collective-permute-start.9
  79.7 4.0 all-to-all-start
  85.0 6.6 %all-to-all-done = bf16[32,2,272]{2,1,0:T(2,128)(2,1)S(1)} async-done(((bf16[32,2,272]{2,1,0:T(2,128)(2,1)}), bf16[32,2,272]{2,1,0:T(2,128)(2,1)S(1)}, u32[]{:S(2)}, u32[]{:S(2)}) %all-to-all-start) | async-done | bytes 34848 | tf_op jit(solution)/shard_map/all_to_all | solution.py:1046
  99.4 13.3 %project.1 = (bf16[1024,1024]{1,0:T(8,128)(2,1)}, bf16[1024,3072]{1,0:T(8,128)(2,1)}) custom-call(s32[1]{0:T(128)} %bitcast.3.refs_0_, s32[1]{0:T(128)} %bitcast.2.refs_0_.refs_1_, bf16[1024,1024]{1,0:T(8,128)(2,1)} %refs_2_.7, f32[1,1024]{1,0:T(1,128)} %reshape.209.refs_3_.refs_6_, f32[1,1024]{1,0:T(1,128)} %reshape.210.refs_4_, ...), custom_call_target="tpu_custom_call" | custom-call | flops 12884901888 | bytes 16777216 | tf_op jit(solution)/shard_map/project/pallas_call | solution.py:45
  113.1 32.8 %attention_forward.1 = (bf16[1024,1024]{1,0:T(8,128)(2,1)}, f32[8,2,1024]{2,1,0:T(2,128)}) custom-call(s32[1024,1]{1,0:T(8,128)} %copy.136.refs_0_.refs_1_, s32[1,1024]{1,0:T(1,128)} %refs_2_.6, bf16[1024,3072]{1,0:T(8,128)(2,1)} %get-tuple-element.69.refs_2_.refs_3_.refs_4_.refs_5_, bf16[1024,3072]{1,0:T(8,128)(2,1)} %get-tuple-element.69.refs_2_.refs_3_.refs_4_.refs_5_, ...), custom_call_target="tpu_custom_call" | custom-call | flops 34359738368 | bytes 8388608 | tf_op jit(solution)/shard_map/attention_forward/pallas_call | solution.py:45
  147.9 2.7 cut_halves.4
  152.6 12.5 %middle.1 = (f32[1024,1024]{1,0:T(8,128)}, bf16[640,1024]{1,0:T(8,128)(2,1)}, bf16[640,1024]{1,0:T(8,128)(2,1)}) custom-call(s32[1]{0:T(128)} %bitcast.3.refs_0_, s32[1]{0:T(128)} %bitcast.2.refs_0_.refs_1_, s32[1,1024]{1,0:T(1,128)} %add.50.refs_0_.refs_2_, bf16[1024,1024]{1,0:T(8,128)(2,1)} %refs_2_.7, ...), custom_call_target="tpu_custom_call" | custom-call | flops 9663676416 | bytes 13107200 | tf_op jit(solution)/shard_map/middle/pallas_call | solution.py:45
  165.1 4.7 place.12
  169.8 4.6 place.13
  174.4 1.7 collective-permute-done.20.refs_1_.refs_7_.refs_9_
  181.3 25.3 %experts_up.1 = (bf16[1280,4096]{1,0:T(8,128)(2,1)}, bf16[1280,4096]{1,0:T(8,128)(2,1)}) custom-call(s32[1]{0:T(128)} %bitcast.2.refs_0_.refs_1_, bf16[640,1024]{1,0:T(8,128)(2,1)} %get-tuple-element.74.refs_1_.refs_3_, bf16[640,1024]{1,0:T(8,128)(2,1)} %collective-permute-done.22.refs_2_.refs_4_, f32[1,4096]{1,0:T(1,128)} %dynamic-slice_bitcast_fusion.3.refs_3_, ...), custom_call_target="tpu_custom_call" | custom-call | flops 21474836480 | bytes 29360128 | tf_op jit(solution)/shard_map/experts_up/pallas_call | solution.py:45
  207.9 2.0 cut_halves.5
  212.0 16.8 %experts_outer.1 = (bf16[4096,1024]{1,0:T(8,128)(2,1)}, f32[1,1024]{1,0:T(1,128)}) custom-call(bf16[1280,4096]{1,0:T(8,128)(2,1)} %get-tuple-element.77.refs_2_.refs_0_.refs_1_, bf16[640,1024]{1,0:T(8,128)(2,1)} %get-tuple-element.65.refs_3_.refs_1_, bf16[640,1024]{1,0:T(8,128)(2,1)} %collective-permute-done.16.refs_17_.refs_2_, ...), custom_call_target="tpu_custom_call" | custom-call | flops 21474836480 | bytes 18874368 | tf_op jit(solution)/shard_map/experts_outer/pallas_call | solution.py:45
  229.8 50.6 %experts_grad.1 = (bf16[640,1024]{1,0:T(8,128)(2,1)}, bf16[640,1024]{1,0:T(8,128)(2,1)}, bf16[1024,4096]{1,0:T(8,128)(2,1)}, bf16[256,2048]{1,0:T(8,128)(2,1)}, ...) custom-call(s32[1]{0:T(128)} %bitcast.2.refs_0_.refs_1_, bf16[640,1024]{1,0:T(8,128)(2,1)} %get-tuple-element.65.refs_3_.refs_1_, ...), custom_call_target="tpu_custom_call" | custom-call | flops 64424509440 | bytes 35651584 | tf_op jit(solution)/shard_map/experts_grad/pallas_call | solution.py:45
  282.8 1.9 collective-permute-done.27.refs_3_
  285.9 14.8 %middle_grad.1 = (f32[1024,1024]{1,0:T(8,128)}, bf16[1024,512]{1,0:T(8,128)(2,1)}, bf16[1024,512]{1,0:T(8,128)(2,1)}, bf16[1024,1024]{1,0:T(8,128)(2,1)}, f32[1,...) custom-call(s32[1]{0:T(128)} %bitcast.3.refs_0_, s32[1024,1]{1,0:T(8,128)} %get-tuple-element.126.refs_1_.refs_0_, ...), custom_call_target="tpu_custom_call" | custom-call | flops 9663676416 | bytes 19398656 | tf_op jit(solution)/shard_map/middle_grad/pallas_call | solution.py:45
  300.9 18.8 %attention_backward.2.refs_5_.refs_1_ = bf16[3,1024,512]{2,1,0:T(8,128)(2,1)} custom-call(s32[1]{0:T(128)} %bitcast.26.refs_0_, s32[1024,1]{1,0:T(8,128)} %copy.136.refs_0_.refs_1_, s32[1,1024]{1,0:T(1,128)} %refs_2_.6, bf16[1024,3072]{1,0:T(8,128)(2,1)} %get-tuple-element.69.refs_2_.refs_3_.refs_4_.refs_5_, ...), custom_call_target="tpu_custom_call" | custom-call | flops 25769803776 | bytes 8388608 | tf_op jit(solution)/shard_map/attention_backward/pallas_call | solution.py:45
  321.2 6.4 %two_sum.2 = (bf16[1024,2048]{1,0:T(8,128)(2,1)}, bf16[256,1024]{1,0:T(8,128)(2,1)}, bf16[256,1024]{1,0:T(8,128)(2,1)}) custom-call(s32[1]{0:T(128)} %bitcast.2.refs_0_.refs_1_, bf16[1024,1024]{1,0:T(8,128)(2,1)} %get-tuple-element.70.refs_2_.refs_4_.refs_1_, bf16[1,1024,512]{2,1,0:T(8,128)(2,1)} %bitcast.154, ...), custom_call_target="tpu_custom_call" | custom-call | flops 4294967296 | bytes 6291456 | tf_op jit(solution)/shard_map/two_sum/pallas_call | solution.py:517
  328.9 5.3 %far_add.2 = (bf16[256,4096]{1,0:T(8,128)(2,1)}, bf16[256,4096]{1,0:T(8,128)(2,1)}) custom-call(s32[1]{0:T(128)} %bitcast.2.refs_0_.refs_1_, bf16[4,256,4096]{2,1,0:T(8,128)(2,1)} %bitcast.87, bf16[4,256,4096]{2,1,0:T(8,128)(2,1)} %bitcast.88, bf16[256,2048]{1,0:T(8,128)(2,1)} %copy-done.17, bf16[256,2048]{1,0:T(8,128)(2,1)} %copy-done.18, ...), custom_call_target="tpu_custom_call" | custom-call | tf_op jit(solution)/shard_map/far_add/pallas_call | solution.py:45
  335.4 18.8 %attention_backward.3.refs_2_.refs_0_ = bf16[3,1024,512]{2,1,0:T(8,128)(2,1)} custom-call(s32[1]{0:T(128)} %bitcast.22.refs_0_, s32[1024,1]{1,0:T(8,128)} %copy.136.refs_0_.refs_1_, s32[1,1024]{1,0:T(1,128)} %refs_2_.6, bf16[1024,3072]{1,0:T(8,128)(2,1)} %get-tuple-element.69.refs_2_.refs_3_.refs_4_.refs_5_, ...), custom_call_target="tpu_custom_call" | custom-call | flops 25769803776 | bytes 8388608 | tf_op jit(solution)/shard_map/attention_backward/pallas_call | solution.py:45
  354.2 12.6 %two_sum.3 = (bf16[1024,2048]{1,0:T(8,128)(2,1)}, bf16[256,1024]{1,0:T(8,128)(2,1)}, bf16[256,1024]{1,0:T(8,128)(2,1)}) custom-call(s32[1]{0:T(128)} %bitcast.2.refs_0_.refs_1_, bf16[1024,1024]{1,0:T(8,128)(2,1)} %get-tuple-element.73.refs_1_, ...), custom_call_target="tpu_custom_call", output_to_operand_aliasing={{0}: (5, {}), {1}: (6, {}), {2}: (7, {})} | custom-call | flops 12884901888 | bytes 10485760 | tf_op jit(solution)/shard_map/two_sum/pallas_call | solution.py:517
  367.7 1.8 collective-permute-start.34
  369.6 14.6 %input_grad.1 = (f32[1024,1024]{1,0:T(8,128)}, f32[1,1024]{1,0:T(1,128)}, f32[1,1024]{1,0:T(1,128)}, f32[4,512]{1,0:T(4,128)}) custom-call(bf16[3,1024,512]{2,1,0:T(8,128)(2,1)} %attention_backward.3.refs_2_.refs_0_, bf16[3,1024,512]{2,1,0:T(8,128)(2,1)} %attention_backward.2.refs_5_.refs_1_, bf16[1024,1024]{1,0:T(8,128)(2,1)} %refs_2_.7, ...), custom_call_target="tpu_custom_call" | custom-call | bytes 2097152 | tf_op jit(solution)/shard_map/input_grad/pallas_call | solution.py:45
  384.2 4.9 %near_add.2.refs_0_ = bf16[256,4096]{1,0:T(8,128)(2,1)} custom-call(s32[1]{0:T(128)} %bitcast.2.refs_0_.refs_1_, bf16[4,256,4096]{2,1,0:T(8,128)(2,1)} %bitcast.89, bf16[256,4096]{1,0:T(8,128)(2,1)} %collective-permute-done.35.refs_2_, bf16[256,4096]{1,0:T(8,128)(2,1)} %collective-permute-done.36.refs_3_, f32[1024,1024]{1,0:T(8,128)} %get-tuple-element.51.refs_4_, ...), custom_call_target="tpu_custom_call" | custom-call | tf_op jit(solution)/shard_map/near_add/pallas_call | solution.py:45
  389.1 4.3 collective-permute-done.33.refs_1_.refs_3_
  396.1 4.4 far_add.3
  402.4 2.3 pair.2.refs_10_.refs_2_
  404.7 21.4 %experts_down.1 = (bf16[640,1024]{1,0:T(8,128)(2,1)}, bf16[640,1024]{1,0:T(8,128)(2,1)}) custom-call(s32[1]{0:T(128)} %bitcast.2.refs_0_.refs_1_, bf16[1280,4096]{1,0:T(8,128)(2,1)} %get-tuple-element.77.refs_2_.refs_0_.refs_1_, bf16[1024,512]{1,0:T(8,128)(2,1)} %later.9.refs_3_.refs_11_.refs_2_, bf16[1024,512]{1,0:T(8,128)(2,1)} %copy-done.12, ...), custom_call_target="tpu_custom_call" | custom-call | flops 21474836480 | bytes 18874368 | tf_op jit(solution)/shard_map/experts_down/pallas_call | solution.py:45
  428.0 4.0 near_add.3.refs_6_.refs_1_
  439.6 2.6 all-to-all-start.1
  446.2 3.7 all-to-all-done.1
  452.3 7.4 %output.1.refs_4_ = bf16[1024,1024]{1,0:T(8,128)(2,1)} custom-call(s32[1024,1]{1,0:T(8,128)} %get-tuple-element.126.refs_1_.refs_0_, s32[1024,1]{1,0:T(8,128)} %copy.141.refs_1_, bf16[640,1024]{1,0:T(8,128)(2,1)} %get-tuple-element.103.refs_4_.refs_2_, bf16[640,1024]{1,0:T(8,128)(2,1)} %copy-done.11, f32[1024,1024]{1,0:T(8,128)} %get-tuple-element.76.refs_1_.refs_6_.refs_4_, ...), custom_call_target="tpu_custom_call" | custom-call | bytes 2097152 | tf_op jit(solution)/shard_map/output/pallas_call | solution.py:45
  460.3 2.3 pair.3.refs_3_
  462.6 2.3 reduce-scatter.9.cloned.1.call-done.refs_0_
  467.9 1.8 finish.1
  (304 shorter events, 80.6 us)
Async XLA Ops:
  7.2 37.8 %all-gather.6.cloned.1.call-start = ((), (), s32[]{:S(2)}) async-start(), calls=%async_computation.6 | async-start | bytes 1310720 | tf_op jit(solution)/shard_map/all_gather | solution.py:914
  14.0 82.6 %all-gather.8.cloned.1.call-start = ((), (), s32[]{:S(2)}) async-start(), calls=%async_computation.7 | async-start | bytes 2621440 | tf_op jit(solution)/shard_map/all_gather | solution.py:914
  15.6 5.6 %collective-permute-start.5 = (bf16[32,4096]{1,0:T(8,128)(2,1)S(1)}, bf16[32,4096]{1,0:T(8,128)(2,1)S(1)}, u32[]{:S(2)}, u32[]{:S(2)}) collective-permute-start(bf16[32,4096]{1,0:T(8,128)(2,1)S(1)} %bitcast.129), channel_id=1, source_target_pairs={{0,1},{1,0},{2,3},{3,2},{4,5},{5,4},{6,7},{7,6},{8,9},{9,8},{10,11... | collective-permute-start | bytes 786440 | tf_op jit(solution)/shard_map/ppermute | solution.py:822
  23.8 146.0 %all-gather.10.cloned.1.call-start = ((), (), s32[]{:S(2)}) async-start(), calls=%async_computation.8 | async-start | bytes 1310720 | tf_op jit(solution)/shard_map/all_gather | solution.py:914
  24.4 32.3 %collective-permute-start.8 = (bf16[128,512]{1,0:T(8,128)(2,1)S(1)}, bf16[128,512]{1,0:T(8,128)(2,1)S(1)}, u32[]{:S(2)}, u32[]{:S(2)}) collective-permute-start(bf16[128,512]{1,0:T(8,128)(2,1)S(1)} %bitcast.130), channel_id=1, source_target_pairs={{0,1},{1,0},{2,3},{3,2},{4,5},{5,4},{6,7},{7,6},{8,9},{9,8},{10,11... | collective-permute-start | bytes 393224 | tf_op jit(solution)/shard_map/ppermute | solution.py:822
  24.8 9.8 %collective-permute-start.2 = (bf16[256,512]{1,0:T(8,128)(2,1)S(1)}, bf16[256,512]{1,0:T(8,128)(2,1)S(1)}, u32[]{:S(2)}, u32[]{:S(2)}) collective-permute-start(bf16[256,512]{1,0:T(8,128)(2,1)S(1)} %bitcast.111), channel_id=1, source_target_pairs={{0,8},{8,0},{16,24},{24,16},{1,9},{9,1},{17,25},{25,17},{2,10},{10... | collective-permute-start | bytes 786440 | tf_op jit(solution)/shard_map/ppermute | solution.py:822
  27.5 13.9 %collective-permute-start.3 = (bf16[256,512]{1,0:T(8,128)(2,1)S(1)}, bf16[256,512]{1,0:T(8,128)(2,1)S(1)}, u32[]{:S(2)}, u32[]{:S(2)}) collective-permute-start(bf16[256,512]{1,0:T(8,128)(2,1)S(1)} %bitcast.112), channel_id=1, source_target_pairs={{0,16},{8,24},{16,0},{24,8},{1,17},{9,25},{17,1},{25,9},{2,18},{10... | collective-permute-start | bytes 786440 | tf_op jit(solution)/shard_map/ppermute | solution.py:822
  29.0 12.4 %collective-permute-start.4 = (bf16[256,512]{1,0:T(8,128)(2,1)S(1)}, bf16[256,512]{1,0:T(8,128)(2,1)S(1)}, u32[]{:S(2)}, u32[]{:S(2)}) collective-permute-start(bf16[256,512]{1,0:T(8,128)(2,1)S(1)} %bitcast.113), channel_id=1, source_target_pairs={{0,24},{8,16},{16,8},{24,0},{1,25},{9,17},{17,9},{25,1},{2,26},{10... | collective-permute-start | bytes 786440 | tf_op jit(solution)/shard_map/ppermute | solution.py:822
  45.0 24.7 %collective-permute-start.6 = (bf16[256,2048]{1,0:T(8,128)(2,1)}, bf16[256,2048]{1,0:T(8,128)(2,1)S(1)}, u32[]{:S(2)}, u32[]{:S(2)}) collective-permute-start(bf16[256,2048]{1,0:T(8,128)(2,1)} %later.8.refs_2_.refs_6_.refs_5_.refs_1_), channel_id=1, source_target_pairs={{0,8},{8,0},{16,24},{24,16},{1,9},{9,1},{17,25},{25,17},{2,10},{10... | collective-permute-start | bytes 3145736 | tf_op jit(solution)/shard_map/ppermute | solution.py:822
  46.2 24.7 %collective-permute-start.7 = (bf16[256,2048]{1,0:T(8,128)(2,1)}, bf16[256,2048]{1,0:T(8,128)(2,1)S(1)}, u32[]{:S(2)}, u32[]{:S(2)}) collective-permute-start(bf16[256,2048]{1,0:T(8,128)(2,1)} %later.8.refs_2_.refs_6_.refs_5_.refs_1_), channel_id=1, source_target_pairs={{0,16},{8,24},{16,0},{24,8},{1,17},{9,25},{17,1},{25,9},{2,18},{10... | collective-permute-start | bytes 3145736 | tf_op jit(solution)/shard_map/ppermute | solution.py:822
  47.6 29.1 %collective-permute-start.11 = (bf16[256,2048]{1,0:T(8,128)(2,1)}, bf16[256,2048]{1,0:T(8,128)(2,1)}, u32[]{:S(2)}, u32[]{:S(2)}) collective-permute-start(bf16[256,2048]{1,0:T(8,128)(2,1)} %later.8.refs_2_.refs_6_.refs_5_.refs_1_), channel_id=1, source_target_pairs={{0,1},{1,0},{2,3},{3,2},{4,5},{5,4},{6,7},{7,6},{8,9},{9,8},{10,11... | collective-permute-start | bytes 3145736 | tf_op jit(solution)/shard_map/ppermute | solution.py:822
  59.2 37.4 %collective-permute-start.16 = (bf16[640,1024]{1,0:T(8,128)(2,1)}, bf16[640,1024]{1,0:T(8,128)(2,1)}, u32[]{:S(2)}, u32[]{:S(2)}) collective-permute-start(bf16[640,1024]{1,0:T(8,128)(2,1)} %get-tuple-element.68), channel_id=1, source_target_pairs={{0,1},{1,0},{2,3},{3,2},{4,5},{5,4},{6,7},{7,6},{8,9},{9,8},{10,11... | collective-permute-start | bytes 3932168 | tf_op jit(solution)/shard_map/ppermute | solution.py:822
  74.0 21.4 %collective-permute-start.9 = (bf16[256,1024]{1,0:T(8,128)(2,1)}, bf16[256,1024]{1,0:T(8,128)(2,1)S(1)}, u32[]{:S(2)}, u32[]{:S(2)}) collective-permute-start(bf16[256,1024]{1,0:T(8,128)(2,1)} %get-tuple-element.66), channel_id=1, source_target_pairs={{0,16},{8,24},{16,0},{24,8},{1,17},{9,25},{17,1},{25,9},{2,18},{10... | collective-permute-start | bytes 1572872 | tf_op jit(solution)/shard_map/ppermute | solution.py:822
  75.5 20.2 %collective-permute-start.10 = (bf16[256,1024]{1,0:T(8,128)(2,1)}, bf16[256,1024]{1,0:T(8,128)(2,1)}, u32[]{:S(2)}, u32[]{:S(2)}) collective-permute-start(bf16[256,1024]{1,0:T(8,128)(2,1)} %get-tuple-element.67), channel_id=1, source_target_pairs={{0,8},{8,0},{16,24},{24,16},{1,9},{9,1},{17,25},{25,17},{2,10},{10... | collective-permute-start | bytes 1572872 | tf_op jit(solution)/shard_map/ppermute | solution.py:822
  76.7 21.6 %collective-permute-start.12 = (bf16[256,2048]{1,0:T(8,128)(2,1)}, bf16[256,2048]{1,0:T(8,128)(2,1)S(1)}, u32[]{:S(2)}, u32[]{:S(2)}) collective-permute-start(bf16[256,2048]{1,0:T(8,128)(2,1)} %copy-done), channel_id=1, source_target_pairs={{0,1},{1,0},{2,3},{3,2},{4,5},{5,4},{6,7},{7,6},{8,9},{9,8},{10,11... | collective-permute-start | bytes 3145736 | tf_op jit(solution)/shard_map/ppermute | solution.py:822
  76.8 21.6 %collective-permute-start.13 = (bf16[256,2048]{1,0:T(8,128)(2,1)}, bf16[256,2048]{1,0:T(8,128)(2,1)}, u32[]{:S(2)}, u32[]{:S(2)}) collective-permute-start(bf16[256,2048]{1,0:T(8,128)(2,1)} %copy-done.1), channel_id=1, source_target_pairs={{0,1},{1,0},{2,3},{3,2},{4,5},{5,4},{6,7},{7,6},{8,9},{9,8},{10,11... | collective-permute-start | bytes 3145736 | tf_op jit(solution)/shard_map/ppermute | solution.py:822
  79.7 11.9 %all-to-all-start = ((bf16[32,2,272]{2,1,0:T(2,128)(2,1)}), bf16[32,2,272]{2,1,0:T(2,128)(2,1)S(1)}, u32[]{:S(2)}, u32[]{:S(2)}) async-start(bf16[32,2,272]{2,1,0:T(2,128)(2,1)} %reshape.292), calls=%async_computation | async-start | bytes 98304 | tf_op jit(solution)/shard_map/all_to_all | solution.py:1046
  83.7 128.2 %all-gather.12.cloned.1.call-start = ((), (), s32[]{:S(2)}) async-start(), calls=%async_computation.13 | async-start | bytes 5242880 | tf_op jit(solution)/shard_map/all_gather | solution.py:1079
  96.5 237.6 %reduce-scatter.5.cloned.1.call-start = ((), (), s32[]{:S(2)}) async-start(), calls=%async_computation.9 | async-start | bytes 10485760 | tf_op jit(solution)/shard_map/reduce_scatter | solution.py:1117
  96.6 49.3 %collective-permute-start.17 = (bf16[256,4096]{1,0:T(8,128)(2,1)}, bf16[256,4096]{1,0:T(8,128)(2,1)S(1)}, u32[]{:S(2)}, u32[]{:S(2)}) collective-permute-start(bf16[256,4096]{1,0:T(8,128)(2,1)} %all-gather.8.cloned.1.call-done.refs_16_.refs_4_.refs_6_), channel_id=1, source_target_pairs={{0,8},{8,0},{16,24},{24,16},{1,9},{9,1},{17,25},{25,17},{2,10},{10... | collective-permute-start | bytes 6291464 | tf_op jit(solution)/shard_map/ppermute | solution.py:822
  97.5 48.4 %collective-permute-start.18 = (bf16[256,4096]{1,0:T(8,128)(2,1)}, bf16[256,4096]{1,0:T(8,128)(2,1)S(1)}, u32[]{:S(2)}, u32[]{:S(2)}) collective-permute-start(bf16[256,4096]{1,0:T(8,128)(2,1)} %all-gather.8.cloned.1.call-done.refs_16_.refs_4_.refs_6_), channel_id=1, source_target_pairs={{0,16},{8,24},{16,0},{24,8},{1,17},{9,25},{17,1},{25,9},{2,18},{10... | collective-permute-start | bytes 6291464 | tf_op jit(solution)/shard_map/ppermute | solution.py:822
  112.7 39.9 %collective-permute-start.19 = (bf16[1024,1024]{1,0:T(8,128)(2,1)}, bf16[1024,1024]{1,0:T(8,128)(2,1)}, u32[]{:S(2)}, u32[]{:S(2)}) collective-permute-start(bf16[1024,1024]{1,0:T(8,128)(2,1)} %get-tuple-element.73.refs_1_), channel_id=1, source_target_pairs={{0,1},{1,0},{2,3},{3,2},{4,5},{5,4},{6,7},{7,6},{8,9},{9,8},{10,11... | collective-permute-start | bytes 6291464 | tf_op jit(solution)/shard_map/ppermute | solution.py:822
  150.6 25.5 %collective-permute-start.20 = (bf16[256,2048]{1,0:T(8,128)(2,1)}, bf16[256,2048]{1,0:T(8,128)(2,1)S(1)}, u32[]{:S(2)}, u32[]{:S(2)}) collective-permute-start(bf16[256,2048]{1,0:T(8,128)(2,1)} %get-tuple-element.71.refs_16_), channel_id=1, source_target_pairs={{0,16},{8,24},{16,0},{24,8},{1,17},{9,25},{17,1},{25,9},{2,18},{10... | collective-permute-start | bytes 3145736 | tf_op jit(solution)/shard_map/ppermute | solution.py:822
  151.5 25.5 %collective-permute-start.21 = (bf16[256,2048]{1,0:T(8,128)(2,1)}, bf16[256,2048]{1,0:T(8,128)(2,1)S(1)}, u32[]{:S(2)}, u32[]{:S(2)}) collective-permute-start(bf16[256,2048]{1,0:T(8,128)(2,1)} %get-tuple-element.72.refs_17_), channel_id=1, source_target_pairs={{0,8},{8,0},{16,24},{24,16},{1,9},{9,1},{17,25},{25,17},{2,10},{10... | collective-permute-start | bytes 3145736 | tf_op jit(solution)/shard_map/ppermute | solution.py:822
  177.9 3.4 collective-permute-start.22
  179.2 27.4 %collective-permute-start.23 = (bf16[1024,512]{1,0:T(8,128)(2,1)S(1)}, bf16[1024,512]{1,0:T(8,128)(2,1)S(1)}, u32[]{:S(2)}, u32[]{:S(2)}) collective-permute-start(bf16[1024,512]{1,0:T(8,128)(2,1)S(1)} %copy-done.2), channel_id=1, source_target_pairs={{0,8},{8,0},{16,24},{24,16},{1,9},{9,1},{17,25},{25,17},{2,10},{10... | collective-permute-start | bytes 3145736 | tf_op jit(solution)/shard_map/ppermute | solution.py:822
  180.3 26.3 %collective-permute-start.24 = (bf16[1024,512]{1,0:T(8,128)(2,1)S(1)}, bf16[1024,512]{1,0:T(8,128)(2,1)S(1)}, u32[]{:S(2)}, u32[]{:S(2)}) collective-permute-start(bf16[1024,512]{1,0:T(8,128)(2,1)S(1)} %copy-done.2), channel_id=1, source_target_pairs={{0,16},{8,24},{16,0},{24,8},{1,17},{9,25},{17,1},{25,9},{2,18},{10... | collective-permute-start | bytes 3145736 | tf_op jit(solution)/shard_map/ppermute | solution.py:822
  209.9 18.8 %collective-permute-start.25 = (bf16[1024,256]{1,0:T(8,128)(2,1)}, bf16[1024,256]{1,0:T(8,128)(2,1)S(1)}, u32[]{:S(2)}, u32[]{:S(2)}) collective-permute-start(bf16[1024,256]{1,0:T(8,128)(2,1)} %get-tuple-element.78.refs_3_), channel_id=1, source_target_pairs={{0,16},{8,24},{16,0},{24,8},{1,17},{9,25},{17,1},{25,9},{2,18},{10... | collective-permute-start | bytes 1572872 | tf_op jit(solution)/shard_map/ppermute | solution.py:822
  211.0 17.8 %collective-permute-start.26 = (bf16[1024,256]{1,0:T(8,128)(2,1)}, bf16[1024,256]{1,0:T(8,128)(2,1)S(1)}, u32[]{:S(2)}, u32[]{:S(2)}) collective-permute-start(bf16[1024,256]{1,0:T(8,128)(2,1)} %get-tuple-element.79.refs_4_), channel_id=1, source_target_pairs={{0,8},{8,0},{16,24},{24,16},{1,9},{9,1},{17,25},{25,17},{2,10},{10... | collective-permute-start | bytes 1572872 | tf_op jit(solution)/shard_map/ppermute | solution.py:822
  229.8 154.4 %reduce-scatter.7.cloned.1.call-start = ((), (), s32[]{:S(2)}) async-start(), calls=%async_computation.10 | async-start | bytes 2621440 | tf_op jit(solution)/shard_map/reduce_scatter | solution.py:918
  280.5 4.3 collective-permute-start.27
  280.6 39.6 %collective-permute-start.30 = (bf16[1024,1024]{1,0:T(8,128)(2,1)S(1)}, bf16[1024,1024]{1,0:T(8,128)(2,1)}, u32[]{:S(2)}, u32[]{:S(2)}) collective-permute-start(bf16[1024,1024]{1,0:T(8,128)(2,1)S(1)} %copy-done.5), channel_id=1, source_target_pairs={{0,1},{1,0},{2,3},{3,2},{4,5},{5,4},{6,7},{7,6},{8,9},{9,8},{10,11... | collective-permute-start | bytes 6291464 | tf_op jit(solution)/shard_map/ppermute | solution.py:822
  281.1 46.5 %collective-permute-start.28 = (bf16[256,2048]{1,0:T(8,128)(2,1)}, bf16[256,2048]{1,0:T(8,128)(2,1)S(1)}, u32[]{:S(2)}, u32[]{:S(2)}) collective-permute-start(bf16[256,2048]{1,0:T(8,128)(2,1)} %get-tuple-element.86), channel_id=1, source_target_pairs={{0,8},{8,0},{16,24},{24,16},{1,9},{9,1},{17,25},{25,17},{2,10},{10... | collective-permute-start | bytes 3145736 | tf_op jit(solution)/shard_map/ppermute | solution.py:822
  281.8 45.7 %collective-permute-start.29 = (bf16[256,2048]{1,0:T(8,128)(2,1)}, bf16[256,2048]{1,0:T(8,128)(2,1)S(1)}, u32[]{:S(2)}, u32[]{:S(2)}) collective-permute-start(bf16[256,2048]{1,0:T(8,128)(2,1)} %get-tuple-element.87), channel_id=1, source_target_pairs={{0,16},{8,24},{16,0},{24,8},{1,17},{9,25},{17,1},{25,9},{2,18},{10... | collective-permute-start | bytes 3145736 | tf_op jit(solution)/shard_map/ppermute | solution.py:822
  300.7 19.5 %collective-permute-start.31 = (bf16[1024,512]{1,0:T(8,128)(2,1)}, bf16[1024,512]{1,0:T(8,128)(2,1)S(1)}, u32[]{:S(2)}, u32[]{:S(2)}) collective-permute-start(bf16[1024,512]{1,0:T(8,128)(2,1)} %get-tuple-element.89), channel_id=1, source_target_pairs={{0,1},{1,0},{2,3},{3,2},{4,5},{5,4},{6,7},{7,6},{8,9},{9,8},{10,11... | collective-permute-start | bytes 3145736 | tf_op jit(solution)/shard_map/ppermute | solution.py:822
  319.7 34.5 %collective-permute-start.32 = (bf16[3,1024,512]{2,1,0:T(8,128)(2,1)}, bf16[3,1024,512]{2,1,0:T(8,128)(2,1)}, u32[]{:S(2)}, u32[]{:S(2)}) collective-permute-start(bf16[3,1024,512]{2,1,0:T(8,128)(2,1)} %attention_backward.2.refs_5_.refs_1_), channel_id=1, source_target_pairs={{0,1},{1,0},{2,3},{3,2},{4,5},{5,4},{6,7},{7,6},{8,9},{9,8},{10,11... | collective-permute-start | bytes 9437192 | tf_op jit(solution)/shard_map/ppermute | solution.py:822
  334.2 108.0 %reduce-scatter.11.cloned.1.call-start = ((), (), s32[]{:S(2)}) async-start(), calls=%async_computation.12 | async-start | bytes 2621440 | tf_op jit(solution)/shard_map/reduce_scatter | solution.py:918
  334.2 49.9 %collective-permute-start.35 = (bf16[256,4096]{1,0:T(8,128)(2,1)}, bf16[256,4096]{1,0:T(8,128)(2,1)}, u32[]{:S(2)}, u32[]{:S(2)}) collective-permute-start(bf16[256,4096]{1,0:T(8,128)(2,1)} %get-tuple-element.91.refs_8_.refs_1_), channel_id=1, source_target_pairs={{0,8},{8,0},{16,24},{24,16},{1,9},{9,1},{17,25},{25,17},{2,10},{10... | collective-permute-start | bytes 6291464 | tf_op jit(solution)/shard_map/ppermute | solution.py:822
  334.4 49.8 %collective-permute-start.36 = (bf16[256,4096]{1,0:T(8,128)(2,1)}, bf16[256,4096]{1,0:T(8,128)(2,1)}, u32[]{:S(2)}, u32[]{:S(2)}) collective-permute-start(bf16[256,4096]{1,0:T(8,128)(2,1)} %get-tuple-element.92.refs_9_.refs_2_), channel_id=1, source_target_pairs={{0,16},{8,24},{16,0},{24,8},{1,17},{9,25},{17,1},{25,9},{2,18},{10... | collective-permute-start | bytes 6291464 | tf_op jit(solution)/shard_map/ppermute | solution.py:822
  366.8 26.6 %collective-permute-start.33 = (bf16[256,1024]{1,0:T(8,128)(2,1)}, bf16[256,1024]{1,0:T(8,128)(2,1)S(1)}, u32[]{:S(2)}, u32[]{:S(2)}) collective-permute-start(bf16[256,1024]{1,0:T(8,128)(2,1)} %get-tuple-element.96.refs_7_), channel_id=1, source_target_pairs={{0,8},{8,0},{16,24},{24,16},{1,9},{9,1},{17,25},{25,17},{2,10},{10... | collective-permute-start | bytes 1572872 | tf_op jit(solution)/shard_map/ppermute | solution.py:822
  367.7 25.7 %collective-permute-start.34 = (bf16[256,1024]{1,0:T(8,128)(2,1)}, bf16[256,1024]{1,0:T(8,128)(2,1)S(1)}, u32[]{:S(2)}, u32[]{:S(2)}) collective-permute-start(bf16[256,1024]{1,0:T(8,128)(2,1)} %get-tuple-element.97), channel_id=1, source_target_pairs={{0,16},{8,24},{16,0},{24,8},{1,17},{9,25},{17,1},{25,9},{2,18},{10... | collective-permute-start | bytes 1572872 | tf_op jit(solution)/shard_map/ppermute | solution.py:822
  395.0 69.9 %reduce-scatter.9.cloned.1.call-start = ((), (), s32[]{:S(2)}) async-start(), calls=%async_computation.11 | async-start | bytes 1310720 | tf_op jit(solution)/shard_map/reduce_scatter | solution.py:918
  396.0 5.7 %collective-permute-start.37 = (bf16[128,1024]{1,0:T(8,128)(2,1)S(1)}, bf16[128,1024]{1,0:T(8,128)(2,1)S(1)}, u32[]{:S(2)}, u32[]{:S(2)}) collective-permute-start(bf16[128,1024]{1,0:T(8,128)(2,1)S(1)} %dynamic-slice_bitcast_fusion.1), channel_id=1, source_target_pairs={{0,1},{1,0},{2,3},{3,2},{4,5},{5,4},{6,7},{7,6},{8,9},{9,8},{10,11... | collective-permute-start | bytes 786440 | tf_op jit(solution)/shard_map/ppermute | solution.py:822
  400.5 25.7 %collective-permute-start.39 = (bf16[256,2048]{1,0:T(8,128)(2,1)}, bf16[256,2048]{1,0:T(8,128)(2,1)S(1)}, u32[]{:S(2)}, u32[]{:S(2)}) collective-permute-start(bf16[256,2048]{1,0:T(8,128)(2,1)} %get-tuple-element.101.refs_8_), channel_id=1, source_target_pairs={{0,8},{8,0},{16,24},{24,16},{1,9},{9,1},{17,25},{25,17},{2,10},{10... | collective-permute-start | bytes 3145736 | tf_op jit(solution)/shard_map/ppermute | solution.py:822
  401.5 25.4 %collective-permute-start.40 = (bf16[256,2048]{1,0:T(8,128)(2,1)}, bf16[256,2048]{1,0:T(8,128)(2,1)S(1)}, u32[]{:S(2)}, u32[]{:S(2)}) collective-permute-start(bf16[256,2048]{1,0:T(8,128)(2,1)} %get-tuple-element.102.refs_9_), channel_id=1, source_target_pairs={{0,16},{8,24},{16,0},{24,8},{1,17},{9,25},{17,1},{25,9},{2,18},{10... | collective-permute-start | bytes 3145736 | tf_op jit(solution)/shard_map/ppermute | solution.py:822
  432.0 19.2 %collective-permute-start.38 = (bf16[640,1024]{1,0:T(8,128)(2,1)S(1)}, bf16[640,1024]{1,0:T(8,128)(2,1)S(1)}, u32[]{:S(2)}, u32[]{:S(2)}) collective-permute-start(bf16[640,1024]{1,0:T(8,128)(2,1)S(1)} %copy-done.55), channel_id=1, source_target_pairs={{0,1},{1,0},{2,3},{3,2},{4,5},{5,4},{6,7},{7,6},{8,9},{9,8},{10,11... | collective-permute-start | bytes 3932168 | tf_op jit(solution)/shard_map/ppermute | solution.py:822
  439.6 10.2 %all-to-all-start.1 = ((f32[32,1,384]{2,1,0:T(1,128)}), f32[32,1,384]{2,1,0:T(1,128)S(1)}, u32[]{:S(2)}, u32[]{:S(2)}) async-start(f32[32,1,384]{2,1,0:T(1,128)} %copy.150), calls=%async_computation.3 | async-start | bytes 98304 | tf_op jit(solution)/shard_map/all_to_all | solution.py:1177
  443.2 16.4 %collective-permute-start.41 = (bf16[32,4096]{1,0:T(8,128)(2,1)S(1)}, bf16[32,4096]{1,0:T(8,128)(2,1)S(1)}, u32[]{:S(2)}, u32[]{:S(2)}) collective-permute-start(bf16[32,4096]{1,0:T(8,128)(2,1)S(1)} %dynamic-slice_bitcast_fusion), channel_id=1, source_target_pairs={{0,1},{1,0},{2,3},{3,2},{4,5},{5,4},{6,7},{7,6},{8,9},{9,8},{10,11... | collective-permute-start | bytes 786440 | tf_op jit(solution)/shard_map/ppermute | solution.py:822
  (64 other events, 492.6 us)
Sparse Core Ops, SparseCore 0:
  14.1 30.5 all-gather.5
  46.8 46.4 all-gather.7
  95.5 26.6 all-gather.9
  124.2 80.2 all-gather.11
  229.9 100.8 reduce-scatter.4
  334.3 40.3 reduce-scatter.6
  395.1 40.5 reduce-scatter.10
  438.1 26.7 reduce-scatter.8
